TPU v7x, 256 devices: a whole 4x4x8 slice. The times are simulated.
256 devices in a mesh: seq: 32 (over z, x), head: 2 (over y_hi), batch: 4 (over y_lo, core).
Axes of the slice: x: 4, y: 4 (y_hi: 2, y_lo: 2; y = y_hi * 2 + y_lo), z: 8, core: 2. Of those that a mesh axis runs over, the one named last changes fastest.
Arguments:
- query: bfloat16 [8, 32, 128, 32, 128], P('batch', 'seq', None, 'head'), parts along dimension 0, may hold values from -6 to 6
- keys: bfloat16 [8, 32, 128, 8, 128], P('batch', 'seq', None, 'head'), parts along dimension 0, may hold values from -6 to 6
- values: bfloat16 [8, 32, 128, 8, 128], P('batch', 'seq', None, 'head'), parts along dimension 0, may hold values from -6 to 6
- grad_out: bfloat16 [8, 32, 128, 32, 128], P('batch', 'seq', None, 'head'), parts along dimension 0, may hold values from -6 to 6
- doc_starts: int32 [16384], P('batch'), parts along dimension 0, may hold values from 0 to 8192, as said below
Outputs:
- attended: bfloat16 [8, 32, 128, 32, 128], P('batch', 'seq', None, 'head'), parts along dimension 0
- grad_query: bfloat16 [8, 32, 128, 32, 128], P('batch', 'seq', None, 'head'), parts along dimension 0
- grad_keys: bfloat16 [8, 32, 128, 8, 128], P('batch', 'seq', None, 'head'), parts along dimension 0
- grad_values: bfloat16 [8, 32, 128, 8, 128], P('batch', 'seq', None, 'head'), parts along dimension 0
There are 4 independent parts, one for each index of `batch`. A program takes and returns all parts, laid end to end along the dimension named above; each array names one. Nothing has to cross between parts.
Inputs may be any that keep to these rules, and one draw needn't show every extreme that they name: `doc_starts`: entry 0 is 0; entries rise with differences of 2 to 2048 until an entry reaches 8192, and every later entry equals 8192; one difference is exactly 2048. So every document has at most 2048 tokens.
All inputs are finite; a program needn't handle non-finite values.
Results may differ from a plain program's by a relative error of at most 0.0065.
Values may be sent and summed in bfloat16 or wider, within the bound.
A program may use at most 128 MiB of HBM per device.

v0:
```python
import jax
import jax.numpy as jnp
from jax import lax
from jax.sharding import PartitionSpec as P


def shifted(value, axis, steps):
    count = lax.axis_size(axis)
    initial, last = (max(0, -steps), min(count, count - steps))
    return lax.ppermute(value, axis, [(source, source + steps) for source in range(initial, last)])


def doc_index(doc_starts, positions, span_len):
    blocks = positions.reshape(-1, span_len)

    def count_block(block_pos):
        below = (doc_starts[None, :] <= block_pos[:, None]).astype(jnp.int32)
        return jnp.sum(below, axis=1) - 1

    return lax.map(count_block, blocks).reshape(-1)


def softmax_rows(scores, allowed):
    scores = jnp.where(allowed[None], scores, -jnp.inf)
    top_score = jnp.max(scores, axis=-1, keepdims=True)
    expons = jnp.exp(scores - top_score)
    return expons / jnp.sum(expons, axis=-1, keepdims=True)


def grad_of_scores(weights, grad_weights, grad_output, attended, score_scale):
    delta = jnp.sum(grad_output.astype(jnp.float32) * attended.astype(jnp.float32), axis=-1)
    delta = jnp.transpose(delta, (1, 0))
    return (weights * (grad_weights - delta[..., None]) * score_scale).astype(jnp.bfloat16)


def head_dense(pieces, allowed, score_scale):
    queries, key_window, value_window, grad_output = pieces
    scores = (
        jnp.einsum("rgd,jd->grj", queries, key_window, preferred_element_type=jnp.float32)
        * score_scale
    )
    weights = softmax_rows(scores, allowed)
    weights_low = weights.astype(jnp.bfloat16)
    attended = jnp.einsum(
        "grj,jd->rgd", weights_low, value_window, preferred_element_type=jnp.float32
    ).astype(jnp.bfloat16)
    grad_weights = jnp.einsum(
        "rgd,jd->grj", grad_output, value_window, preferred_element_type=jnp.float32
    )
    grad_scores = grad_of_scores(weights, grad_weights, grad_output, attended, score_scale)
    grad_query = jnp.einsum(
        "grj,jd->rgd", grad_scores, key_window, preferred_element_type=jnp.float32
    )
    grad_keys = jnp.einsum("grj,rgd->jd", grad_scores, queries, preferred_element_type=jnp.float32)
    grad_values = jnp.einsum(
        "grj,rgd->jd", weights_low, grad_output, preferred_element_type=jnp.float32
    )
    return (attended, grad_query.astype(jnp.bfloat16), grad_keys, grad_values)


def body(query, keys, values, grad_out, doc_starts):
    shard_count = lax.axis_size("seq")
    device_index = lax.axis_index("seq")
    window = min(16, shard_count // 2)
    span_len = query.shape[2]
    head_count = query.shape[3]
    kv_heads = keys.shape[3]
    head_dim = query.shape[4]
    group_size = head_count // kv_heads
    score_scale = head_dim ** (-0.5)
    last_device = device_index == shard_count - 1
    current = jnp.stack([keys[:, 0], values[:, 0]], axis=1)

    def pass_forward(turn_index, state_now):
        moving, stored = state_now
        from_below = shifted(moving[0], "seq", 1)
        from_above = shifted(moving[1], "seq", -1)
        from_above = jnp.where(last_device, moving[0], from_above)
        moving = jnp.stack([from_below, from_above], axis=0)
        stored = lax.dynamic_update_index_in_dim(stored, moving, window - 1 - turn_index, 0)
        return (moving, stored)

    history = jnp.zeros((window,) + current.shape, jnp.bfloat16)
    moving, history = lax.fori_loop(0, window, pass_forward, (current, history))
    row_ids = jnp.arange(span_len, dtype=jnp.int32)
    key_count = (window + 1) * span_len
    span_firsts = [device_index, 2 * shard_count - 1 - device_index]
    outputs = []
    query_grads = []
    term_list = []
    for half_idx in range(2):
        token_pos = span_firsts[half_idx] * span_len + row_ids
        key_pos = (span_firsts[half_idx] - window) * span_len + jnp.arange(
            key_count, dtype=jnp.int32
        )
        key_doc = doc_index(doc_starts, key_pos, span_len)
        query_doc = key_doc[window * span_len :]
        allowed = (query_doc[:, None] == key_doc[None, :]) & (
            key_pos[None, :] <= token_pos[:, None]
        )
        windows = jnp.concatenate([history[:, half_idx], current[half_idx][None]], axis=0)
        key_window = jnp.transpose(windows[:, 0].reshape(key_count, kv_heads, head_dim), (1, 0, 2))
        value_window = jnp.transpose(
            windows[:, 1].reshape(key_count, kv_heads, head_dim), (1, 0, 2)
        )
        queries = jnp.transpose(
            query[half_idx, 0].reshape(span_len, kv_heads, group_size, head_dim), (1, 0, 2, 3)
        )
        grad_output = jnp.transpose(
            grad_out[half_idx, 0].reshape(span_len, kv_heads, group_size, head_dim), (1, 0, 2, 3)
        )
        attended, grad_query, grad_keys, grad_values = lax.map(
            lambda parts: head_dense(parts, allowed, score_scale),
            (queries, key_window, value_window, grad_output),
        )
        outputs.append(
            jnp.transpose(attended, (1, 0, 2, 3)).reshape(span_len, head_count, head_dim)
        )
        query_grads.append(
            jnp.transpose(grad_query, (1, 0, 2, 3)).reshape(span_len, head_count, head_dim)
        )
        paired = jnp.stack([grad_keys, grad_values], axis=0).reshape(
            2, kv_heads, window + 1, span_len, head_dim
        )
        term_list.append(jnp.transpose(paired, (2, 0, 3, 1, 4)))
    term_all = jnp.stack(term_list, axis=1)

    def pass_back(turn_index, totals):
        from_below = shifted(totals[0].astype(jnp.bfloat16), "seq", -1).astype(jnp.float32)
        from_above = shifted(totals[1].astype(jnp.bfloat16), "seq", 1).astype(jnp.float32)
        from_below = jnp.where(last_device, totals[1], from_below)
        return jnp.stack([from_below, from_above], axis=0) + lax.dynamic_index_in_dim(
            term_all, turn_index, 0, keepdims=False
        )

    totals = lax.fori_loop(1, window + 1, pass_back, term_all[0])
    grad_keys_out = totals[:, 0][:, None].astype(jnp.bfloat16)
    grad_values_out = totals[:, 1][:, None].astype(jnp.bfloat16)
    return (
        jnp.stack(outputs, axis=0)[:, None],
        jnp.stack(query_grads, axis=0)[:, None],
        grad_keys_out,
        grad_values_out,
    )


def solution(mesh):
    placed = (
        P("batch", "seq", None, "head", None),
        P("batch", "seq", None, "head", None),
        P("batch", "seq", None, "head", None),
        P("batch", "seq", None, "head", None),
        P("batch"),
    )
    return jax.shard_map(
        body,
        mesh=mesh,
        in_specs=placed,
        out_specs=(
            P("batch", "seq", None, "head", None),
            P("batch", "seq", None, "head", None),
            P("batch", "seq", None, "head", None),
            P("batch", "seq", None, "head", None),
        ),
        check_vma=False,
    )
```

profile of v0, /device:TPU:126, one launch (start us, length us, event | category | flops | bytes accessed | tf_op | source)
XLA Modules:
  0.0 792.3 jit_solution(14774819136855452987)
XLA Ops:
  3.1 5.4 broadcast_in_dim.87.clone
  8.4 255.1 %while.90 = (s32[]{:T(128)}, bf16[2,2,128,4,128]{4,3,2,1,0:T(4,128)(2,1)S(1)}, bf16[16,2,2,128,4,128]{5,3,0,4,2,1:T(8,128)(2,1)}, pred[]{:T(512)}, s32[]{:T(128)}, /*index=5*/s32[]{:T(128)}, s32[]{:T(128)}, s32[]{:T(128)}) while((s32[]{:T(128)}, bf16[2,2,128,4,128]{4,3,2,1,0:T(4,128)(2,1)S(1)}, bf16[16,2,2,128,4,128]{5,3,0,4,2,1:T(8,128)(2,1)}, ...), condition=%wide.region_1.2_spmd, body=%wide.region_0.1_spmd.sunk | while | flops 655366 | bytes 7078104 | solution.py:84
  11.4 6.4 collective-permute-start.1
  26.9 7.7 collective-permute-start.1
  42.7 7.7 collective-permute-start.1
  58.1 7.7 collective-permute-start.1
  73.5 7.7 collective-permute-start.1
  88.9 7.7 collective-permute-start.1
  104.3 7.7 collective-permute-start.1
  119.7 7.7 collective-permute-start.1
  135.0 7.7 collective-permute-start.1
  150.4 7.7 collective-permute-start.1
  165.8 7.7 collective-permute-start.1
  182.1 7.7 collective-permute-start.1
  199.6 7.7 collective-permute-start.1
  217.3 7.7 collective-permute-start.1
  234.3 7.7 collective-permute-start.1
  250.3 7.7 collective-permute-start.1
  270.5 7.4 while.91
  292.3 84.6 %while.94 = (s32[]{:T(128)}, bf16[4,128,4,128]{1,3,2,0:T(8,128)(2,1)}, bf16[4,128,4,128]{1,3,2,0:T(8,128)(2,1)}, f32[4,2176,128]{2,1,0:T(8,128)}, f32[4,2176,128...) while((s32[]{:T(128)}, ...), condition=%wide.region_9.10_spmd.clone, body=%wide.region_5.9_spmd.clone.sunk | while | flops 1724761728 | bytes 59713756 | solution.py:112
  294.6 5.2 fusion.188
  313.0 5.2 fusion.188
  331.4 5.2 fusion.188
  376.9 7.6 copy.95
  389.6 10.9 %maximum_bitcast_fusion = f32[17,1,2,128,4,128]{5,4,3,2,1,0:T(4,128)} fusion(f32[1,4,17,128,128]{4,1,3,0,2:T(4,128)} %copy.96, f32[1,4,17,128,128]{4,1,3,0,2:T(4,128)} %copy.95), kind=kLoop, calls=%fused_computation.127 | loop fusion | flops 2228224 | bytes 17825792 | tf_op jit(solution)/shard_map/stack | solution.py:126
  400.5 7.4 while.92
  417.7 65.1 %while.95 = (s32[]{:T(128)}, bf16[4,128,4,128]{1,3,2,0:T(8,128)(2,1)}, bf16[4,128,4,128]{1,3,2,0:T(8,128)(2,1)}, f32[4,2176,128]{2,1,0:T(8,128)}, f32[4,2176,128...) while((s32[]{:T(128)}, ...), condition=%wide.region_17.18_spmd.clone, body=%wide.region_13.17_spmd.clone.sunk | while | flops 1724761728 | bytes 59713756 | solution.py:112
  482.8 7.6 copy.97
  495.5 10.8 %maximum_bitcast_fusion.1 = f32[17,1,2,128,4,128]{5,4,3,2,1,0:T(4,128)} fusion(f32[1,4,17,128,128]{4,1,3,0,2:T(4,128)} %copy.98, f32[1,4,17,128,128]{4,1,3,0,2:T(4,128)} %copy.97), kind=kLoop, calls=%fused_computation.128 | loop fusion | flops 2228224 | bytes 17825792 | tf_op jit(solution)/shard_map/stack | solution.py:126
  506.4 18.9 %pad_maximum_fusion.1 = f32[17,2,2,128,4,128]{5,4,3,2,1,0:T(4,128)} fusion(f32[17,1,2,128,4,128]{5,4,3,2,1,0:T(4,128)} %maximum_bitcast_fusion.1, f32[17,1,2,128,4,128]{5,4,3,2,1,0:T(4,128)} %maximum_bitcast_fusion), kind=kLoop, calls=%fused_computation.125 | loop fusion | flops 4456448 | bytes 35651584 | tf_op jit(solution)/shard_map/stack | solution.py:126
  525.6 261.2 %while.93 = (s32[]{:T(128)}, f32[2,2,128,4,128]{4,3,2,1,0:T(4,128)S(1)}, pred[]{:T(512)}, f32[17,2,2,128,4,128]{5,4,3,2,1,0:T(4,128)}, s32[]{:T(128)}, /*index=5*/s32[]{:T(128)}, s32[]{:T(128)}) while((s32[]{:T(128)}, f32[2,2,128,4,128]{4,3,2,1,0:T(4,128)S(1)}, pred[]{:T(512)}, f32[17,2,2,128,4,128]{5,4,3,2,1,0:T(4,128)}, s32[]{:T(128)}, ...), condition=%wide.region_19.20_spmd, body=%wide.region_18.19_spmd.sunk | while | flops 917509 | bytes 8388812 | solution.py:136
  525.8 7.8 collective-permute-start.2
  537.5 7.7 collective-permute-done.3
  555.4 5.2 collective-permute-done.3
  570.9 5.2 collective-permute-done.3
  586.4 5.2 collective-permute-done.3
  601.8 5.2 collective-permute-done.3
  617.3 5.2 collective-permute-done.3
  632.7 5.2 collective-permute-done.3
  649.1 5.2 collective-permute-done.3
  666.7 5.2 collective-permute-done.3
  684.5 5.2 collective-permute-done.3
  701.5 5.2 collective-permute-done.3
  717.7 5.2 collective-permute-done.3
  733.2 5.2 collective-permute-done.3
  748.6 5.2 collective-permute-done.3
  764.1 5.2 collective-permute-done.3
  779.5 5.2 collective-permute-done.3
  (564 shorter events, 484.7 us)
Async XLA Ops:
  8.6 13.3 %collective-permute-start = (bf16[2,128,4,128]{3,2,1,0:T(4,128)(2,1)S(1)}, bf16[2,128,4,128]{3,2,1,0:T(4,128)(2,1)S(1)}, u32[]{:S(2)}, u32[]{:S(2)}) collective-permute-start(bf16[2,128,4,128]{3,2,1,0:T(4,128)(2,1)S(1)} %get-tuple-element.920), channel_id=1, source_target_pairs={{8,0},{16,8},{24,16},{32,24},{40,32},{48,40},{56,48},{64,56},{72,6... | collective-permute-start | bytes 786440 | tf_op jit(solution)/shard_map/while/body/eval_jaxpr/ppermute | solution.py:10
  11.4 11.7 %collective-permute-start.1 = (bf16[2,128,4,128]{3,2,1,0:T(4,128)(2,1)S(1)}, bf16[2,128,4,128]{3,2,1,0:T(4,128)(2,1)S(1)}, u32[]{:S(2)}, u32[]{:S(2)}) collective-permute-start(bf16[2,128,4,128]{3,2,1,0:T(4,128)(2,1)S(1)} %get-tuple-element.921), channel_id=1, source_target_pairs={{0,8},{8,16},{16,24},{24,32},{32,40},{40,48},{48,56},{56,64},{64,7... | collective-permute-start | bytes 786440 | tf_op jit(solution)/shard_map/while/body/eval_jaxpr/ppermute | solution.py:10
  24.9 12.8 %collective-permute-start = (bf16[2,128,4,128]{3,2,1,0:T(4,128)(2,1)S(1)}, bf16[2,128,4,128]{3,2,1,0:T(4,128)(2,1)S(1)}, u32[]{:S(2)}, u32[]{:S(2)}) collective-permute-start(bf16[2,128,4,128]{3,2,1,0:T(4,128)(2,1)S(1)} %get-tuple-element.920), channel_id=1, source_target_pairs={{8,0},{16,8},{24,16},{32,24},{40,32},{48,40},{56,48},{64,56},{72,6... | collective-permute-start | bytes 786440 | tf_op jit(solution)/shard_map/while/body/eval_jaxpr/ppermute | solution.py:10
  26.9 12.1 %collective-permute-start.1 = (bf16[2,128,4,128]{3,2,1,0:T(4,128)(2,1)S(1)}, bf16[2,128,4,128]{3,2,1,0:T(4,128)(2,1)S(1)}, u32[]{:S(2)}, u32[]{:S(2)}) collective-permute-start(bf16[2,128,4,128]{3,2,1,0:T(4,128)(2,1)S(1)} %get-tuple-element.921), channel_id=1, source_target_pairs={{0,8},{8,16},{16,24},{24,32},{32,40},{40,48},{48,56},{56,64},{64,7... | collective-permute-start | bytes 786440 | tf_op jit(solution)/shard_map/while/body/eval_jaxpr/ppermute | solution.py:10
  40.8 12.1 %collective-permute-start = (bf16[2,128,4,128]{3,2,1,0:T(4,128)(2,1)S(1)}, bf16[2,128,4,128]{3,2,1,0:T(4,128)(2,1)S(1)}, u32[]{:S(2)}, u32[]{:S(2)}) collective-permute-start(bf16[2,128,4,128]{3,2,1,0:T(4,128)(2,1)S(1)} %get-tuple-element.920), channel_id=1, source_target_pairs={{8,0},{16,8},{24,16},{32,24},{40,32},{48,40},{56,48},{64,56},{72,6... | collective-permute-start | bytes 786440 | tf_op jit(solution)/shard_map/while/body/eval_jaxpr/ppermute | solution.py:10
  42.7 11.6 %collective-permute-start.1 = (bf16[2,128,4,128]{3,2,1,0:T(4,128)(2,1)S(1)}, bf16[2,128,4,128]{3,2,1,0:T(4,128)(2,1)S(1)}, u32[]{:S(2)}, u32[]{:S(2)}) collective-permute-start(bf16[2,128,4,128]{3,2,1,0:T(4,128)(2,1)S(1)} %get-tuple-element.921), channel_id=1, source_target_pairs={{0,8},{8,16},{16,24},{24,32},{32,40},{40,48},{48,56},{56,64},{64,7... | collective-permute-start | bytes 786440 | tf_op jit(solution)/shard_map/while/body/eval_jaxpr/ppermute | solution.py:10
  56.2 12.1 %collective-permute-start = (bf16[2,128,4,128]{3,2,1,0:T(4,128)(2,1)S(1)}, bf16[2,128,4,128]{3,2,1,0:T(4,128)(2,1)S(1)}, u32[]{:S(2)}, u32[]{:S(2)}) collective-permute-start(bf16[2,128,4,128]{3,2,1,0:T(4,128)(2,1)S(1)} %get-tuple-element.920), channel_id=1, source_target_pairs={{8,0},{16,8},{24,16},{32,24},{40,32},{48,40},{56,48},{64,56},{72,6... | collective-permute-start | bytes 786440 | tf_op jit(solution)/shard_map/while/body/eval_jaxpr/ppermute | solution.py:10
  58.1 11.6 %collective-permute-start.1 = (bf16[2,128,4,128]{3,2,1,0:T(4,128)(2,1)S(1)}, bf16[2,128,4,128]{3,2,1,0:T(4,128)(2,1)S(1)}, u32[]{:S(2)}, u32[]{:S(2)}) collective-permute-start(bf16[2,128,4,128]{3,2,1,0:T(4,128)(2,1)S(1)} %get-tuple-element.921), channel_id=1, source_target_pairs={{0,8},{8,16},{16,24},{24,32},{32,40},{40,48},{48,56},{56,64},{64,7... | collective-permute-start | bytes 786440 | tf_op jit(solution)/shard_map/while/body/eval_jaxpr/ppermute | solution.py:10
  71.6 12.1 %collective-permute-start = (bf16[2,128,4,128]{3,2,1,0:T(4,128)(2,1)S(1)}, bf16[2,128,4,128]{3,2,1,0:T(4,128)(2,1)S(1)}, u32[]{:S(2)}, u32[]{:S(2)}) collective-permute-start(bf16[2,128,4,128]{3,2,1,0:T(4,128)(2,1)S(1)} %get-tuple-element.920), channel_id=1, source_target_pairs={{8,0},{16,8},{24,16},{32,24},{40,32},{48,40},{56,48},{64,56},{72,6... | collective-permute-start | bytes 786440 | tf_op jit(solution)/shard_map/while/body/eval_jaxpr/ppermute | solution.py:10
  73.5 11.6 %collective-permute-start.1 = (bf16[2,128,4,128]{3,2,1,0:T(4,128)(2,1)S(1)}, bf16[2,128,4,128]{3,2,1,0:T(4,128)(2,1)S(1)}, u32[]{:S(2)}, u32[]{:S(2)}) collective-permute-start(bf16[2,128,4,128]{3,2,1,0:T(4,128)(2,1)S(1)} %get-tuple-element.921), channel_id=1, source_target_pairs={{0,8},{8,16},{16,24},{24,32},{32,40},{40,48},{48,56},{56,64},{64,7... | collective-permute-start | bytes 786440 | tf_op jit(solution)/shard_map/while/body/eval_jaxpr/ppermute | solution.py:10
  87.0 12.1 %collective-permute-start = (bf16[2,128,4,128]{3,2,1,0:T(4,128)(2,1)S(1)}, bf16[2,128,4,128]{3,2,1,0:T(4,128)(2,1)S(1)}, u32[]{:S(2)}, u32[]{:S(2)}) collective-permute-start(bf16[2,128,4,128]{3,2,1,0:T(4,128)(2,1)S(1)} %get-tuple-element.920), channel_id=1, source_target_pairs={{8,0},{16,8},{24,16},{32,24},{40,32},{48,40},{56,48},{64,56},{72,6... | collective-permute-start | bytes 786440 | tf_op jit(solution)/shard_map/while/body/eval_jaxpr/ppermute | solution.py:10
  88.9 11.6 %collective-permute-start.1 = (bf16[2,128,4,128]{3,2,1,0:T(4,128)(2,1)S(1)}, bf16[2,128,4,128]{3,2,1,0:T(4,128)(2,1)S(1)}, u32[]{:S(2)}, u32[]{:S(2)}) collective-permute-start(bf16[2,128,4,128]{3,2,1,0:T(4,128)(2,1)S(1)} %get-tuple-element.921), channel_id=1, source_target_pairs={{0,8},{8,16},{16,24},{24,32},{32,40},{40,48},{48,56},{56,64},{64,7... | collective-permute-start | bytes 786440 | tf_op jit(solution)/shard_map/while/body/eval_jaxpr/ppermute | solution.py:10
  102.4 12.1 %collective-permute-start = (bf16[2,128,4,128]{3,2,1,0:T(4,128)(2,1)S(1)}, bf16[2,128,4,128]{3,2,1,0:T(4,128)(2,1)S(1)}, u32[]{:S(2)}, u32[]{:S(2)}) collective-permute-start(bf16[2,128,4,128]{3,2,1,0:T(4,128)(2,1)S(1)} %get-tuple-element.920), channel_id=1, source_target_pairs={{8,0},{16,8},{24,16},{32,24},{40,32},{48,40},{56,48},{64,56},{72,6... | collective-permute-start | bytes 786440 | tf_op jit(solution)/shard_map/while/body/eval_jaxpr/ppermute | solution.py:10
  104.3 11.6 %collective-permute-start.1 = (bf16[2,128,4,128]{3,2,1,0:T(4,128)(2,1)S(1)}, bf16[2,128,4,128]{3,2,1,0:T(4,128)(2,1)S(1)}, u32[]{:S(2)}, u32[]{:S(2)}) collective-permute-start(bf16[2,128,4,128]{3,2,1,0:T(4,128)(2,1)S(1)} %get-tuple-element.921), channel_id=1, source_target_pairs={{0,8},{8,16},{16,24},{24,32},{32,40},{40,48},{48,56},{56,64},{64,7... | collective-permute-start | bytes 786440 | tf_op jit(solution)/shard_map/while/body/eval_jaxpr/ppermute | solution.py:10
  117.7 12.1 %collective-permute-start = (bf16[2,128,4,128]{3,2,1,0:T(4,128)(2,1)S(1)}, bf16[2,128,4,128]{3,2,1,0:T(4,128)(2,1)S(1)}, u32[]{:S(2)}, u32[]{:S(2)}) collective-permute-start(bf16[2,128,4,128]{3,2,1,0:T(4,128)(2,1)S(1)} %get-tuple-element.920), channel_id=1, source_target_pairs={{8,0},{16,8},{24,16},{32,24},{40,32},{48,40},{56,48},{64,56},{72,6... | collective-permute-start | bytes 786440 | tf_op jit(solution)/shard_map/while/body/eval_jaxpr/ppermute | solution.py:10
  119.7 11.6 %collective-permute-start.1 = (bf16[2,128,4,128]{3,2,1,0:T(4,128)(2,1)S(1)}, bf16[2,128,4,128]{3,2,1,0:T(4,128)(2,1)S(1)}, u32[]{:S(2)}, u32[]{:S(2)}) collective-permute-start(bf16[2,128,4,128]{3,2,1,0:T(4,128)(2,1)S(1)} %get-tuple-element.921), channel_id=1, source_target_pairs={{0,8},{8,16},{16,24},{24,32},{32,40},{40,48},{48,56},{56,64},{64,7... | collective-permute-start | bytes 786440 | tf_op jit(solution)/shard_map/while/body/eval_jaxpr/ppermute | solution.py:10
  133.1 12.1 %collective-permute-start = (bf16[2,128,4,128]{3,2,1,0:T(4,128)(2,1)S(1)}, bf16[2,128,4,128]{3,2,1,0:T(4,128)(2,1)S(1)}, u32[]{:S(2)}, u32[]{:S(2)}) collective-permute-start(bf16[2,128,4,128]{3,2,1,0:T(4,128)(2,1)S(1)} %get-tuple-element.920), channel_id=1, source_target_pairs={{8,0},{16,8},{24,16},{32,24},{40,32},{48,40},{56,48},{64,56},{72,6... | collective-permute-start | bytes 786440 | tf_op jit(solution)/shard_map/while/body/eval_jaxpr/ppermute | solution.py:10
  135.0 11.6 %collective-permute-start.1 = (bf16[2,128,4,128]{3,2,1,0:T(4,128)(2,1)S(1)}, bf16[2,128,4,128]{3,2,1,0:T(4,128)(2,1)S(1)}, u32[]{:S(2)}, u32[]{:S(2)}) collective-permute-start(bf16[2,128,4,128]{3,2,1,0:T(4,128)(2,1)S(1)} %get-tuple-element.921), channel_id=1, source_target_pairs={{0,8},{8,16},{16,24},{24,32},{32,40},{40,48},{48,56},{56,64},{64,7... | collective-permute-start | bytes 786440 | tf_op jit(solution)/shard_map/while/body/eval_jaxpr/ppermute | solution.py:10
  148.4 12.1 %collective-permute-start = (bf16[2,128,4,128]{3,2,1,0:T(4,128)(2,1)S(1)}, bf16[2,128,4,128]{3,2,1,0:T(4,128)(2,1)S(1)}, u32[]{:S(2)}, u32[]{:S(2)}) collective-permute-start(bf16[2,128,4,128]{3,2,1,0:T(4,128)(2,1)S(1)} %get-tuple-element.920), channel_id=1, source_target_pairs={{8,0},{16,8},{24,16},{32,24},{40,32},{48,40},{56,48},{64,56},{72,6... | collective-permute-start | bytes 786440 | tf_op jit(solution)/shard_map/while/body/eval_jaxpr/ppermute | solution.py:10
  150.4 11.6 %collective-permute-start.1 = (bf16[2,128,4,128]{3,2,1,0:T(4,128)(2,1)S(1)}, bf16[2,128,4,128]{3,2,1,0:T(4,128)(2,1)S(1)}, u32[]{:S(2)}, u32[]{:S(2)}) collective-permute-start(bf16[2,128,4,128]{3,2,1,0:T(4,128)(2,1)S(1)} %get-tuple-element.921), channel_id=1, source_target_pairs={{0,8},{8,16},{16,24},{24,32},{32,40},{40,48},{48,56},{56,64},{64,7... | collective-permute-start | bytes 786440 | tf_op jit(solution)/shard_map/while/body/eval_jaxpr/ppermute | solution.py:10
  163.8 12.7 %collective-permute-start = (bf16[2,128,4,128]{3,2,1,0:T(4,128)(2,1)S(1)}, bf16[2,128,4,128]{3,2,1,0:T(4,128)(2,1)S(1)}, u32[]{:S(2)}, u32[]{:S(2)}) collective-permute-start(bf16[2,128,4,128]{3,2,1,0:T(4,128)(2,1)S(1)} %get-tuple-element.920), channel_id=1, source_target_pairs={{8,0},{16,8},{24,16},{32,24},{40,32},{48,40},{56,48},{64,56},{72,6... | collective-permute-start | bytes 786440 | tf_op jit(solution)/shard_map/while/body/eval_jaxpr/ppermute | solution.py:10
  165.8 12.6 %collective-permute-start.1 = (bf16[2,128,4,128]{3,2,1,0:T(4,128)(2,1)S(1)}, bf16[2,128,4,128]{3,2,1,0:T(4,128)(2,1)S(1)}, u32[]{:S(2)}, u32[]{:S(2)}) collective-permute-start(bf16[2,128,4,128]{3,2,1,0:T(4,128)(2,1)S(1)} %get-tuple-element.921), channel_id=1, source_target_pairs={{0,8},{8,16},{16,24},{24,32},{32,40},{40,48},{48,56},{56,64},{64,7... | collective-permute-start | bytes 786440 | tf_op jit(solution)/shard_map/while/body/eval_jaxpr/ppermute | solution.py:10
  180.2 13.9 %collective-permute-start = (bf16[2,128,4,128]{3,2,1,0:T(4,128)(2,1)S(1)}, bf16[2,128,4,128]{3,2,1,0:T(4,128)(2,1)S(1)}, u32[]{:S(2)}, u32[]{:S(2)}) collective-permute-start(bf16[2,128,4,128]{3,2,1,0:T(4,128)(2,1)S(1)} %get-tuple-element.920), channel_id=1, source_target_pairs={{8,0},{16,8},{24,16},{32,24},{40,32},{48,40},{56,48},{64,56},{72,6... | collective-permute-start | bytes 786440 | tf_op jit(solution)/shard_map/while/body/eval_jaxpr/ppermute | solution.py:10
  182.1 13.8 %collective-permute-start.1 = (bf16[2,128,4,128]{3,2,1,0:T(4,128)(2,1)S(1)}, bf16[2,128,4,128]{3,2,1,0:T(4,128)(2,1)S(1)}, u32[]{:S(2)}, u32[]{:S(2)}) collective-permute-start(bf16[2,128,4,128]{3,2,1,0:T(4,128)(2,1)S(1)} %get-tuple-element.921), channel_id=1, source_target_pairs={{0,8},{8,16},{16,24},{24,32},{32,40},{40,48},{48,56},{56,64},{64,7... | collective-permute-start | bytes 786440 | tf_op jit(solution)/shard_map/while/body/eval_jaxpr/ppermute | solution.py:10
  197.7 14.7 %collective-permute-start = (bf16[2,128,4,128]{3,2,1,0:T(4,128)(2,1)S(1)}, bf16[2,128,4,128]{3,2,1,0:T(4,128)(2,1)S(1)}, u32[]{:S(2)}, u32[]{:S(2)}) collective-permute-start(bf16[2,128,4,128]{3,2,1,0:T(4,128)(2,1)S(1)} %get-tuple-element.920), channel_id=1, source_target_pairs={{8,0},{16,8},{24,16},{32,24},{40,32},{48,40},{56,48},{64,56},{72,6... | collective-permute-start | bytes 786440 | tf_op jit(solution)/shard_map/while/body/eval_jaxpr/ppermute | solution.py:10
  199.6 13.9 %collective-permute-start.1 = (bf16[2,128,4,128]{3,2,1,0:T(4,128)(2,1)S(1)}, bf16[2,128,4,128]{3,2,1,0:T(4,128)(2,1)S(1)}, u32[]{:S(2)}, u32[]{:S(2)}) collective-permute-start(bf16[2,128,4,128]{3,2,1,0:T(4,128)(2,1)S(1)} %get-tuple-element.921), channel_id=1, source_target_pairs={{0,8},{8,16},{16,24},{24,32},{32,40},{40,48},{48,56},{56,64},{64,7... | collective-permute-start | bytes 786440 | tf_op jit(solution)/shard_map/while/body/eval_jaxpr/ppermute | solution.py:10
  215.4 13.9 %collective-permute-start = (bf16[2,128,4,128]{3,2,1,0:T(4,128)(2,1)S(1)}, bf16[2,128,4,128]{3,2,1,0:T(4,128)(2,1)S(1)}, u32[]{:S(2)}, u32[]{:S(2)}) collective-permute-start(bf16[2,128,4,128]{3,2,1,0:T(4,128)(2,1)S(1)} %get-tuple-element.920), channel_id=1, source_target_pairs={{8,0},{16,8},{24,16},{32,24},{40,32},{48,40},{56,48},{64,56},{72,6... | collective-permute-start | bytes 786440 | tf_op jit(solution)/shard_map/while/body/eval_jaxpr/ppermute | solution.py:10
  217.3 13.2 %collective-permute-start.1 = (bf16[2,128,4,128]{3,2,1,0:T(4,128)(2,1)S(1)}, bf16[2,128,4,128]{3,2,1,0:T(4,128)(2,1)S(1)}, u32[]{:S(2)}, u32[]{:S(2)}) collective-permute-start(bf16[2,128,4,128]{3,2,1,0:T(4,128)(2,1)S(1)} %get-tuple-element.921), channel_id=1, source_target_pairs={{0,8},{8,16},{16,24},{24,32},{32,40},{40,48},{48,56},{56,64},{64,7... | collective-permute-start | bytes 786440 | tf_op jit(solution)/shard_map/while/body/eval_jaxpr/ppermute | solution.py:10
  232.4 13.0 %collective-permute-start = (bf16[2,128,4,128]{3,2,1,0:T(4,128)(2,1)S(1)}, bf16[2,128,4,128]{3,2,1,0:T(4,128)(2,1)S(1)}, u32[]{:S(2)}, u32[]{:S(2)}) collective-permute-start(bf16[2,128,4,128]{3,2,1,0:T(4,128)(2,1)S(1)} %get-tuple-element.920), channel_id=1, source_target_pairs={{8,0},{16,8},{24,16},{32,24},{40,32},{48,40},{56,48},{64,56},{72,6... | collective-permute-start | bytes 786440 | tf_op jit(solution)/shard_map/while/body/eval_jaxpr/ppermute | solution.py:10
  234.3 12.2 %collective-permute-start.1 = (bf16[2,128,4,128]{3,2,1,0:T(4,128)(2,1)S(1)}, bf16[2,128,4,128]{3,2,1,0:T(4,128)(2,1)S(1)}, u32[]{:S(2)}, u32[]{:S(2)}) collective-permute-start(bf16[2,128,4,128]{3,2,1,0:T(4,128)(2,1)S(1)} %get-tuple-element.921), channel_id=1, source_target_pairs={{0,8},{8,16},{16,24},{24,32},{32,40},{40,48},{48,56},{56,64},{64,7... | collective-permute-start | bytes 786440 | tf_op jit(solution)/shard_map/while/body/eval_jaxpr/ppermute | solution.py:10
  248.4 12.1 %collective-permute-start = (bf16[2,128,4,128]{3,2,1,0:T(4,128)(2,1)S(1)}, bf16[2,128,4,128]{3,2,1,0:T(4,128)(2,1)S(1)}, u32[]{:S(2)}, u32[]{:S(2)}) collective-permute-start(bf16[2,128,4,128]{3,2,1,0:T(4,128)(2,1)S(1)} %get-tuple-element.920), channel_id=1, source_target_pairs={{8,0},{16,8},{24,16},{32,24},{40,32},{48,40},{56,48},{64,56},{72,6... | collective-permute-start | bytes 786440 | tf_op jit(solution)/shard_map/while/body/eval_jaxpr/ppermute | solution.py:10
  250.3 11.6 %collective-permute-start.1 = (bf16[2,128,4,128]{3,2,1,0:T(4,128)(2,1)S(1)}, bf16[2,128,4,128]{3,2,1,0:T(4,128)(2,1)S(1)}, u32[]{:S(2)}, u32[]{:S(2)}) collective-permute-start(bf16[2,128,4,128]{3,2,1,0:T(4,128)(2,1)S(1)} %get-tuple-element.921), channel_id=1, source_target_pairs={{0,8},{8,16},{16,24},{24,32},{32,40},{40,48},{48,56},{56,64},{64,7... | collective-permute-start | bytes 786440 | tf_op jit(solution)/shard_map/while/body/eval_jaxpr/ppermute | solution.py:10
  525.8 11.7 %collective-permute-start.2 = (bf16[2,128,4,128]{3,2,1,0:T(4,128)(2,1)S(1)}, bf16[2,128,4,128]{3,2,1,0:T(4,128)(2,1)S(1)}, u32[]{:S(2)}, u32[]{:S(2)}) collective-permute-start(bf16[2,128,4,128]{3,2,1,0:T(4,128)(2,1)S(1)} %get-tuple-element.934), channel_id=1, source_target_pairs={{0,8},{8,16},{16,24},{24,32},{32,40},{40,48},{48,56},{56,64},{64,7... | collective-permute-start | bytes 786440 | tf_op jit(solution)/shard_map/while/body/eval_jaxpr/ppermute | solution.py:10
  533.6 11.6 %collective-permute-start.3 = (bf16[2,128,4,128]{3,2,1,0:T(4,128)(2,1)S(1)}, bf16[2,128,4,128]{3,2,1,0:T(4,128)(2,1)S(1)}, u32[]{:S(2)}, u32[]{:S(2)}) collective-permute-start(bf16[2,128,4,128]{3,2,1,0:T(4,128)(2,1)S(1)} %get-tuple-element.935), channel_id=1, source_target_pairs={{8,0},{16,8},{24,16},{32,24},{40,32},{48,40},{56,48},{64,56},{72,6... | collective-permute-start | bytes 786440 | tf_op jit(solution)/shard_map/while/body/eval_jaxpr/ppermute | solution.py:10
  549.1 11.6 %collective-permute-start.3 = (bf16[2,128,4,128]{3,2,1,0:T(4,128)(2,1)S(1)}, bf16[2,128,4,128]{3,2,1,0:T(4,128)(2,1)S(1)}, u32[]{:S(2)}, u32[]{:S(2)}) collective-permute-start(bf16[2,128,4,128]{3,2,1,0:T(4,128)(2,1)S(1)} %get-tuple-element.935), channel_id=1, source_target_pairs={{8,0},{16,8},{24,16},{32,24},{40,32},{48,40},{56,48},{64,56},{72,6... | collective-permute-start | bytes 786440 | tf_op jit(solution)/shard_map/while/body/eval_jaxpr/ppermute | solution.py:10
  564.5 11.6 %collective-permute-start.3 = (bf16[2,128,4,128]{3,2,1,0:T(4,128)(2,1)S(1)}, bf16[2,128,4,128]{3,2,1,0:T(4,128)(2,1)S(1)}, u32[]{:S(2)}, u32[]{:S(2)}) collective-permute-start(bf16[2,128,4,128]{3,2,1,0:T(4,128)(2,1)S(1)} %get-tuple-element.935), channel_id=1, source_target_pairs={{8,0},{16,8},{24,16},{32,24},{40,32},{48,40},{56,48},{64,56},{72,6... | collective-permute-start | bytes 786440 | tf_op jit(solution)/shard_map/while/body/eval_jaxpr/ppermute | solution.py:10
  580.0 11.6 %collective-permute-start.3 = (bf16[2,128,4,128]{3,2,1,0:T(4,128)(2,1)S(1)}, bf16[2,128,4,128]{3,2,1,0:T(4,128)(2,1)S(1)}, u32[]{:S(2)}, u32[]{:S(2)}) collective-permute-start(bf16[2,128,4,128]{3,2,1,0:T(4,128)(2,1)S(1)} %get-tuple-element.935), channel_id=1, source_target_pairs={{8,0},{16,8},{24,16},{32,24},{40,32},{48,40},{56,48},{64,56},{72,6... | collective-permute-start | bytes 786440 | tf_op jit(solution)/shard_map/while/body/eval_jaxpr/ppermute | solution.py:10
  595.4 11.6 %collective-permute-start.3 = (bf16[2,128,4,128]{3,2,1,0:T(4,128)(2,1)S(1)}, bf16[2,128,4,128]{3,2,1,0:T(4,128)(2,1)S(1)}, u32[]{:S(2)}, u32[]{:S(2)}) collective-permute-start(bf16[2,128,4,128]{3,2,1,0:T(4,128)(2,1)S(1)} %get-tuple-element.935), channel_id=1, source_target_pairs={{8,0},{16,8},{24,16},{32,24},{40,32},{48,40},{56,48},{64,56},{72,6... | collective-permute-start | bytes 786440 | tf_op jit(solution)/shard_map/while/body/eval_jaxpr/ppermute | solution.py:10
  610.9 11.6 %collective-permute-start.3 = (bf16[2,128,4,128]{3,2,1,0:T(4,128)(2,1)S(1)}, bf16[2,128,4,128]{3,2,1,0:T(4,128)(2,1)S(1)}, u32[]{:S(2)}, u32[]{:S(2)}) collective-permute-start(bf16[2,128,4,128]{3,2,1,0:T(4,128)(2,1)S(1)} %get-tuple-element.935), channel_id=1, source_target_pairs={{8,0},{16,8},{24,16},{32,24},{40,32},{48,40},{56,48},{64,56},{72,6... | collective-permute-start | bytes 786440 | tf_op jit(solution)/shard_map/while/body/eval_jaxpr/ppermute | solution.py:10
  626.4 11.6 %collective-permute-start.3 = (bf16[2,128,4,128]{3,2,1,0:T(4,128)(2,1)S(1)}, bf16[2,128,4,128]{3,2,1,0:T(4,128)(2,1)S(1)}, u32[]{:S(2)}, u32[]{:S(2)}) collective-permute-start(bf16[2,128,4,128]{3,2,1,0:T(4,128)(2,1)S(1)} %get-tuple-element.935), channel_id=1, source_target_pairs={{8,0},{16,8},{24,16},{32,24},{40,32},{48,40},{56,48},{64,56},{72,6... | collective-permute-start | bytes 786440 | tf_op jit(solution)/shard_map/while/body/eval_jaxpr/ppermute | solution.py:10
  641.8 12.5 %collective-permute-start.3 = (bf16[2,128,4,128]{3,2,1,0:T(4,128)(2,1)S(1)}, bf16[2,128,4,128]{3,2,1,0:T(4,128)(2,1)S(1)}, u32[]{:S(2)}, u32[]{:S(2)}) collective-permute-start(bf16[2,128,4,128]{3,2,1,0:T(4,128)(2,1)S(1)} %get-tuple-element.935), channel_id=1, source_target_pairs={{8,0},{16,8},{24,16},{32,24},{40,32},{48,40},{56,48},{64,56},{72,6... | collective-permute-start | bytes 786440 | tf_op jit(solution)/shard_map/while/body/eval_jaxpr/ppermute | solution.py:10
  658.2 13.7 %collective-permute-start.3 = (bf16[2,128,4,128]{3,2,1,0:T(4,128)(2,1)S(1)}, bf16[2,128,4,128]{3,2,1,0:T(4,128)(2,1)S(1)}, u32[]{:S(2)}, u32[]{:S(2)}) collective-permute-start(bf16[2,128,4,128]{3,2,1,0:T(4,128)(2,1)S(1)} %get-tuple-element.935), channel_id=1, source_target_pairs={{8,0},{16,8},{24,16},{32,24},{40,32},{48,40},{56,48},{64,56},{72,6... | collective-permute-start | bytes 786440 | tf_op jit(solution)/shard_map/while/body/eval_jaxpr/ppermute | solution.py:10
  675.7 14.0 %collective-permute-start.3 = (bf16[2,128,4,128]{3,2,1,0:T(4,128)(2,1)S(1)}, bf16[2,128,4,128]{3,2,1,0:T(4,128)(2,1)S(1)}, u32[]{:S(2)}, u32[]{:S(2)}) collective-permute-start(bf16[2,128,4,128]{3,2,1,0:T(4,128)(2,1)S(1)} %get-tuple-element.935), channel_id=1, source_target_pairs={{8,0},{16,8},{24,16},{32,24},{40,32},{48,40},{56,48},{64,56},{72,6... | collective-permute-start | bytes 786440 | tf_op jit(solution)/shard_map/while/body/eval_jaxpr/ppermute | solution.py:10
  693.6 13.2 %collective-permute-start.3 = (bf16[2,128,4,128]{3,2,1,0:T(4,128)(2,1)S(1)}, bf16[2,128,4,128]{3,2,1,0:T(4,128)(2,1)S(1)}, u32[]{:S(2)}, u32[]{:S(2)}) collective-permute-start(bf16[2,128,4,128]{3,2,1,0:T(4,128)(2,1)S(1)} %get-tuple-element.935), channel_id=1, source_target_pairs={{8,0},{16,8},{24,16},{32,24},{40,32},{48,40},{56,48},{64,56},{72,6... | collective-permute-start | bytes 786440 | tf_op jit(solution)/shard_map/while/body/eval_jaxpr/ppermute | solution.py:10
  710.6 12.3 %collective-permute-start.3 = (bf16[2,128,4,128]{3,2,1,0:T(4,128)(2,1)S(1)}, bf16[2,128,4,128]{3,2,1,0:T(4,128)(2,1)S(1)}, u32[]{:S(2)}, u32[]{:S(2)}) collective-permute-start(bf16[2,128,4,128]{3,2,1,0:T(4,128)(2,1)S(1)} %get-tuple-element.935), channel_id=1, source_target_pairs={{8,0},{16,8},{24,16},{32,24},{40,32},{48,40},{56,48},{64,56},{72,6... | collective-permute-start | bytes 786440 | tf_op jit(solution)/shard_map/while/body/eval_jaxpr/ppermute | solution.py:10
  726.8 11.6 %collective-permute-start.3 = (bf16[2,128,4,128]{3,2,1,0:T(4,128)(2,1)S(1)}, bf16[2,128,4,128]{3,2,1,0:T(4,128)(2,1)S(1)}, u32[]{:S(2)}, u32[]{:S(2)}) collective-permute-start(bf16[2,128,4,128]{3,2,1,0:T(4,128)(2,1)S(1)} %get-tuple-element.935), channel_id=1, source_target_pairs={{8,0},{16,8},{24,16},{32,24},{40,32},{48,40},{56,48},{64,56},{72,6... | collective-permute-start | bytes 786440 | tf_op jit(solution)/shard_map/while/body/eval_jaxpr/ppermute | solution.py:10
  742.2 11.6 %collective-permute-start.3 = (bf16[2,128,4,128]{3,2,1,0:T(4,128)(2,1)S(1)}, bf16[2,128,4,128]{3,2,1,0:T(4,128)(2,1)S(1)}, u32[]{:S(2)}, u32[]{:S(2)}) collective-permute-start(bf16[2,128,4,128]{3,2,1,0:T(4,128)(2,1)S(1)} %get-tuple-element.935), channel_id=1, source_target_pairs={{8,0},{16,8},{24,16},{32,24},{40,32},{48,40},{56,48},{64,56},{72,6... | collective-permute-start | bytes 786440 | tf_op jit(solution)/shard_map/while/body/eval_jaxpr/ppermute | solution.py:10
  757.7 11.6 %collective-permute-start.3 = (bf16[2,128,4,128]{3,2,1,0:T(4,128)(2,1)S(1)}, bf16[2,128,4,128]{3,2,1,0:T(4,128)(2,1)S(1)}, u32[]{:S(2)}, u32[]{:S(2)}) collective-permute-start(bf16[2,128,4,128]{3,2,1,0:T(4,128)(2,1)S(1)} %get-tuple-element.935), channel_id=1, source_target_pairs={{8,0},{16,8},{24,16},{32,24},{40,32},{48,40},{56,48},{64,56},{72,6... | collective-permute-start | bytes 786440 | tf_op jit(solution)/shard_map/while/body/eval_jaxpr/ppermute | solution.py:10
  (55 other events, 906.0 us)
where the time goes:
time: 804 us; the launch traced here: 792 us
  starting transfers between devices  251 us (31%)
  waiting for transfers between devices  200 us (25%)
  other arithmetic  144 us (18%)
  matrix products  95.5 us (12%)
  local copies, waits for them, and re-layouts  86.5 us (11%)
  loops' own time  13.8 us (2%)
    ppermute x64, starting transfers between devices, shifted(): lax.ppermute(value, axis, [(source, source + steps) for source in range(i...  251 us
    ppermute x64, waiting for transfers between devices, shifted(): lax.ppermute(value, axis, [(source, source + steps) for source in range(i...  200 us
    another operation x3, other arithmetic, body(): term_all = jnp.stack(term_list, axis=1)  40.6 us
    sub x8, matrix products, softmax_rows(): expons = jnp.exp(scores - top_score)  37 us
    add x16, other arithmetic, pass_back(): jnp.stack([from_below, from_above], axis=0)  25.5 us
    another operation x4, local copies, waits for them, and re-layouts, body(): jnp.stack([grad_keys, grad_values], axis=0)  25.4 us
    convert_element_type x8, other arithmetic, head_dense(): weights_low = weights.astype(jnp.bfloat16)  22.1 us
    and x8, other arithmetic, body(): (query_doc[:, None] == key_doc[None, :]) & (key_pos[None, :] <= token_pos...  18.1 us
  transfers between devices with their start and end apart: 64, of which 64 were waited for; matrix products, arithmetic and copies ran while one was open for 0% of the time, Pallas kernels for 0%

commit v1 on v0

--- a/solution.py
+++ b/solution.py
@@ -1,7 +1,148 @@
+import functools
+
 import jax
 import jax.numpy as jnp
 from jax import lax
 from jax.sharding import PartitionSpec as P
+
+from jax.experimental import pallas as pl
+from jax.experimental.pallas import tpu as pltpu
+
+ROUNDS = 16
+
+
+def greet_neighbours(me, count):
+    barrier = pltpu.get_barrier_semaphore()
+
+    @pl.when(me > 0)
+    def _():
+        pl.semaphore_signal(barrier, 1, device_id={"seq": me - 1})
+
+    @pl.when(me < count - 1)
+    def _():
+        pl.semaphore_signal(barrier, 1, device_id={"seq": me + 1})
+
+    @pl.when(jnp.logical_and(me > 0, me < count - 1))
+    def _():
+        pl.semaphore_wait(barrier, 2)
+
+    @pl.when(jnp.logical_or(me == 0, me == count - 1))
+    def _():
+        pl.semaphore_wait(barrier, 1)
+
+
+def forward_chain_kernel(count, cur, hist, send_sem, recv_sem, local_sem):
+    me = lax.axis_index("seq")
+    greet_neighbours(me, count)
+    for k in range(1, ROUNDS + 1):
+        slot = ROUNDS - k
+        src_a = cur.at[0] if k == 1 else hist.at[slot + 1, 0]
+        src_b = cur.at[1] if k == 1 else hist.at[slot + 1, 1]
+        send_a = pltpu.make_async_remote_copy(
+            src_a, hist.at[slot, 0], send_sem.at[slot, 0], recv_sem.at[slot, 0],
+            device_id={"seq": me + 1})
+        send_b = pltpu.make_async_remote_copy(
+            src_b, hist.at[slot, 1], send_sem.at[slot, 1], recv_sem.at[slot, 1],
+            device_id={"seq": me - 1})
+        local_b = pltpu.make_async_copy(src_a, hist.at[slot, 1], local_sem.at[slot])
+        a_sends = jnp.logical_and(me < count - 1, me >= k - 1)
+        a_gets = me >= k
+        b_sends = me > 0
+        b_gets = me < count - 1
+        pl.when(a_sends)(send_a.start)
+        pl.when(b_sends)(send_b.start)
+        pl.when(me == count - 1)(local_b.start)
+
+        @pl.when(jnp.logical_not(a_gets))
+        def _():
+            hist[slot, 0] = jnp.zeros(hist.shape[2:], hist.dtype)
+
+        pl.when(a_gets)(send_a.wait_recv)
+        pl.when(b_gets)(send_b.wait_recv)
+        pl.when(me == count - 1)(local_b.wait)
+        pl.when(a_sends)(send_a.wait_send)
+        pl.when(b_sends)(send_b.wait_send)
+
+
+def backward_chain_kernel(count, terms, out, send_buf, recv_buf, send_sem, recv_sem, local_sem):
+    me = lax.axis_index("seq")
+    greet_neighbours(me, count)
+    send_buf[0] = terms[0].astype(send_buf.dtype)
+    for t in range(1, ROUNDS + 1):
+        slot = t - 1
+        send_a = pltpu.make_async_remote_copy(
+            send_buf.at[slot, 0], recv_buf.at[slot, 0], send_sem.at[slot, 0], recv_sem.at[slot, 0],
+            device_id={"seq": me - 1})
+        send_b = pltpu.make_async_remote_copy(
+            send_buf.at[slot, 1], recv_buf.at[slot, 1], send_sem.at[slot, 1], recv_sem.at[slot, 1],
+            device_id={"seq": me + 1})
+        local_b = pltpu.make_async_copy(send_buf.at[slot, 1], recv_buf.at[slot, 0], local_sem.at[slot])
+        pl.when(me > 0)(send_a.start)
+        pl.when(me < count - 1)(send_b.start)
+        pl.when(me == count - 1)(local_b.start)
+        pl.when(me < count - 1)(send_a.wait_recv)
+        pl.when(me == count - 1)(local_b.wait)
+        pl.when(me > 0)(send_b.wait_recv)
+        pl.when(me > 0)(send_a.wait_send)
+        pl.when(me < count - 1)(send_b.wait_send)
+        total_a = recv_buf[slot, 0].astype(jnp.float32) + terms[t, 0]
+
+        @pl.when(me > 0)
+        def _():
+            total_b = recv_buf[slot, 1].astype(jnp.float32) + terms[t, 1]
+            if t < ROUNDS:
+                send_buf[t, 1] = total_b.astype(send_buf.dtype)
+            else:
+                out[1] = total_b.astype(out.dtype)
+
+        @pl.when(me == 0)
+        def _():
+            total_b = terms[t, 1]
+            if t < ROUNDS:
+                send_buf[t, 1] = total_b.astype(send_buf.dtype)
+            else:
+                out[1] = total_b.astype(out.dtype)
+
+        if t < ROUNDS:
+            send_buf[t, 0] = total_a.astype(send_buf.dtype)
+        else:
+            out[0] = total_a.astype(out.dtype)
+
+
+def forward_chain(current, count):
+    shape = current.shape
+    return pl.pallas_call(
+        functools.partial(forward_chain_kernel, count),
+        out_shape=jax.ShapeDtypeStruct((ROUNDS,) + shape, current.dtype),
+        in_specs=[pl.BlockSpec(memory_space=pltpu.VMEM)],
+        out_specs=pl.BlockSpec(memory_space=pltpu.VMEM),
+        scratch_shapes=[
+            pltpu.SemaphoreType.DMA((ROUNDS, 2)),
+            pltpu.SemaphoreType.DMA((ROUNDS, 2)),
+            pltpu.SemaphoreType.DMA((ROUNDS,)),
+        ],
+        compiler_params=pltpu.CompilerParams(
+            collective_id=0, has_side_effects=True, vmem_limit_bytes=48 * 1024 * 1024),
+    )(current)
+
+
+def backward_chain(terms, count):
+    shape = terms.shape[1:]
+    return pl.pallas_call(
+        functools.partial(backward_chain_kernel, count),
+        out_shape=jax.ShapeDtypeStruct(shape, jnp.bfloat16),
+        in_specs=[pl.BlockSpec(memory_space=pltpu.VMEM)],
+        out_specs=pl.BlockSpec(memory_space=pltpu.VMEM),
+        scratch_shapes=[
+            pltpu.VMEM((ROUNDS,) + shape, jnp.bfloat16),
+            pltpu.VMEM((ROUNDS,) + shape, jnp.bfloat16),
+            pltpu.SemaphoreType.DMA((ROUNDS, 2)),
+            pltpu.SemaphoreType.DMA((ROUNDS, 2)),
+            pltpu.SemaphoreType.DMA((ROUNDS,)),
+        ],
+        compiler_params=pltpu.CompilerParams(
+            collective_id=1, has_side_effects=True, vmem_limit_bytes=60 * 1024 * 1024),
+    )(terms)
 
 
 def shifted(value, axis, steps):
@@ -68,20 +209,10 @@
     head_dim = query.shape[4]
     group_size = head_count // kv_heads
     score_scale = head_dim ** (-0.5)
-    last_device = device_index == shard_count - 1
     current = jnp.stack([keys[:, 0], values[:, 0]], axis=1)
 
-    def pass_forward(turn_index, state_now):
-        moving, stored = state_now
-        from_below = shifted(moving[0], "seq", 1)
-        from_above = shifted(moving[1], "seq", -1)
-        from_above = jnp.where(last_device, moving[0], from_above)
-        moving = jnp.stack([from_below, from_above], axis=0)
-        stored = lax.dynamic_update_index_in_dim(stored, moving, window - 1 - turn_index, 0)
-        return (moving, stored)
-
-    history = jnp.zeros((window,) + current.shape, jnp.bfloat16)
-    moving, history = lax.fori_loop(0, window, pass_forward, (current, history))
+    flat = current.reshape(2, 2, span_len * kv_heads, head_dim)
+    history = forward_chain(flat, shard_count).reshape((window,) + current.shape)
     row_ids = jnp.arange(span_len, dtype=jnp.int32)
     key_count = (window + 1) * span_len
     span_firsts = [device_index, 2 * shard_count - 1 - device_index]
@@ -125,15 +256,8 @@
         term_list.append(jnp.transpose(paired, (2, 0, 3, 1, 4)))
     term_all = jnp.stack(term_list, axis=1)
 
-    def pass_back(turn_index, totals):
-        from_below = shifted(totals[0].astype(jnp.bfloat16), "seq", -1).astype(jnp.float32)
-        from_above = shifted(totals[1].astype(jnp.bfloat16), "seq", 1).astype(jnp.float32)
-        from_below = jnp.where(last_device, totals[1], from_below)
-        return jnp.stack([from_below, from_above], axis=0) + lax.dynamic_index_in_dim(
-            term_all, turn_index, 0, keepdims=False
-        )
-
-    totals = lax.fori_loop(1, window + 1, pass_back, term_all[0])
+    term_flat = term_all.reshape(window + 1, 2, 2, span_len * kv_heads, head_dim)
+    totals = backward_chain(term_flat, shard_count).reshape(term_all.shape[1:])
     grad_keys_out = totals[:, 0][:, None].astype(jnp.bfloat16)
     grad_values_out = totals[:, 1][:, None].astype(jnp.bfloat16)
     return (

time: 804 us -> 598 us (0.74)
  Pallas kernels: 0 us -> 276 us
  starting transfers between devices: 251 us -> 0 us
  waiting for transfers between devices: 200 us -> 0 us
  other arithmetic: 144 us -> 120 us
  local copies, waits for them, and re-layouts: 86.5 us -> 74.3 us
  matrix products: 95.5 us -> 104 us
    pallas_call x0 -> x2, Pallas kernels: none -> 276 us  [the longest x1 142 us: backward_chain(): pl.pallas_call(functools.partial(backward_chain_kernel, count), out_shape...]
    ppermute x64 -> x0, starting transfers between devices: 251 us -> none  [shifted(): lax.ppermute(value, axis, [(source, source + steps) for source in range(i...]
    ppermute x64 -> x0, waiting for transfers between devices: 200 us -> none  [shifted(): lax.ppermute(value, axis, [(source, source + steps) for source in range(i...]
    another operation x3 -> x1, other arithmetic: 40.6 us -> 12.2 us  [body(): term_all = jnp.stack(term_list, axis=1)]
    add x16 -> x0, other arithmetic: 25.5 us -> none  [pass_back(): jnp.stack([from_below, from_above], axis=0)]
    reduce_sum x34, other arithmetic: 12.3 us -> 36.6 us  [count_block(): return jnp.sum(below, axis=1) - 1]
    dynamic_update_slice x16 -> x0, local copies, waits for them, and re-layouts: 14.8 us -> none  [pass_forward(): lax.dynamic_update_index_in_dim(stored, moving, window - 1 - turn_index, 0)]
    another operation x65 -> x2, other arithmetic: 11.1 us -> 21.5 us  [body(): jnp.stack([grad_keys, grad_values], axis=0)]
  transfers between devices with their start and end apart: 64 -> 0, of which waited for: 64 -> 0; matrix products, arithmetic and copies ran while one was open for 0% -> 0% of each run, Pallas kernels for 0% -> 0%
where the time goes in v1:
time: 598 us; the launch traced here: 587 us
  Pallas kernels  276 us (46%)
  other arithmetic  120 us (20%)
  matrix products  104 us (17%)
  local copies, waits for them, and re-layouts  74.3 us (12%)
  loops' own time  13 us (2%)
    pallas_call x1, Pallas kernels, backward_chain(): pl.pallas_call(functools.partial(backward_chain_kernel, count), out_shape...  142 us
    pallas_call x1, Pallas kernels, forward_chain(): pl.pallas_call(functools.partial(forward_chain_kernel, count), out_shape=...  134 us
    sub x8, matrix products, softmax_rows(): expons = jnp.exp(scores - top_score)  41 us
    reduce_sum x34, other arithmetic, count_block(): return jnp.sum(below, axis=1) - 1  36.6 us
    another operation x4, local copies, waits for them, and re-layouts, body(): jnp.stack([grad_keys, grad_values], axis=0)  27.7 us
    convert_element_type x8, other arithmetic, head_dense(): weights_low = weights.astype(jnp.bfloat16)  22.1 us
    another operation x2, other arithmetic, body(): jnp.stack([grad_keys, grad_values], axis=0)  21.5 us
    and x8, other arithmetic, body(): (query_doc[:, None] == key_doc[None, :]) & (key_pos[None, :] <= token_pos...  18.1 us

profile of v1, /device:TPU:126, one launch (start us, length us, event | category | flops | bytes accessed | tf_op | source)
XLA Modules:
  0.0 587.4 jit_solution(4576033325380732393)
XLA Ops:
  3.1 133.5 %shard_map.84 = bf16[16,2,2,512,128]{4,3,2,1,0:T(8,128)(2,1)} custom-call(bf16[2,2,512,128]{3,2,1,0:T(8,128)(2,1)S(1)} %bitcast.341), custom_call_target="tpu_custom_call" | custom-call | tf_op jit(solution)/shard_map/pallas_call | solution.py:114
  136.7 6.0 %fusion.120 = (bf16[16,1,2,128,4,128]{5,4,3,2,1,0:T(4,128)(2,1)S(1)}, bf16[16,1,2,128,4,128]{5,4,3,2,1,0:T(4,128)(2,1)S(1)}) fusion(bf16[16,2,2,128,4,128]{5,4,3,2,1,0:T(4,128)(2,1)} %bitcast.344), kind=kLoop, calls=%fused_computation.140 | loop fusion | bytes 16777216 | tf_op jit(solution)/shard_map/slice | solution.py:232
  144.9 2.9 pad_maximum_fusion.3
  151.5 19.6 %while.59 = (s32[]{:T(128)}, s32[17,128]{1,0:T(8,128)S(1)}, s32[4096]{0:T(1024)}, s32[17,128]{1,0:T(8,128)S(1)}, s32[]{:T(128)}, /*index=5*/s32[]{:T(128)}) while((s32[]{:T(128)}, s32[17,128]{1,0:T(8,128)S(1)}, s32[4096]{0:T(1024)}, s32[17,128]{1,0:T(8,128)S(1)}, s32[]{:T(128)}, /*index=5*/s32[]{:T(128)}) %tuple.108), condition=%wide.region_10.11_spmd, body=%wide.region_8.10_spmd.sunk | while | flops 1572866 | bytes 20565 | solution.py:161
  174.7 2.3 broadcast.88.clone
  177.0 2.4 broadcast.88.clone.1
  179.4 75.9 %while.61 = (s32[]{:T(128)}, bf16[4,128,4,128]{1,3,2,0:T(8,128)(2,1)}, bf16[4,128,4,128]{1,3,2,0:T(8,128)(2,1)}, f32[4,2176,128]{2,1,0:T(8,128)}, f32[4,2176,128...) while((s32[]{:T(128)}, ...), condition=%wide.region_15.16_spmd.clone, body=%wide.region_11.15_spmd.clone.sunk | while | flops 1724761728 | bytes 59783452 | solution.py:243
  180.0 2.3 compare_and_fusion.5
  182.3 5.1 fusion.195
  187.4 2.8 fusion.196
  192.6 2.3 fusion.198
  199.0 2.3 compare_and_fusion.5
  201.3 5.1 fusion.195
  206.4 2.8 fusion.196
  218.0 2.3 compare_and_fusion.5
  220.3 5.1 fusion.195
  225.4 2.8 fusion.196
  236.9 2.3 compare_and_fusion.5
  239.2 5.1 fusion.195
  244.3 2.8 fusion.196
  260.3 19.6 %while.58 = (s32[]{:T(128)}, s32[17,128]{1,0:T(8,128)S(1)}, s32[4096]{0:T(1024)}, s32[17,128]{1,0:T(8,128)S(1)}, s32[]{:T(128)}, /*index=5*/s32[]{:T(128)}) while((s32[]{:T(128)}, s32[17,128]{1,0:T(8,128)S(1)}, s32[4096]{0:T(1024)}, s32[17,128]{1,0:T(8,128)S(1)}, s32[]{:T(128)}, /*index=5*/s32[]{:T(128)}) %tuple.128), condition=%wide.region_2.3_spmd, body=%wide.region_0.2_spmd.sunk | while | flops 1572866 | bytes 20565 | solution.py:161
  283.6 2.4 broadcast.88.clone.2
  286.0 2.3 broadcast.88.clone.3
  288.3 86.5 %while.60 = (s32[]{:T(128)}, bf16[4,128,4,128]{1,3,2,0:T(8,128)(2,1)}, bf16[4,128,4,128]{1,3,2,0:T(8,128)(2,1)}, f32[4,2176,128]{2,1,0:T(8,128)}, f32[4,2176,128...) while((s32[]{:T(128)}, ...), condition=%wide.region_7.8_spmd.clone, body=%wide.region_3.7_spmd.clone.sunk | while | flops 1724761728 | bytes 50870528 | solution.py:243
  300.8 2.3 compare_and_fusion.4
  303.0 5.1 fusion.178
  308.1 2.8 fusion.179
  313.1 2.3 fusion.181
  319.4 2.3 compare_and_fusion.4
  321.7 5.1 fusion.178
  326.8 2.8 fusion.179
  331.7 2.3 fusion.181
  338.1 2.3 compare_and_fusion.4
  340.3 5.1 fusion.178
  345.4 2.8 fusion.179
  350.4 2.3 fusion.181
  356.7 2.3 compare_and_fusion.4
  359.0 5.1 fusion.178
  364.1 2.8 fusion.179
  369.0 2.3 fusion.181
  381.5 7.6 %copy.98 = f32[1,4,17,128,128]{4,1,3,0,2:T(4,128)} copy(f32[1,4,17,128,128]{4,3,2,1,0:T(8,128)} %bitcast.350) | data formatting | bytes 8912896 | tf_op jit(solution)/shard_map/stack | solution.py:253
  389.1 5.1 copy.97
  394.2 10.8 %pad_maximum_fusion.2 = f32[2,4,17,128,128]{4,1,3,0,2:T(4,128)} fusion(f32[1,4,17,128,128]{4,1,3,0,2:T(4,128)} %copy.98, f32[1,4,17,128,128]{4,1,3,0,2:T(4,128)} %copy.97), kind=kLoop, calls=%fused_computation.114 | loop fusion | flops 2228224 | bytes 17825792 | tf_op jit(solution)/shard_map/stack | solution.py:253
  405.0 7.5 %copy.96 = f32[1,4,17,128,128]{4,1,3,0,2:T(4,128)} copy(f32[1,4,17,128,128]{4,3,2,1,0:T(8,128)} %bitcast.346) | data formatting | bytes 8912896 | tf_op jit(solution)/shard_map/stack | solution.py:253
  412.5 7.4 %copy.95 = f32[1,4,17,128,128]{4,1,3,0,2:T(4,128)} copy(f32[1,4,17,128,128]{4,3,2,1,0:T(8,128)} %bitcast.345) | data formatting | bytes 8912896 | tf_op jit(solution)/shard_map/stack | solution.py:253
  420.0 10.7 %pad_maximum_fusion.1 = f32[2,4,17,128,128]{4,1,3,0,2:T(4,128)} fusion(f32[1,4,17,128,128]{4,1,3,0,2:T(4,128)} %copy.96, f32[1,4,17,128,128]{4,1,3,0,2:T(4,128)} %copy.95), kind=kLoop, calls=%fused_computation.113 | loop fusion | flops 2228224 | bytes 17825792 | tf_op jit(solution)/shard_map/stack | solution.py:253
  430.7 12.2 %pad_maximum_fusion.terms = f32[17,2,2,512,128]{4,3,2,1,0:T(8,128)} fusion(f32[17,1,2,512,128]{4,3,2,1,0:T(8,128)} %bitcast.342, f32[17,1,2,512,128]{4,3,2,1,0:T(8,128)} %bitcast.343), kind=kLoop, calls=%fused_computation.112 | loop fusion | flops 4456448 | bytes 35651584 | tf_op jit(solution)/shard_map/stack | solution.py:257
  442.8 142.3 %shard_map.85 = bf16[2,2,512,128]{3,2,1,0:T(8,128)(2,1)} custom-call(f32[17,2,2,512,128]{4,3,2,1,0:T(8,128)} %pad_maximum_fusion.terms), custom_call_target="tpu_custom_call" | custom-call | tf_op jit(solution)/shard_map/pallas_call | solution.py:131
  (295 shorter events, 125.4 us)
Async XLA Ops:
  144.9 2.9 copy-start.4
  144.9 4.0 copy-start.5
  179.4 0.6 copy-start.6
  187.4 3.0 copy-start.2
  187.4 4.3 copy-start
  187.4 4.3 copy-start.10
  196.6 1.8 copy-start.7
  198.4 0.6 copy-start.6
  206.4 3.0 copy-start.2
  206.4 4.3 copy-start
  206.4 4.3 copy-start.10
  215.6 1.7 copy-start.7
  217.4 0.6 copy-start.6
  225.4 3.0 copy-start.2
  225.4 4.3 copy-start
  225.4 4.3 copy-start.10
  234.6 1.7 copy-start.7
  236.3 0.6 copy-start.6
  244.3 3.0 copy-start.2
  244.3 4.3 copy-start
  244.3 4.3 copy-start.10
  253.5 1.8 copy-start.7
  300.2 0.6 copy-start.8
  308.1 4.0 copy-start.1
  308.1 4.0 copy-start.11
  317.1 1.7 copy-start.9
  318.8 0.6 copy-start.8
  326.8 4.0 copy-start.1
  326.8 4.0 copy-start.11
  335.7 1.8 copy-start.9
  337.5 0.6 copy-start.8
  345.4 4.0 copy-start.1
  345.4 4.0 copy-start.11
  354.4 1.8 copy-start.9
  356.1 0.6 copy-start.8
  364.1 4.0 copy-start.1
  364.1 4.0 copy-start.11
  373.1 1.7 copy-start.9
  374.8 5.1 copy-start.3
  380.0 9.1 %slice-start = ((s8[4456448]{0:T(1024)(128)(4,1)}), s8[262144]{0:T(1024)(128)(4,1)S(1)}, s32[]{:S(2)}) async-start(s8[4456448]{0:T(1024)(128)(4,1)} %bitcast.347), calls=%async_computation | async-start | bytes 524288
  381.5 7.6 %slice-start.1 = ((s8[4456448]{0:T(1024)(128)(4,1)}), s8[4194304]{0:T(1024)(128)(4,1)S(1)}, s32[]{:S(2)}) async-start(s8[4456448]{0:T(1024)(128)(4,1)} %bitcast.347), calls=%async_computation.1 | async-start | bytes 8388608

commit v2 on v1

v2 whole, which is shorter than its diff:
```python
import functools

import jax
import jax.numpy as jnp
from jax import lax
from jax.sharding import PartitionSpec as P

from jax.experimental import pallas as pl
from jax.experimental.pallas import tpu as pltpu

ROUNDS = 16


def greet_neighbours(me, count):
    barrier = pltpu.get_barrier_semaphore()

    @pl.when(me > 0)
    def _():
        pl.semaphore_signal(barrier, 1, device_id={"seq": me - 1})

    @pl.when(me < count - 1)
    def _():
        pl.semaphore_signal(barrier, 1, device_id={"seq": me + 1})

    @pl.when(jnp.logical_and(me > 0, me < count - 1))
    def _():
        pl.semaphore_wait(barrier, 2)

    @pl.when(jnp.logical_or(me == 0, me == count - 1))
    def _():
        pl.semaphore_wait(barrier, 1)


def forward_chain_kernel(count, cur, hist, send_sem, recv_sem, local_sem):
    me = lax.axis_index("seq")
    own = pltpu.make_async_copy(cur, hist.at[ROUNDS], local_sem.at[ROUNDS])
    own.start()
    greet_neighbours(me, count)
    for k in range(1, ROUNDS + 1):
        slot = ROUNDS - k
        src_a = cur.at[0] if k == 1 else hist.at[slot + 1, 0]
        src_b = cur.at[1] if k == 1 else hist.at[slot + 1, 1]
        send_a = pltpu.make_async_remote_copy(
            src_a, hist.at[slot, 0], send_sem.at[slot, 0], recv_sem.at[slot, 0],
            device_id={"seq": me + 1})
        send_b = pltpu.make_async_remote_copy(
            src_b, hist.at[slot, 1], send_sem.at[slot, 1], recv_sem.at[slot, 1],
            device_id={"seq": me - 1})
        local_b = pltpu.make_async_copy(src_a, hist.at[slot, 1], local_sem.at[slot])
        a_sends = jnp.logical_and(me < count - 1, me >= k - 1)
        a_gets = me >= k
        b_sends = me > 0
        b_gets = me < count - 1
        pl.when(a_sends)(send_a.start)
        pl.when(b_sends)(send_b.start)
        pl.when(me == count - 1)(local_b.start)

        @pl.when(jnp.logical_not(a_gets))
        def _():
            hist[slot, 0] = jnp.zeros(hist.shape[2:], hist.dtype)

        pl.when(a_gets)(send_a.wait_recv)
        pl.when(b_gets)(send_b.wait_recv)
        pl.when(me == count - 1)(local_b.wait)
        pl.when(a_sends)(send_a.wait_send)
        pl.when(b_sends)(send_b.wait_send)
    own.wait()


def backward_chain_kernel(count, terms, out, send_buf, recv_buf, send_sem, recv_sem, local_sem):
    me = lax.axis_index("seq")
    greet_neighbours(me, count)
    send_buf[0] = terms[0].astype(send_buf.dtype)
    for t in range(1, ROUNDS + 1):
        slot = t - 1
        send_a = pltpu.make_async_remote_copy(
            send_buf.at[slot, 0], recv_buf.at[slot, 0], send_sem.at[slot, 0], recv_sem.at[slot, 0],
            device_id={"seq": me - 1})
        send_b = pltpu.make_async_remote_copy(
            send_buf.at[slot, 1], recv_buf.at[slot, 1], send_sem.at[slot, 1], recv_sem.at[slot, 1],
            device_id={"seq": me + 1})
        local_b = pltpu.make_async_copy(send_buf.at[slot, 1], recv_buf.at[slot, 0], local_sem.at[slot])
        pl.when(me > 0)(send_a.start)
        pl.when(me < count - 1)(send_b.start)
        pl.when(me == count - 1)(local_b.start)
        pl.when(me < count - 1)(send_a.wait_recv)
        pl.when(me == count - 1)(local_b.wait)
        pl.when(me > 0)(send_b.wait_recv)
        pl.when(me > 0)(send_a.wait_send)
        pl.when(me < count - 1)(send_b.wait_send)
        total_a = recv_buf[slot, 0].astype(jnp.float32) + terms[t, 0]

        @pl.when(me > 0)
        def _():
            total_b = recv_buf[slot, 1].astype(jnp.float32) + terms[t, 1]
            if t < ROUNDS:
                send_buf[t, 1] = total_b.astype(send_buf.dtype)
            else:
                out[1] = total_b.astype(out.dtype)

        @pl.when(me == 0)
        def _():
            total_b = terms[t, 1]
            if t < ROUNDS:
                send_buf[t, 1] = total_b.astype(send_buf.dtype)
            else:
                out[1] = total_b.astype(out.dtype)

        if t < ROUNDS:
            send_buf[t, 0] = total_a.astype(send_buf.dtype)
        else:
            out[0] = total_a.astype(out.dtype)


def forward_chain(current, count):
    shape = current.shape
    return pl.pallas_call(
        functools.partial(forward_chain_kernel, count),
        out_shape=jax.ShapeDtypeStruct((ROUNDS + 1,) + shape, current.dtype),
        in_specs=[pl.BlockSpec(memory_space=pltpu.VMEM)],
        out_specs=pl.BlockSpec(memory_space=pltpu.VMEM),
        scratch_shapes=[
            pltpu.SemaphoreType.DMA((ROUNDS, 2)),
            pltpu.SemaphoreType.DMA((ROUNDS, 2)),
            pltpu.SemaphoreType.DMA((ROUNDS + 1,)),
        ],
        compiler_params=pltpu.CompilerParams(
            collective_id=0, has_side_effects=True, vmem_limit_bytes=48 * 1024 * 1024),
    )(current)


def backward_chain(terms, count):
    shape = terms.shape[1:]
    return pl.pallas_call(
        functools.partial(backward_chain_kernel, count),
        out_shape=jax.ShapeDtypeStruct(shape, jnp.bfloat16),
        in_specs=[pl.BlockSpec(memory_space=pltpu.VMEM)],
        out_specs=pl.BlockSpec(memory_space=pltpu.VMEM),
        scratch_shapes=[
            pltpu.VMEM((ROUNDS,) + shape, jnp.bfloat16),
            pltpu.VMEM((ROUNDS,) + shape, jnp.bfloat16),
            pltpu.SemaphoreType.DMA((ROUNDS, 2)),
            pltpu.SemaphoreType.DMA((ROUNDS, 2)),
            pltpu.SemaphoreType.DMA((ROUNDS,)),
        ],
        compiler_params=pltpu.CompilerParams(
            collective_id=1, has_side_effects=True, vmem_limit_bytes=60 * 1024 * 1024),
    )(terms)


def attention_kernel(skip_ref, q_ref, do_ref, win_ref, qdoc_ref, kdoc_ref,
                     o_ref, dq_ref, terms_ref):
    stream = pl.program_id(0)
    first = skip_ref[stream]
    group, span_len, head_dim = q_ref.shape[1:]
    rows = group * span_len
    last = win_ref.shape[0] - 1
    scale = head_dim ** (-0.5)
    q = q_ref[0].reshape(rows, head_dim)
    grad_output = do_ref[0].reshape(rows, head_dim)
    query_doc = qdoc_ref[0]
    later = lax.broadcasted_iota(jnp.int32, (span_len, span_len), 1) > lax.broadcasted_iota(
        jnp.int32, (span_len, span_len), 0)
    contract_last = (((1,), (1,)), ((), ()))
    contract_first = (((0,), (0,)), ((), ()))

    def scores(j, causal):
        sc = lax.dot_general(q, win_ref[j, 0, 0, 0], contract_last,
                             preferred_element_type=jnp.float32) * scale
        allowed = query_doc == kdoc_ref[0, j]
        if causal:
            allowed = jnp.logical_and(allowed, jnp.logical_not(later))
        sc = jnp.where(allowed[None], sc.reshape(group, span_len, span_len), -jnp.inf)
        return sc.reshape(rows, span_len)

    sc = scores(last, True)
    top = jnp.max(sc, axis=1, keepdims=True)
    total = jnp.sum(jnp.exp(sc - top), axis=1, keepdims=True)

    def stat_step(j, carry):
        top, total = carry
        sc = scores(j, False)
        new_top = jnp.maximum(top, jnp.max(sc, axis=1, keepdims=True))
        total = total * jnp.exp(top - new_top) + jnp.sum(jnp.exp(sc - new_top), axis=1, keepdims=True)
        return new_top, total

    top, total = lax.fori_loop(first, last, stat_step, (top, total))
    inverse = 1.0 / total

    def weights(j, causal):
        return jnp.exp(scores(j, causal) - top) * inverse

    def out_step(j, acc, causal=False):
        low = weights(j, causal).astype(jnp.bfloat16)
        return acc + jnp.dot(low, win_ref[j, 0, 1, 0], preferred_element_type=jnp.float32)

    acc = out_step(last, jnp.zeros((rows, head_dim), jnp.float32), True)
    acc = lax.fori_loop(first, last, out_step, acc)
    attended = acc.astype(jnp.bfloat16)
    o_ref[0] = attended.reshape(group, span_len, head_dim)
    delta = jnp.sum(grad_output.astype(jnp.float32) * attended.astype(jnp.float32), axis=1, keepdims=True)

    def grad_step(j, dq, causal=False):
        prob = weights(j, causal)
        low = prob.astype(jnp.bfloat16)
        key_j = win_ref[j, 0, 0, 0]
        grad_w = lax.dot_general(grad_output, win_ref[j, 0, 1, 0], contract_last,
                                 preferred_element_type=jnp.float32)
        grad_s = (prob * (grad_w - delta) * scale).astype(jnp.bfloat16)
        terms_ref[j, 0, 0, 0] = lax.dot_general(grad_s, q, contract_first,
                                                preferred_element_type=jnp.float32)
        terms_ref[j, 0, 1, 0] = lax.dot_general(low, grad_output, contract_first,
                                                preferred_element_type=jnp.float32)
        return dq + jnp.dot(grad_s, key_j, preferred_element_type=jnp.float32)

    dq = grad_step(last, jnp.zeros((rows, head_dim), jnp.float32), True)
    dq = lax.fori_loop(first, last, grad_step, dq)
    dq_ref[0] = dq.astype(jnp.bfloat16).reshape(group, span_len, head_dim)

    def clear(j, carry):
        terms_ref[j] = jnp.zeros(terms_ref.shape[1:], terms_ref.dtype)
        return carry

    lax.fori_loop(0, first, clear, 0)


def attention(skip, q, grad_out, window, query_doc, key_doc, group):
    streams, heads, span_len, head_dim = q.shape
    kv_heads = heads // group
    spans = window.shape[0]
    head_block = pl.BlockSpec((1, group, span_len, head_dim), lambda s, h, sk: (s, h, 0, 0))
    return pl.pallas_call(
        attention_kernel,
        out_shape=(
            jax.ShapeDtypeStruct(q.shape, jnp.bfloat16),
            jax.ShapeDtypeStruct(q.shape, jnp.bfloat16),
            jax.ShapeDtypeStruct((spans, streams, 2, kv_heads, span_len, head_dim), jnp.float32),
        ),
        grid_spec=pltpu.PrefetchScalarGridSpec(
            num_scalar_prefetch=1,
            grid=(streams, kv_heads),
            in_specs=[
                head_block,
                head_block,
                pl.BlockSpec((spans, 1, 2, 1, span_len, head_dim), lambda s, h, sk: (0, s, 0, h, 0, 0)),
                pl.BlockSpec((1, span_len, 1), lambda s, h, sk: (s, 0, 0)),
                pl.BlockSpec((1, spans, 1, span_len), lambda s, h, sk: (s, 0, 0, 0)),
            ],
            out_specs=[
                head_block,
                head_block,
                pl.BlockSpec((spans, 1, 2, 1, span_len, head_dim), lambda s, h, sk: (0, s, 0, h, 0, 0)),
            ],
        ),
        compiler_params=pltpu.CompilerParams(vmem_limit_bytes=48 * 1024 * 1024),
    )(skip, q, grad_out, window, query_doc, key_doc)


def body(query, keys, values, grad_out, doc_starts):
    shard_count = lax.axis_size("seq")
    device_index = lax.axis_index("seq")
    window = ROUNDS
    span_len = query.shape[2]
    kv_heads = keys.shape[3]
    head_dim = query.shape[4]
    group = query.shape[3] // kv_heads
    q = jnp.transpose(query[:, 0], (0, 2, 1, 3))
    grad_o = jnp.transpose(grad_out[:, 0], (0, 2, 1, 3))
    current = jnp.stack([jnp.transpose(keys[:, 0], (0, 2, 1, 3)),
                         jnp.transpose(values[:, 0], (0, 2, 1, 3))], axis=1)
    flat = current.reshape(2, 2, kv_heads * span_len, head_dim)
    spans = forward_chain(flat, shard_count).reshape((window + 1,) + current.shape)
    span_firsts = jnp.stack([device_index, 2 * shard_count - 1 - device_index])
    key_pos = (span_firsts[:, None] - window) * span_len + jnp.arange(
        (window + 1) * span_len, dtype=jnp.int32)[None]
    key_doc = (jnp.searchsorted(doc_starts, key_pos, side="right") - 1).astype(jnp.int32)
    key_doc = key_doc.reshape(2, window + 1, span_len)
    query_doc = key_doc[:, window]
    skip = jnp.sum(key_doc[:, :window, span_len - 1] < query_doc[:, :1], axis=1).astype(jnp.int32)
    attended, grad_q, terms = attention(
        skip, q, grad_o, spans, query_doc[:, :, None], key_doc[:, :, None, :], group)
    term_flat = terms.reshape(window + 1, 2, 2, kv_heads * span_len, head_dim)
    totals = backward_chain(term_flat, shard_count).reshape(current.shape)
    grad_kv = jnp.transpose(totals, (1, 0, 3, 2, 4))[:, :, None]
    return (
        jnp.transpose(attended, (0, 2, 1, 3))[:, None],
        jnp.transpose(grad_q, (0, 2, 1, 3))[:, None],
        grad_kv[0],
        grad_kv[1],
    )


def solution(mesh):
    placed = (
        P("batch", "seq", None, "head", None),
        P("batch", "seq", None, "head", None),
        P("batch", "seq", None, "head", None),
        P("batch", "seq", None, "head", None),
        P("batch"),
    )
    return jax.shard_map(
        body,
        mesh=mesh,
        in_specs=placed,
        out_specs=(
            P("batch", "seq", None, "head", None),
            P("batch", "seq", None, "head", None),
            P("batch", "seq", None, "head", None),
            P("batch", "seq", None, "head", None),
        ),
        check_vma=False,
    )
```

time: 598 us -> 677 us (1.13); the launches traced: 587 us -> 676 us
  local copies, waits for them, and re-layouts: 74.3 us -> 260 us
  Pallas kernels: 276 us -> 412 us
  other arithmetic: 120 us -> 1.89 us
  matrix products: 104 us -> 0 us
  loops' own time: 13 us -> 0.66 us
    gather x0 -> x13, local copies, waits for them, and re-layouts: none -> 253 us  [body(): jnp.searchsorted(doc_starts, key_pos, side='right') - 1]
    pallas_call x0 -> x1, Pallas kernels: none -> 135 us  [attention(): pl.pallas_call(attention_kernel, out_shape=(jax.ShapeDtypeStruct(q.shape,...]
    dot_general x40 -> x0, matrix products: 62.7 us -> none  [the longest x8 18 us: head_dense(): jnp.einsum('grj,jd->rgd', grad_scores, key_window, preferred_element_type...]
    another operation x16 -> x2, local copies, waits for them, and re-layouts: 42.3 us -> 0.17 us  [the longest x1 0.14 us: body(): query_doc[:, :, None]]
    sub x8 -> x0, matrix products: 41 us -> none  [softmax_rows(): expons = jnp.exp(scores - top_score)]
    reduce_sum x42 -> x1, other arithmetic: 37.1 us -> 0.18 us  [body(): jnp.sum(key_doc[:, :window, span_len - 1] < query_doc[:, :1], axis=1)]
    another operation x3 -> x1, other arithmetic: 33.7 us -> 0.05 us  [body(): jnp.stack([jnp.transpose(keys[:, 0], (0, 2, 1, 3)), jnp.transpose(values[...]
    convert_element_type x8 -> x0, other arithmetic: 22.1 us -> none  [head_dense(): weights_low = weights.astype(jnp.bfloat16)]
where the time goes in v2:
time: 677 us; the launch traced here: 676 us
  Pallas kernels  412 us (61%)
  local copies, waits for them, and re-layouts  260 us (38%)
    gather x13, local copies, waits for them, and re-layouts, body(): jnp.searchsorted(doc_starts, key_pos, side='right') - 1  253 us
    pallas_call x1, Pallas kernels, backward_chain(): pl.pallas_call(functools.partial(backward_chain_kernel, count), out_shape...  143 us
    pallas_call x1, Pallas kernels, attention(): pl.pallas_call(attention_kernel, out_shape=(jax.ShapeDtypeStruct(q.shape,...  135 us
    pallas_call x1, Pallas kernels, forward_chain(): pl.pallas_call(functools.partial(forward_chain_kernel, count), out_shape=...  134 us

profile of v2, /device:TPU:126, one launch (start us, length us, event | category | flops | bytes accessed | tf_op | source)
XLA Modules:
  0.0 675.7 jit_solution(1525394430418690969)
XLA Ops:
  0.6 0.1 fusion.5
  0.7 0.0 copy-start.2
  0.7 0.0 copy-start.3
  0.7 0.0 copy-start.1
  0.7 255.8 %while.27 = (s32[]{:T(128)}, u32[2,2176]{1,0:T(2,128)S(1)}, u32[2,2176]{1,0:T(2,128)S(1)}, s32[4096]{0:T(1024)}, s32[2]{0:T(128)S(1)}, /*index=5*/s32[]{:T(128)}, s32[]{:T(128)}, s32[]{}) while((s32[]{:T(128)}, u32[2,2176]{1,0:T(2,128)S(1)}, u32[2,2176]{1,0:T(2,128)S(1)}, s32[4096]{0:T(1024)}, s32[2]{0:T(128)S(1)}, ...), condition=%wide.region_1.2_spmd.clone, body=%wide.region_0.1_spmd.clone.sunk | while | flops 66052 | bytes 299124 | solution.py:276
  0.8 19.6 %gather_fusion = s32[4352]{0:T(1024)S(1)} fusion(s32[4096]{0:T(1024)} %get-tuple-element.183, u32[5120]{0:T(1024)S(1)} %pad_clamp_fusion.2), kind=kCustom, calls=%fused_computation.clone.clone.1 | custom fusion | bytes 52224 | tf_op jit(solution)/shard_map/jit(searchsorted)/jit(_searchsorted_scan_impl)/vmap(jit(_searchsorted_scan_impl))/while/body/eval_jaxpr/gather | solution.py:276
  20.5 0.1 fusion.7
  20.6 19.5 %gather_fusion = s32[4352]{0:T(1024)S(1)} fusion(s32[4096]{0:T(1024)} %get-tuple-element.183, u32[5120]{0:T(1024)S(1)} %pad_clamp_fusion.2), kind=kCustom, calls=%fused_computation.clone.clone.1 | custom fusion | bytes 52224 | tf_op jit(solution)/shard_map/jit(searchsorted)/jit(_searchsorted_scan_impl)/vmap(jit(_searchsorted_scan_impl))/while/body/eval_jaxpr/gather | solution.py:276
  40.1 0.1 fusion.7
  40.3 19.5 %gather_fusion = s32[4352]{0:T(1024)S(1)} fusion(s32[4096]{0:T(1024)} %get-tuple-element.183, u32[5120]{0:T(1024)S(1)} %pad_clamp_fusion.2), kind=kCustom, calls=%fused_computation.clone.clone.1 | custom fusion | bytes 52224 | tf_op jit(solution)/shard_map/jit(searchsorted)/jit(_searchsorted_scan_impl)/vmap(jit(_searchsorted_scan_impl))/while/body/eval_jaxpr/gather | solution.py:276
  59.8 0.1 fusion.7
  60.0 19.5 %gather_fusion = s32[4352]{0:T(1024)S(1)} fusion(s32[4096]{0:T(1024)} %get-tuple-element.183, u32[5120]{0:T(1024)S(1)} %pad_clamp_fusion.2), kind=kCustom, calls=%fused_computation.clone.clone.1 | custom fusion | bytes 52224 | tf_op jit(solution)/shard_map/jit(searchsorted)/jit(_searchsorted_scan_impl)/vmap(jit(_searchsorted_scan_impl))/while/body/eval_jaxpr/gather | solution.py:276
  79.5 0.1 fusion.7
  79.6 19.5 %gather_fusion = s32[4352]{0:T(1024)S(1)} fusion(s32[4096]{0:T(1024)} %get-tuple-element.183, u32[5120]{0:T(1024)S(1)} %pad_clamp_fusion.2), kind=kCustom, calls=%fused_computation.clone.clone.1 | custom fusion | bytes 52224 | tf_op jit(solution)/shard_map/jit(searchsorted)/jit(_searchsorted_scan_impl)/vmap(jit(_searchsorted_scan_impl))/while/body/eval_jaxpr/gather | solution.py:276
  99.1 0.1 fusion.7
  99.3 19.5 %gather_fusion = s32[4352]{0:T(1024)S(1)} fusion(s32[4096]{0:T(1024)} %get-tuple-element.183, u32[5120]{0:T(1024)S(1)} %pad_clamp_fusion.2), kind=kCustom, calls=%fused_computation.clone.clone.1 | custom fusion | bytes 52224 | tf_op jit(solution)/shard_map/jit(searchsorted)/jit(_searchsorted_scan_impl)/vmap(jit(_searchsorted_scan_impl))/while/body/eval_jaxpr/gather | solution.py:276
  118.8 0.1 fusion.7
  119.0 19.5 %gather_fusion = s32[4352]{0:T(1024)S(1)} fusion(s32[4096]{0:T(1024)} %get-tuple-element.183, u32[5120]{0:T(1024)S(1)} %pad_clamp_fusion.2), kind=kCustom, calls=%fused_computation.clone.clone.1 | custom fusion | bytes 52224 | tf_op jit(solution)/shard_map/jit(searchsorted)/jit(_searchsorted_scan_impl)/vmap(jit(_searchsorted_scan_impl))/while/body/eval_jaxpr/gather | solution.py:276
  138.5 0.1 fusion.7
  138.6 19.5 %gather_fusion = s32[4352]{0:T(1024)S(1)} fusion(s32[4096]{0:T(1024)} %get-tuple-element.183, u32[5120]{0:T(1024)S(1)} %pad_clamp_fusion.2), kind=kCustom, calls=%fused_computation.clone.clone.1 | custom fusion | bytes 52224 | tf_op jit(solution)/shard_map/jit(searchsorted)/jit(_searchsorted_scan_impl)/vmap(jit(_searchsorted_scan_impl))/while/body/eval_jaxpr/gather | solution.py:276
  158.1 0.1 fusion.7
  158.3 19.5 %gather_fusion = s32[4352]{0:T(1024)S(1)} fusion(s32[4096]{0:T(1024)} %get-tuple-element.183, u32[5120]{0:T(1024)S(1)} %pad_clamp_fusion.2), kind=kCustom, calls=%fused_computation.clone.clone.1 | custom fusion | bytes 52224 | tf_op jit(solution)/shard_map/jit(searchsorted)/jit(_searchsorted_scan_impl)/vmap(jit(_searchsorted_scan_impl))/while/body/eval_jaxpr/gather | solution.py:276
  177.8 0.1 fusion.7
  178.0 19.5 %gather_fusion = s32[4352]{0:T(1024)S(1)} fusion(s32[4096]{0:T(1024)} %get-tuple-element.183, u32[5120]{0:T(1024)S(1)} %pad_clamp_fusion.2), kind=kCustom, calls=%fused_computation.clone.clone.1 | custom fusion | bytes 52224 | tf_op jit(solution)/shard_map/jit(searchsorted)/jit(_searchsorted_scan_impl)/vmap(jit(_searchsorted_scan_impl))/while/body/eval_jaxpr/gather | solution.py:276
  197.5 0.1 fusion.7
  197.6 19.5 %gather_fusion = s32[4352]{0:T(1024)S(1)} fusion(s32[4096]{0:T(1024)} %get-tuple-element.183, u32[5120]{0:T(1024)S(1)} %pad_clamp_fusion.2), kind=kCustom, calls=%fused_computation.clone.clone.1 | custom fusion | bytes 52224 | tf_op jit(solution)/shard_map/jit(searchsorted)/jit(_searchsorted_scan_impl)/vmap(jit(_searchsorted_scan_impl))/while/body/eval_jaxpr/gather | solution.py:276
  217.1 0.1 fusion.7
  217.3 19.5 %gather_fusion = s32[4352]{0:T(1024)S(1)} fusion(s32[4096]{0:T(1024)} %get-tuple-element.183, u32[5120]{0:T(1024)S(1)} %pad_clamp_fusion.2), kind=kCustom, calls=%fused_computation.clone.clone.1 | custom fusion | bytes 52224 | tf_op jit(solution)/shard_map/jit(searchsorted)/jit(_searchsorted_scan_impl)/vmap(jit(_searchsorted_scan_impl))/while/body/eval_jaxpr/gather | solution.py:276
  236.8 0.1 fusion.7
  237.0 19.5 %gather_fusion = s32[4352]{0:T(1024)S(1)} fusion(s32[4096]{0:T(1024)} %get-tuple-element.183, u32[5120]{0:T(1024)S(1)} %pad_clamp_fusion.2), kind=kCustom, calls=%fused_computation.clone.clone.1 | custom fusion | bytes 52224 | tf_op jit(solution)/shard_map/jit(searchsorted)/jit(_searchsorted_scan_impl)/vmap(jit(_searchsorted_scan_impl))/while/body/eval_jaxpr/gather | solution.py:276
  256.5 0.1 fusion.7
  256.7 0.2 slice_reduce_fusion
  256.8 0.1 slice_reduce_fusion.1
  256.9 0.2 fusion.4.skip_ref
  257.1 0.1 copy.39.qdoc_ref
  257.3 0.0 copy-done.2
  257.3 0.0 copy-done.3
  257.4 0.1 pad_maximum_fusion.cur
  257.5 0.0 copy-done
  257.5 0.0 copy-done.1
  257.5 0.5 copy_bitcast_fusion
  258.0 133.9 %shard_map.84 = bf16[17,2,2,512,128]{4,3,2,1,0:T(8,128)(2,1)} custom-call(bf16[2,2,512,128]{3,2,1,0:T(8,128)(2,1)S(1)} %pad_maximum_fusion.cur), custom_call_target="tpu_custom_call" | custom-call | tf_op jit(solution)/shard_map/pallas_call | solution.py:117
  391.9 134.6 %shard_map.85 = (bf16[2,16,128,128]{3,2,1,0:T(8,128)(2,1)S(1)}, bf16[2,16,128,128]{3,2,1,0:T(8,128)(2,1)S(1)}, f32[17,2,2,4,128,128]{5,4,3,2,1,0:T(8,128)}) custom-call(s32[2]{0:T(128)S(1)} %fusion.4.skip_ref, bf16[2,16,128,128]{3,2,1,0:T(8,128)(2,1)S(1)} %get-tuple-element.128.q_ref, bf16[2,16,128,128]{3,2,1,0:T(8,128)(2,1)S(1)} %get-tuple-element.127.do_ref, ...), custom_call_target="tpu_custom_call" | custom-call | tf_op jit(solution)/shard_map/pallas_call | solution.py:232
  526.5 1.6 copy.41
  528.2 1.6 copy.42
  529.8 143.5 %shard_map.86 = bf16[2,2,512,128]{3,2,1,0:T(8,128)(2,1)} custom-call(f32[17,2,2,512,128]{4,3,2,1,0:T(8,128)} %bitcast.39), custom_call_target="tpu_custom_call" | custom-call | tf_op jit(solution)/shard_map/pallas_call | solution.py:134
  673.3 1.5 copy.46
  674.8 1.0 slice_bitcast_fusion
  (61 shorter events, 0.9 us)
Async XLA Ops:
  0.7 256.6 %copy-start.2 = (bf16[2,1,128,4,128]{4,3,2,1,0:T(4,128)(2,1)S(1)}, bf16[2,1,128,4,128]{4,3,2,1,0:T(4,128)(2,1)}, u32[]{:S(2)}) copy-start(bf16[2,1,128,4,128]{4,3,2,1,0:T(4,128)(2,1)} %param.8) | copy-start | bytes 786436
  0.7 256.6 %copy-start.3 = (bf16[2,1,128,4,128]{4,3,2,1,0:T(4,128)(2,1)S(1)}, bf16[2,1,128,4,128]{4,3,2,1,0:T(4,128)(2,1)}, u32[]{:S(2)}) copy-start(bf16[2,1,128,4,128]{4,3,2,1,0:T(4,128)(2,1)} %param.9) | copy-start | bytes 786436
  0.7 256.7 %copy-start = (bf16[2,1,128,16,128]{4,3,2,1,0:T(8,128)(2,1)S(1)}, bf16[2,1,128,16,128]{4,3,2,1,0:T(8,128)(2,1)}, u32[]{:S(2)}) copy-start(bf16[2,1,128,16,128]{4,3,2,1,0:T(8,128)(2,1)} %param.10) | copy-start | bytes 3145732
  0.7 256.7 %copy-start.1 = (bf16[2,1,128,16,128]{4,3,2,1,0:T(8,128)(2,1)S(1)}, bf16[2,1,128,16,128]{4,3,2,1,0:T(8,128)(2,1)}, u32[]{:S(2)}) copy-start(bf16[2,1,128,16,128]{4,3,2,1,0:T(8,128)(2,1)} %param.7) | copy-start | bytes 3145732

commit v3 on v2

--- a/solution.py
+++ b/solution.py
@@ -256,6 +256,16 @@
     )(skip, q, grad_out, window, query_doc, key_doc)
 
 
+def window_docs(doc_starts, key_pos):
+    width = key_pos.shape[1]
+    before = jnp.sum((doc_starts[None, :] < key_pos[:, :1]).astype(jnp.int32), axis=1)
+    padded = jnp.concatenate(
+        [doc_starts, jnp.full((width // 2,), jnp.iinfo(jnp.int32).max, doc_starts.dtype)])
+    local = jnp.stack([lax.dynamic_slice_in_dim(padded, before[i], width // 2) for i in range(2)])
+    inside = jnp.sum((local[:, None, :] <= key_pos[:, :, None]).astype(jnp.int32), axis=2)
+    return before[:, None] + inside - 1
+
+
 def body(query, keys, values, grad_out, doc_starts):
     shard_count = lax.axis_size("seq")
     device_index = lax.axis_index("seq")
@@ -273,7 +283,7 @@
     span_firsts = jnp.stack([device_index, 2 * shard_count - 1 - device_index])
     key_pos = (span_firsts[:, None] - window) * span_len + jnp.arange(
         (window + 1) * span_len, dtype=jnp.int32)[None]
-    key_doc = (jnp.searchsorted(doc_starts, key_pos, side="right") - 1).astype(jnp.int32)
+    key_doc = window_docs(doc_starts, key_pos)
     key_doc = key_doc.reshape(2, window + 1, span_len)
     query_doc = key_doc[:, window]
     skip = jnp.sum(key_doc[:, :window, span_len - 1] < query_doc[:, :1], axis=1).astype(jnp.int32)

time: 677 us -> 416 us (0.61)
  local copies, waits for them, and re-layouts: 260 us -> 11.8 us
  Pallas kernels: 412 us -> 395 us
    gather x13 -> x0, local copies, waits for them, and re-layouts: 253 us -> none  [body(): jnp.searchsorted(doc_starts, key_pos, side='right') - 1]
    pallas_call x1, Pallas kernels: 135 us -> 114 us  [attention(): pl.pallas_call(attention_kernel, out_shape=(jax.ShapeDtypeStruct(q.shape,...]
where the time goes in v3:
time: 416 us
  Pallas kernels  395 us (95%)
  local copies, waits for them, and re-layouts  11.8 us (3%)
  between operations  4.63 us (1%)
  other arithmetic  4.26 us (1%)
    pallas_call x1, Pallas kernels, backward_chain(): pl.pallas_call(functools.partial(backward_chain_kernel, count), out_shape...  147 us
    pallas_call x1, Pallas kernels, forward_chain(): pl.pallas_call(functools.partial(forward_chain_kernel, count), out_shape=...  134 us
    pallas_call x1, Pallas kernels, attention(): pl.pallas_call(attention_kernel, out_shape=(jax.ShapeDtypeStruct(q.shape,...  114 us

profile of v3, /device:TPU:126, one launch (start us, length us, event | category | flops | bytes accessed | tf_op | source)
XLA Modules:
  0.0 415.6 jit_solution(17629381910748363259)
XLA Ops:
  0.6 0.0 copy-start
  0.6 0.1 fusion.2
  0.7 1.1 copy.51
  1.8 1.0 copy.52
  2.8 0.1 pad_maximum_fusion.cur
  2.8 0.1 iota_add_fusion
  2.9 0.3 copy.48
  3.3 1.0 fusion
  4.2 0.6 fusion.3
  8.7 0.9 pad_dynamic-slice_fusion.1
  9.6 2.7 convert_reduce_fusion
  12.4 0.1 add_add_fusion.1.kdoc_ref
  12.5 0.1 add_add_fusion
  12.6 0.2 slice_reduce_fusion
  12.8 0.1 slice_reduce_fusion.1
  12.9 0.2 fusion.1.skip_ref
  13.1 0.1 copy.53.qdoc_ref
  13.2 0.0 copy-done
  13.2 1.8 copy_bitcast_fusion
  15.0 133.9 %shard_map.84 = bf16[17,2,2,512,128]{4,3,2,1,0:T(8,128)(2,1)} custom-call(bf16[2,2,512,128]{3,2,1,0:T(8,128)(2,1)S(1)} %pad_maximum_fusion.cur), custom_call_target="tpu_custom_call" | custom-call | tf_op jit(solution)/shard_map/pallas_call | solution.py:117
  148.8 113.8 %shard_map.85 = (bf16[2,16,128,128]{3,2,1,0:T(8,128)(2,1)S(1)}, bf16[2,16,128,128]{3,2,1,0:T(8,128)(2,1)S(1)}, f32[17,2,2,4,128,128]{5,4,3,2,1,0:T(8,128)}) custom-call(s32[2]{0:T(128)S(1)} %fusion.1.skip_ref, bf16[2,16,128,128]{3,2,1,0:T(8,128)(2,1)S(1)} %get-tuple-element.37.q_ref, bf16[2,16,128,128]{3,2,1,0:T(8,128)(2,1)S(1)} %get-tuple-element.36.do_ref, ...), custom_call_target="tpu_custom_call" | custom-call | tf_op jit(solution)/shard_map/pallas_call | solution.py:232
  262.6 1.6 copy.55
  264.3 1.6 copy.56
  265.9 147.2 %shard_map.86 = bf16[2,2,512,128]{3,2,1,0:T(8,128)(2,1)} custom-call(f32[17,2,2,512,128]{4,3,2,1,0:T(8,128)} %bitcast.43), custom_call_target="tpu_custom_call" | custom-call | tf_op jit(solution)/shard_map/pallas_call | solution.py:134
  413.2 1.5 copy.60
  414.6 1.0 slice_bitcast_fusion
  (7 shorter events, 0.1 us)
Async XLA Ops:
  0.6 12.6 %copy-start = (bf16[2,1,128,16,128]{4,3,2,1,0:T(8,128)(2,1)S(1)}, bf16[2,1,128,16,128]{4,3,2,1,0:T(8,128)(2,1)}, u32[]{:S(2)}) copy-start(bf16[2,1,128,16,128]{4,3,2,1,0:T(8,128)(2,1)} %param.8) | copy-start | bytes 3145732

commit v4 on v3

--- a/solution.py
+++ b/solution.py
@@ -149,7 +149,7 @@
 
 
 def attention_kernel(skip_ref, q_ref, do_ref, win_ref, qdoc_ref, kdoc_ref,
-                     o_ref, dq_ref, terms_ref):
+                     o_ref, dq_ref, terms_ref, cache):
     stream = pl.program_id(0)
     first = skip_ref[stream]
     group, span_len, head_dim = q_ref.shape[1:]
@@ -159,63 +159,62 @@
     q = q_ref[0].reshape(rows, head_dim)
     grad_output = do_ref[0].reshape(rows, head_dim)
     query_doc = qdoc_ref[0]
-    later = lax.broadcasted_iota(jnp.int32, (span_len, span_len), 1) > lax.broadcasted_iota(
-        jnp.int32, (span_len, span_len), 0)
+    later = lax.broadcasted_iota(jnp.int32, (span_len, span_len), 0) > lax.broadcasted_iota(
+        jnp.int32, (span_len, span_len), 1)
     contract_last = (((1,), (1,)), ((), ()))
-    contract_first = (((0,), (0,)), ((), ()))
 
     def scores(j, causal):
-        sc = lax.dot_general(q, win_ref[j, 0, 0, 0], contract_last,
+        sc = lax.dot_general(win_ref[j, 0, 0, 0], q, contract_last,
                              preferred_element_type=jnp.float32) * scale
-        allowed = query_doc == kdoc_ref[0, j]
+        allowed = kdoc_ref[0, j] == query_doc
         if causal:
             allowed = jnp.logical_and(allowed, jnp.logical_not(later))
-        sc = jnp.where(allowed[None], sc.reshape(group, span_len, span_len), -jnp.inf)
-        return sc.reshape(rows, span_len)
+        allowed = jnp.tile(allowed, (1, group))
+        sc = jnp.where(allowed, sc, -jnp.inf)
+        cache[j] = sc
+        return sc
 
     sc = scores(last, True)
-    top = jnp.max(sc, axis=1, keepdims=True)
-    total = jnp.sum(jnp.exp(sc - top), axis=1, keepdims=True)
+    top = jnp.max(sc, axis=0, keepdims=True)
+    total = jnp.sum(jnp.exp(sc - top), axis=0, keepdims=True)
 
     def stat_step(j, carry):
         top, total = carry
         sc = scores(j, False)
-        new_top = jnp.maximum(top, jnp.max(sc, axis=1, keepdims=True))
-        total = total * jnp.exp(top - new_top) + jnp.sum(jnp.exp(sc - new_top), axis=1, keepdims=True)
+        new_top = jnp.maximum(top, jnp.max(sc, axis=0, keepdims=True))
+        total = total * jnp.exp(top - new_top) + jnp.sum(jnp.exp(sc - new_top), axis=0, keepdims=True)
         return new_top, total
 
     top, total = lax.fori_loop(first, last, stat_step, (top, total))
     inverse = 1.0 / total
 
-    def weights(j, causal):
-        return jnp.exp(scores(j, causal) - top) * inverse
-
-    def out_step(j, acc, causal=False):
-        low = weights(j, causal).astype(jnp.bfloat16)
-        return acc + jnp.dot(low, win_ref[j, 0, 1, 0], preferred_element_type=jnp.float32)
-
-    acc = out_step(last, jnp.zeros((rows, head_dim), jnp.float32), True)
+    def out_step(j, acc):
+        prob = jnp.exp(cache[j] - top) * inverse
+        cache[j] = prob
+        value_t = win_ref[j, 0, 1, 0].astype(jnp.float32).T.astype(jnp.bfloat16)
+        return acc + jnp.dot(value_t, prob.astype(jnp.bfloat16), preferred_element_type=jnp.float32)
+
+    acc = out_step(last, jnp.zeros((head_dim, rows), jnp.float32))
     acc = lax.fori_loop(first, last, out_step, acc)
-    attended = acc.astype(jnp.bfloat16)
-    o_ref[0] = attended.reshape(group, span_len, head_dim)
-    delta = jnp.sum(grad_output.astype(jnp.float32) * attended.astype(jnp.float32), axis=1, keepdims=True)
-
-    def grad_step(j, dq, causal=False):
-        prob = weights(j, causal)
+    attended_t = acc.astype(jnp.bfloat16)
+    o_ref[0] = attended_t.astype(jnp.float32).T.astype(jnp.bfloat16).reshape(group, span_len, head_dim)
+    grad_t = grad_output.astype(jnp.float32).T
+    delta = jnp.sum(grad_t * attended_t.astype(jnp.float32), axis=0, keepdims=True)
+
+    def grad_step(j, dq):
+        prob = cache[j]
         low = prob.astype(jnp.bfloat16)
-        key_j = win_ref[j, 0, 0, 0]
-        grad_w = lax.dot_general(grad_output, win_ref[j, 0, 1, 0], contract_last,
+        grad_w = lax.dot_general(win_ref[j, 0, 1, 0], grad_output, contract_last,
                                  preferred_element_type=jnp.float32)
         grad_s = (prob * (grad_w - delta) * scale).astype(jnp.bfloat16)
-        terms_ref[j, 0, 0, 0] = lax.dot_general(grad_s, q, contract_first,
-                                                preferred_element_type=jnp.float32)
-        terms_ref[j, 0, 1, 0] = lax.dot_general(low, grad_output, contract_first,
-                                                preferred_element_type=jnp.float32)
-        return dq + jnp.dot(grad_s, key_j, preferred_element_type=jnp.float32)
-
-    dq = grad_step(last, jnp.zeros((rows, head_dim), jnp.float32), True)
+        terms_ref[j, 0, 0, 0] = jnp.dot(grad_s, q, preferred_element_type=jnp.float32)
+        terms_ref[j, 0, 1, 0] = jnp.dot(low, grad_output, preferred_element_type=jnp.float32)
+        key_t = win_ref[j, 0, 0, 0].astype(jnp.float32).T.astype(jnp.bfloat16)
+        return dq + jnp.dot(key_t, grad_s, preferred_element_type=jnp.float32)
+
+    dq = grad_step(last, jnp.zeros((head_dim, rows), jnp.float32))
     dq = lax.fori_loop(first, last, grad_step, dq)
-    dq_ref[0] = dq.astype(jnp.bfloat16).reshape(group, span_len, head_dim)
+    dq_ref[0] = dq.T.astype(jnp.bfloat16).reshape(group, span_len, head_dim)
 
     def clear(j, carry):
         terms_ref[j] = jnp.zeros(terms_ref.shape[1:], terms_ref.dtype)
@@ -243,14 +242,15 @@
                 head_block,
                 head_block,
                 pl.BlockSpec((spans, 1, 2, 1, span_len, head_dim), lambda s, h, sk: (0, s, 0, h, 0, 0)),
-                pl.BlockSpec((1, span_len, 1), lambda s, h, sk: (s, 0, 0)),
-                pl.BlockSpec((1, spans, 1, span_len), lambda s, h, sk: (s, 0, 0, 0)),
+                pl.BlockSpec((1, 1, span_len), lambda s, h, sk: (s, 0, 0)),
+                pl.BlockSpec((1, spans, span_len, 1), lambda s, h, sk: (s, 0, 0, 0)),
             ],
             out_specs=[
                 head_block,
                 head_block,
                 pl.BlockSpec((spans, 1, 2, 1, span_len, head_dim), lambda s, h, sk: (0, s, 0, h, 0, 0)),
             ],
+            scratch_shapes=[pltpu.VMEM((spans, span_len, group * span_len), jnp.float32)],
         ),
         compiler_params=pltpu.CompilerParams(vmem_limit_bytes=48 * 1024 * 1024),
     )(skip, q, grad_out, window, query_doc, key_doc)
@@ -288,7 +288,7 @@
     query_doc = key_doc[:, window]
     skip = jnp.sum(key_doc[:, :window, span_len - 1] < query_doc[:, :1], axis=1).astype(jnp.int32)
     attended, grad_q, terms = attention(
-        skip, q, grad_o, spans, query_doc[:, :, None], key_doc[:, :, None, :], group)
+        skip, q, grad_o, spans, query_doc[:, None, :], key_doc[:, :, :, None], group)
     term_flat = terms.reshape(window + 1, 2, 2, kv_heads * span_len, head_dim)
     totals = backward_chain(term_flat, shard_count).reshape(current.shape)
     grad_kv = jnp.transpose(totals, (1, 0, 3, 2, 4))[:, :, None]

time: 416 us -> 391 us (0.940)
  the two profiles are of different devices: /device:TPU:126 before, /device:TPU:144 now
where the time goes in v4:
time: 391 us
  Pallas kernels  365 us (93%)
  local copies, waits for them, and re-layouts  14.7 us (4%)
  other arithmetic  6.8 us (2%)
  between operations  4.61 us (1%)
    pallas_call x1, Pallas kernels, backward_chain(): pl.pallas_call(functools.partial(backward_chain_kernel, count), out_shape...  143 us
    pallas_call x1, Pallas kernels, forward_chain(): pl.pallas_call(functools.partial(forward_chain_kernel, count), out_shape=...  135 us
    pallas_call x1, Pallas kernels, attention(): pl.pallas_call(attention_kernel, out_shape=(jax.ShapeDtypeStruct(q.shape,...  87.2 us

profile of v4, /device:TPU:144, one launch (start us, length us, event | category | flops | bytes accessed | tf_op | source)
XLA Modules:
  0.0 391.0 jit_solution(573122050889580847)
XLA Ops:
  0.6 0.0 copy-start
  0.6 0.1 fusion.2
  0.7 1.0 copy.38
  1.7 1.0 copy.39
  2.7 0.1 pad_maximum_fusion.cur
  2.8 0.1 iota_add_fusion
  2.9 0.3 copy.35
  3.2 0.0 copy-done
  3.2 0.2 fusion
  3.4 0.6 fusion.3
  7.9 0.1 pad_dynamic-slice_fusion.1
  8.0 2.7 convert_reduce_fusion
  10.8 0.1 add_add_fusion.1
  10.9 0.2 slice_reduce_fusion
  11.1 0.1 slice_reduce_fusion.1
  11.2 0.2 fusion.1.skip_ref
  11.4 2.1 copy_bitcast_fusion
  13.5 3.5 reduce_sum.36
  17.0 3.3 add_add_fusion.kdoc_ref
  20.3 135.0 %shard_map.84 = bf16[17,2,2,512,128]{4,3,2,1,0:T(8,128)(2,1)} custom-call(bf16[2,2,512,128]{3,2,1,0:T(8,128)(2,1)S(1)} %pad_maximum_fusion.cur), custom_call_target="tpu_custom_call" | custom-call | tf_op jit(solution)/shard_map/pallas_call | solution.py:117
  155.4 87.2 %shard_map.85 = (bf16[2,16,128,128]{3,2,1,0:T(8,128)(2,1)S(1)}, bf16[2,16,128,128]{3,2,1,0:T(8,128)(2,1)S(1)}, f32[17,2,2,4,128,128]{5,4,3,2,1,0:T(8,128)}) custom-call(s32[2]{0:T(128)S(1)} %fusion.1.skip_ref, bf16[2,16,128,128]{3,2,1,0:T(8,128)(2,1)S(1)} %get-tuple-element.33.q_ref, bf16[2,16,128,128]{3,2,1,0:T(8,128)(2,1)S(1)} %get-tuple-element.32.do_ref, ...), custom_call_target="tpu_custom_call" | custom-call | tf_op jit(solution)/shard_map/pallas_call | solution.py:231
  242.6 1.6 copy.43
  244.2 1.6 copy.44
  245.9 142.7 %shard_map.86 = bf16[2,2,512,128]{3,2,1,0:T(8,128)(2,1)} custom-call(f32[17,2,2,512,128]{4,3,2,1,0:T(8,128)} %bitcast.43), custom_call_target="tpu_custom_call" | custom-call | tf_op jit(solution)/shard_map/pallas_call | solution.py:134
  388.6 1.5 copy.50
  390.1 1.0 slice_bitcast_fusion
  (6 shorter events, 0.0 us)
Async XLA Ops:
  0.6 2.6 copy-start

commit v5 on v4

--- a/solution.py
+++ b/solution.py
@@ -31,85 +31,132 @@
         pl.semaphore_wait(barrier, 1)
 
 
+PIECES = 4
+
+
+def piece_rows(i, total):
+    size = total // (PIECES // 2)
+    return i // (PIECES // 2), pl.ds((i % (PIECES // 2)) * size, size)
+
+
 def forward_chain_kernel(count, cur, hist, send_sem, recv_sem, local_sem):
     me = lax.axis_index("seq")
-    own = pltpu.make_async_copy(cur, hist.at[ROUNDS], local_sem.at[ROUNDS])
+    own = pltpu.make_async_copy(cur, hist.at[ROUNDS], local_sem.at[ROUNDS, 0])
     own.start()
     greet_neighbours(me, count)
-    for k in range(1, ROUNDS + 1):
+    total = cur.shape[2]
+
+    def copies(k, i):
         slot = ROUNDS - k
-        src_a = cur.at[0] if k == 1 else hist.at[slot + 1, 0]
-        src_b = cur.at[1] if k == 1 else hist.at[slot + 1, 1]
+        kv, rows = piece_rows(i, total)
+        src_a = cur.at[0, kv, rows] if k == 1 else hist.at[slot + 1, 0, kv, rows]
+        src_b = cur.at[1, kv, rows] if k == 1 else hist.at[slot + 1, 1, kv, rows]
         send_a = pltpu.make_async_remote_copy(
-            src_a, hist.at[slot, 0], send_sem.at[slot, 0], recv_sem.at[slot, 0],
+            src_a, hist.at[slot, 0, kv, rows], send_sem.at[slot, 0, i], recv_sem.at[slot, 0, i],
             device_id={"seq": me + 1})
         send_b = pltpu.make_async_remote_copy(
-            src_b, hist.at[slot, 1], send_sem.at[slot, 1], recv_sem.at[slot, 1],
+            src_b, hist.at[slot, 1, kv, rows], send_sem.at[slot, 1, i], recv_sem.at[slot, 1, i],
             device_id={"seq": me - 1})
-        local_b = pltpu.make_async_copy(src_a, hist.at[slot, 1], local_sem.at[slot])
-        a_sends = jnp.logical_and(me < count - 1, me >= k - 1)
-        a_gets = me >= k
-        b_sends = me > 0
-        b_gets = me < count - 1
-        pl.when(a_sends)(send_a.start)
-        pl.when(b_sends)(send_b.start)
-        pl.when(me == count - 1)(local_b.start)
-
-        @pl.when(jnp.logical_not(a_gets))
+        local_b = pltpu.make_async_copy(src_a, hist.at[slot, 1, kv, rows], local_sem.at[slot, i])
+        return send_a, send_b, local_b
+
+    def a_sends(k):
+        return jnp.logical_and(me < count - 1, me >= k - 1)
+
+    def receive(k, i):
+        send_a, send_b, local_b = copies(k, i)
+        pl.when(me >= k)(send_a.wait_recv)
+        pl.when(me < count - 1)(send_b.wait_recv)
+        pl.when(me == count - 1)(local_b.wait)
+
+    for k in range(1, ROUNDS + 1):
+        for i in range(PIECES):
+            if k > 1:
+                receive(k - 1, i)
+            send_a, send_b, local_b = copies(k, i)
+            pl.when(a_sends(k))(send_a.start)
+            pl.when(me > 0)(send_b.start)
+            pl.when(me == count - 1)(local_b.start)
+
+        @pl.when(me < k)
         def _():
-            hist[slot, 0] = jnp.zeros(hist.shape[2:], hist.dtype)
-
-        pl.when(a_gets)(send_a.wait_recv)
-        pl.when(b_gets)(send_b.wait_recv)
-        pl.when(me == count - 1)(local_b.wait)
-        pl.when(a_sends)(send_a.wait_send)
-        pl.when(b_sends)(send_b.wait_send)
+            hist[ROUNDS - k, 0] = jnp.zeros(hist.shape[2:], hist.dtype)
+
+    for i in range(PIECES):
+        receive(ROUNDS, i)
+    for k in range(1, ROUNDS + 1):
+        for i in range(PIECES):
+            send_a, send_b, _ = copies(k, i)
+            pl.when(a_sends(k))(send_a.wait_send)
+            pl.when(me > 0)(send_b.wait_send)
     own.wait()
 
 
 def backward_chain_kernel(count, terms, out, send_buf, recv_buf, send_sem, recv_sem, local_sem):
     me = lax.axis_index("seq")
     greet_neighbours(me, count)
-    send_buf[0] = terms[0].astype(send_buf.dtype)
-    for t in range(1, ROUNDS + 1):
+    total = terms.shape[3]
+
+    def copies(t, i):
         slot = t - 1
+        kv, rows = piece_rows(i, total)
         send_a = pltpu.make_async_remote_copy(
-            send_buf.at[slot, 0], recv_buf.at[slot, 0], send_sem.at[slot, 0], recv_sem.at[slot, 0],
-            device_id={"seq": me - 1})
+            send_buf.at[slot, 0, kv, rows], recv_buf.at[slot, 0, kv, rows],
+            send_sem.at[slot, 0, i], recv_sem.at[slot, 0, i], device_id={"seq": me - 1})
         send_b = pltpu.make_async_remote_copy(
-            send_buf.at[slot, 1], recv_buf.at[slot, 1], send_sem.at[slot, 1], recv_sem.at[slot, 1],
-            device_id={"seq": me + 1})
-        local_b = pltpu.make_async_copy(send_buf.at[slot, 1], recv_buf.at[slot, 0], local_sem.at[slot])
+            send_buf.at[slot, 1, kv, rows], recv_buf.at[slot, 1, kv, rows],
+            send_sem.at[slot, 1, i], recv_sem.at[slot, 1, i], device_id={"seq": me + 1})
+        local_b = pltpu.make_async_copy(
+            send_buf.at[slot, 1, kv, rows], recv_buf.at[slot, 0, kv, rows], local_sem.at[slot, i])
+        return send_a, send_b, local_b
+
+    def start(t, i):
+        send_a, send_b, local_b = copies(t, i)
         pl.when(me > 0)(send_a.start)
         pl.when(me < count - 1)(send_b.start)
         pl.when(me == count - 1)(local_b.start)
-        pl.when(me < count - 1)(send_a.wait_recv)
-        pl.when(me == count - 1)(local_b.wait)
-        pl.when(me > 0)(send_b.wait_recv)
-        pl.when(me > 0)(send_a.wait_send)
-        pl.when(me < count - 1)(send_b.wait_send)
-        total_a = recv_buf[slot, 0].astype(jnp.float32) + terms[t, 0]
-
-        @pl.when(me > 0)
-        def _():
-            total_b = recv_buf[slot, 1].astype(jnp.float32) + terms[t, 1]
+
+    for i in range(PIECES):
+        kv, rows = piece_rows(i, total)
+        send_buf[0, :, kv, rows] = terms[0, :, kv, rows].astype(send_buf.dtype)
+        start(1, i)
+    for t in range(1, ROUNDS + 1):
+        slot = t - 1
+        for i in range(PIECES):
+            kv, rows = piece_rows(i, total)
+            send_a, send_b, local_b = copies(t, i)
+            pl.when(me < count - 1)(send_a.wait_recv)
+            pl.when(me == count - 1)(local_b.wait)
+            pl.when(me > 0)(send_b.wait_recv)
+            total_a = recv_buf[slot, 0, kv, rows].astype(jnp.float32) + terms[t, 0, kv, rows]
             if t < ROUNDS:
-                send_buf[t, 1] = total_b.astype(send_buf.dtype)
+                send_buf[t, 0, kv, rows] = total_a.astype(send_buf.dtype)
             else:
-                out[1] = total_b.astype(out.dtype)
-
-        @pl.when(me == 0)
-        def _():
-            total_b = terms[t, 1]
+                out[0, kv, rows] = total_a.astype(out.dtype)
+
+            @pl.when(me > 0)
+            def _():
+                total_b = recv_buf[slot, 1, kv, rows].astype(jnp.float32) + terms[t, 1, kv, rows]
+                if t < ROUNDS:
+                    send_buf[t, 1, kv, rows] = total_b.astype(send_buf.dtype)
+                else:
+                    out[1, kv, rows] = total_b.astype(out.dtype)
+
+            @pl.when(me == 0)
+            def _():
+                total_b = terms[t, 1, kv, rows]
+                if t < ROUNDS:
+                    send_buf[t, 1, kv, rows] = total_b.astype(send_buf.dtype)
+                else:
+                    out[1, kv, rows] = total_b.astype(out.dtype)
+
             if t < ROUNDS:
-                send_buf[t, 1] = total_b.astype(send_buf.dtype)
-            else:
-                out[1] = total_b.astype(out.dtype)
-
-        if t < ROUNDS:
-            send_buf[t, 0] = total_a.astype(send_buf.dtype)
-        else:
-            out[0] = total_a.astype(out.dtype)
+                start(t + 1, i)
+    for t in range(1, ROUNDS + 1):
+        for i in range(PIECES):
+            send_a, send_b, _ = copies(t, i)
+            pl.when(me > 0)(send_a.wait_send)
+            pl.when(me < count - 1)(send_b.wait_send)
 
 
 def forward_chain(current, count):
@@ -120,9 +167,9 @@
         in_specs=[pl.BlockSpec(memory_space=pltpu.VMEM)],
         out_specs=pl.BlockSpec(memory_space=pltpu.VMEM),
         scratch_shapes=[
-            pltpu.SemaphoreType.DMA((ROUNDS, 2)),
-            pltpu.SemaphoreType.DMA((ROUNDS, 2)),
-            pltpu.SemaphoreType.DMA((ROUNDS + 1,)),
+            pltpu.SemaphoreType.DMA((ROUNDS, 2, PIECES)),
+            pltpu.SemaphoreType.DMA((ROUNDS, 2, PIECES)),
+            pltpu.SemaphoreType.DMA((ROUNDS + 1, PIECES)),
         ],
         compiler_params=pltpu.CompilerParams(
             collective_id=0, has_side_effects=True, vmem_limit_bytes=48 * 1024 * 1024),
@@ -139,9 +186,9 @@
         scratch_shapes=[
             pltpu.VMEM((ROUNDS,) + shape, jnp.bfloat16),
             pltpu.VMEM((ROUNDS,) + shape, jnp.bfloat16),
-            pltpu.SemaphoreType.DMA((ROUNDS, 2)),
-            pltpu.SemaphoreType.DMA((ROUNDS, 2)),
-            pltpu.SemaphoreType.DMA((ROUNDS,)),
+            pltpu.SemaphoreType.DMA((ROUNDS, 2, PIECES)),
+            pltpu.SemaphoreType.DMA((ROUNDS, 2, PIECES)),
+            pltpu.SemaphoreType.DMA((ROUNDS, PIECES)),
         ],
         compiler_params=pltpu.CompilerParams(
             collective_id=1, has_side_effects=True, vmem_limit_bytes=60 * 1024 * 1024),

time: 391 us -> 330 us (0.84)
  the two profiles are of different devices: /device:TPU:144 before, /device:TPU:111 now
where the time goes in v5:
time: 330 us; the launch traced here: 329 us
  Pallas kernels  303 us (92%)
  local copies, waits for them, and re-layouts  14.7 us (4%)
  other arithmetic  6.8 us (2%)
  between operations  4.61 us (1%)
    pallas_call x1, Pallas kernels, attention(): pl.pallas_call(attention_kernel, out_shape=(jax.ShapeDtypeStruct(q.shape,...  106 us
    pallas_call x1, Pallas kernels, forward_chain(): pl.pallas_call(functools.partial(forward_chain_kernel, count), out_shape=...  101 us
    pallas_call x1, Pallas kernels, backward_chain(): pl.pallas_call(functools.partial(backward_chain_kernel, count), out_shape...  96.6 us

profile of v5, /device:TPU:111, one launch (start us, length us, event | category | flops | bytes accessed | tf_op | source)
XLA Modules:
  0.0 329.3 jit_solution(16004364839055331974)
XLA Ops:
  0.6 0.0 copy-start
  0.6 0.1 fusion.2
  0.7 1.0 copy.38
  1.7 1.0 copy.39
  2.7 0.1 pad_maximum_fusion.cur
  2.8 0.1 iota_add_fusion
  2.9 0.3 copy.35
  3.2 0.0 copy-done
  3.2 0.2 fusion
  3.4 0.6 fusion.3
  7.9 0.1 pad_dynamic-slice_fusion.1
  8.0 2.7 convert_reduce_fusion
  10.8 0.1 add_add_fusion.1
  10.9 0.2 slice_reduce_fusion
  11.1 0.1 slice_reduce_fusion.1
  11.2 0.2 fusion.1.skip_ref
  11.4 2.1 copy_bitcast_fusion
  13.5 3.5 %reduce_sum.36 = s32[2,17,128,1]{3,2,1,0:T(8,128)} reshape(s32[2,2176]{1,0:T(2,128)S(1)} %convert_reduce_fusion) | data formatting | bytes 34816 | tf_op jit(solution)/shard_map/reduce_sum | solution.py:312
  17.0 3.3 %add_add_fusion.kdoc_ref = s32[2,17,128,1]{3,2,1,0:T(8,128)} fusion(s32[2,17,128,1]{3,2,1,0:T(8,128)} %reduce_sum.36, s32[2]{0:T(128)S(1)} %fusion), kind=kLoop, calls=%fused_computation.1 | loop fusion | flops 8704 | bytes 34824 | tf_op jit(solution)/shard_map/sub | solution.py:313
  20.3 101.1 %shard_map.84 = bf16[17,2,2,512,128]{4,3,2,1,0:T(8,128)(2,1)} custom-call(bf16[2,2,512,128]{3,2,1,0:T(8,128)(2,1)S(1)} %pad_maximum_fusion.cur), custom_call_target="tpu_custom_call" | custom-call | tf_op jit(solution)/shard_map/pallas_call | solution.py:164
  121.4 105.6 %shard_map.85 = (bf16[2,16,128,128]{3,2,1,0:T(8,128)(2,1)S(1)}, bf16[2,16,128,128]{3,2,1,0:T(8,128)(2,1)S(1)}, f32[17,2,2,4,128,128]{5,4,3,2,1,0:T(8,128)}) custom-call(s32[2]{0:T(128)S(1)} %fusion.1.skip_ref, bf16[2,16,128,128]{3,2,1,0:T(8,128)(2,1)S(1)} %get-tuple-element.33.q_ref, bf16[2,16,128,128]{3,2,1,0:T(8,128)(2,1)S(1)} %get-tuple-element.32.do_ref, ...), custom_call_target="tpu_custom_call" | custom-call | tf_op jit(solution)/shard_map/pallas_call | solution.py:278
  227.0 1.6 copy.43
  228.7 1.6 copy.44
  230.3 96.6 %shard_map.86 = bf16[2,2,512,128]{3,2,1,0:T(8,128)(2,1)} custom-call(f32[17,2,2,512,128]{4,3,2,1,0:T(8,128)} %bitcast.43), custom_call_target="tpu_custom_call" | custom-call | tf_op jit(solution)/shard_map/pallas_call | solution.py:181
  326.9 1.5 copy.50
  328.3 1.0 slice_bitcast_fusion
  (6 shorter events, 0.0 us)
Async XLA Ops:
  0.6 2.6 copy-start

commit v6 on v5

--- a/solution.py
+++ b/solution.py
@@ -31,7 +31,7 @@
         pl.semaphore_wait(barrier, 1)
 
 
-PIECES = 4
+PIECES = 8
 
 
 def piece_rows(i, total):

time: 330 us -> 323 us (0.979)
  the two profiles are of different devices: /device:TPU:111 before, /device:TPU:126 now
where the time goes in v6:
time: 323 us
  Pallas kernels  297 us (92%)
  local copies, waits for them, and re-layouts  14.7 us (5%)
  other arithmetic  6.8 us (2%)
  between operations  4.61 us (1%)
    pallas_call x1, Pallas kernels, forward_chain(): pl.pallas_call(functools.partial(forward_chain_kernel, count), out_shape=...  106 us
    pallas_call x1, Pallas kernels, backward_chain(): pl.pallas_call(functools.partial(backward_chain_kernel, count), out_shape...  104 us
    pallas_call x1, Pallas kernels, attention(): pl.pallas_call(attention_kernel, out_shape=(jax.ShapeDtypeStruct(q.shape,...  87.2 us

profile of v6, /device:TPU:126, one launch (start us, length us, event | category | flops | bytes accessed | tf_op | source)
XLA Modules:
  0.0 322.8 jit_solution(16000312521578575523)
XLA Ops:
  0.6 0.0 copy-start
  0.6 0.1 fusion.2
  0.7 1.0 copy.38
  1.7 1.0 copy.39
  2.7 0.1 pad_maximum_fusion.cur
  2.8 0.1 iota_add_fusion
  2.9 0.3 copy.35
  3.2 0.0 copy-done
  3.2 0.2 fusion
  3.4 0.6 fusion.3
  7.9 0.1 pad_dynamic-slice_fusion.1
  8.0 2.7 convert_reduce_fusion
  10.8 0.1 add_add_fusion.1
  10.9 0.2 slice_reduce_fusion
  11.1 0.1 slice_reduce_fusion.1
  11.2 0.2 fusion.1.skip_ref
  11.4 2.1 copy_bitcast_fusion
  13.5 3.5 %reduce_sum.36 = s32[2,17,128,1]{3,2,1,0:T(8,128)} reshape(s32[2,2176]{1,0:T(2,128)S(1)} %convert_reduce_fusion) | data formatting | bytes 34816 | tf_op jit(solution)/shard_map/reduce_sum | solution.py:312
  17.0 3.3 %add_add_fusion.kdoc_ref = s32[2,17,128,1]{3,2,1,0:T(8,128)} fusion(s32[2,17,128,1]{3,2,1,0:T(8,128)} %reduce_sum.36, s32[2]{0:T(128)S(1)} %fusion), kind=kLoop, calls=%fused_computation.1 | loop fusion | flops 8704 | bytes 34824 | tf_op jit(solution)/shard_map/sub | solution.py:313
  20.3 105.8 %shard_map.84 = bf16[17,2,2,512,128]{4,3,2,1,0:T(8,128)(2,1)} custom-call(bf16[2,2,512,128]{3,2,1,0:T(8,128)(2,1)S(1)} %pad_maximum_fusion.cur), custom_call_target="tpu_custom_call" | custom-call | tf_op jit(solution)/shard_map/pallas_call | solution.py:164
  126.1 87.2 %shard_map.85 = (bf16[2,16,128,128]{3,2,1,0:T(8,128)(2,1)S(1)}, bf16[2,16,128,128]{3,2,1,0:T(8,128)(2,1)S(1)}, f32[17,2,2,4,128,128]{5,4,3,2,1,0:T(8,128)}) custom-call(s32[2]{0:T(128)S(1)} %fusion.1.skip_ref, bf16[2,16,128,128]{3,2,1,0:T(8,128)(2,1)S(1)} %get-tuple-element.33.q_ref, bf16[2,16,128,128]{3,2,1,0:T(8,128)(2,1)S(1)} %get-tuple-element.32.do_ref, ...), custom_call_target="tpu_custom_call" | custom-call | tf_op jit(solution)/shard_map/pallas_call | solution.py:278
  213.4 1.6 copy.43
  215.0 1.6 copy.44
  216.7 103.7 %shard_map.86 = bf16[2,2,512,128]{3,2,1,0:T(8,128)(2,1)} custom-call(f32[17,2,2,512,128]{4,3,2,1,0:T(8,128)} %bitcast.43), custom_call_target="tpu_custom_call" | custom-call | tf_op jit(solution)/shard_map/pallas_call | solution.py:181
  320.4 1.5 copy.50
  321.8 1.0 slice_bitcast_fusion
  (6 shorter events, 0.0 us)
Async XLA Ops:
  0.6 2.6 copy-start

commit v7 on v6

--- a/solution.py
+++ b/solution.py
@@ -205,14 +205,15 @@
     scale = head_dim ** (-0.5)
     q = q_ref[0].reshape(rows, head_dim)
     grad_output = do_ref[0].reshape(rows, head_dim)
+    q_t = q.astype(jnp.float32).T.astype(jnp.bfloat16)
+    grad_t = grad_output.astype(jnp.float32).T
+    grad_t_low = grad_t.astype(jnp.bfloat16)
     query_doc = qdoc_ref[0]
     later = lax.broadcasted_iota(jnp.int32, (span_len, span_len), 0) > lax.broadcasted_iota(
         jnp.int32, (span_len, span_len), 1)
-    contract_last = (((1,), (1,)), ((), ()))
 
     def scores(j, causal):
-        sc = lax.dot_general(win_ref[j, 0, 0, 0], q, contract_last,
-                             preferred_element_type=jnp.float32) * scale
+        sc = jnp.dot(win_ref[j, 0, 0, 0], q_t, preferred_element_type=jnp.float32) * scale
         allowed = kdoc_ref[0, j] == query_doc
         if causal:
             allowed = jnp.logical_and(allowed, jnp.logical_not(later))
@@ -245,14 +246,12 @@
     acc = lax.fori_loop(first, last, out_step, acc)
     attended_t = acc.astype(jnp.bfloat16)
     o_ref[0] = attended_t.astype(jnp.float32).T.astype(jnp.bfloat16).reshape(group, span_len, head_dim)
-    grad_t = grad_output.astype(jnp.float32).T
     delta = jnp.sum(grad_t * attended_t.astype(jnp.float32), axis=0, keepdims=True)
 
     def grad_step(j, dq):
         prob = cache[j]
         low = prob.astype(jnp.bfloat16)
-        grad_w = lax.dot_general(win_ref[j, 0, 1, 0], grad_output, contract_last,
-                                 preferred_element_type=jnp.float32)
+        grad_w = jnp.dot(win_ref[j, 0, 1, 0], grad_t_low, preferred_element_type=jnp.float32)
         grad_s = (prob * (grad_w - delta) * scale).astype(jnp.bfloat16)
         terms_ref[j, 0, 0, 0] = jnp.dot(grad_s, q, preferred_element_type=jnp.float32)
         terms_ref[j, 0, 1, 0] = jnp.dot(low, grad_output, preferred_element_type=jnp.float32)

time: 323 us -> 317 us (0.981)
  Pallas kernels: 297 us -> 291 us
    pallas_call x1, Pallas kernels: 87.2 us -> 77 us  [attention(): pl.pallas_call(attention_kernel, out_shape=(jax.ShapeDtypeStruct(q.shape,...]
    pallas_call x1, Pallas kernels: 104 us -> 108 us  [backward_chain(): pl.pallas_call(functools.partial(backward_chain_kernel, count), out_shape...]
where the time goes in v7:
time: 317 us
  Pallas kernels  291 us (92%)
  local copies, waits for them, and re-layouts  14.7 us (5%)
  other arithmetic  6.8 us (2%)
  between operations  4.61 us (1%)
    pallas_call x1, Pallas kernels, backward_chain(): pl.pallas_call(functools.partial(backward_chain_kernel, count), out_shape...  108 us
    pallas_call x1, Pallas kernels, forward_chain(): pl.pallas_call(functools.partial(forward_chain_kernel, count), out_shape=...  106 us
    pallas_call x1, Pallas kernels, attention(): pl.pallas_call(attention_kernel, out_shape=(jax.ShapeDtypeStruct(q.shape,...  77 us

profile of v7, /device:TPU:126, one launch (start us, length us, event | category | flops | bytes accessed | tf_op | source)
XLA Modules:
  0.0 316.7 jit_solution(13794598292456346227)
XLA Ops:
  0.6 0.0 copy-start
  0.6 0.1 fusion.2
  0.7 1.0 copy.38
  1.7 1.0 copy.39
  2.7 0.1 pad_maximum_fusion.cur
  2.8 0.1 iota_add_fusion
  2.9 0.3 copy.35
  3.2 0.0 copy-done
  3.2 0.2 fusion
  3.4 0.6 fusion.3
  7.9 0.1 pad_dynamic-slice_fusion.1
  8.0 2.7 convert_reduce_fusion
  10.8 0.1 add_add_fusion.1
  10.9 0.2 slice_reduce_fusion
  11.1 0.1 slice_reduce_fusion.1
  11.2 0.2 fusion.1.skip_ref
  11.4 2.1 copy_bitcast_fusion
  13.5 3.5 %reduce_sum.36 = s32[2,17,128,1]{3,2,1,0:T(8,128)} reshape(s32[2,2176]{1,0:T(2,128)S(1)} %convert_reduce_fusion) | data formatting | bytes 34816 | tf_op jit(solution)/shard_map/reduce_sum | solution.py:311
  17.0 3.3 %add_add_fusion.kdoc_ref = s32[2,17,128,1]{3,2,1,0:T(8,128)} fusion(s32[2,17,128,1]{3,2,1,0:T(8,128)} %reduce_sum.36, s32[2]{0:T(128)S(1)} %fusion), kind=kLoop, calls=%fused_computation.1 | loop fusion | flops 8704 | bytes 34824 | tf_op jit(solution)/shard_map/sub | solution.py:312
  20.3 105.8 %shard_map.84 = bf16[17,2,2,512,128]{4,3,2,1,0:T(8,128)(2,1)} custom-call(bf16[2,2,512,128]{3,2,1,0:T(8,128)(2,1)S(1)} %pad_maximum_fusion.cur), custom_call_target="tpu_custom_call" | custom-call | tf_op jit(solution)/shard_map/pallas_call | solution.py:164
  126.1 77.0 %shard_map.85 = (bf16[2,16,128,128]{3,2,1,0:T(8,128)(2,1)S(1)}, bf16[2,16,128,128]{3,2,1,0:T(8,128)(2,1)S(1)}, f32[17,2,2,4,128,128]{5,4,3,2,1,0:T(8,128)}) custom-call(s32[2]{0:T(128)S(1)} %fusion.1.skip_ref, bf16[2,16,128,128]{3,2,1,0:T(8,128)(2,1)S(1)} %get-tuple-element.33.q_ref, bf16[2,16,128,128]{3,2,1,0:T(8,128)(2,1)S(1)} %get-tuple-element.32.do_ref, ...), custom_call_target="tpu_custom_call" | custom-call | tf_op jit(solution)/shard_map/pallas_call | solution.py:277
  203.2 1.6 copy.43
  204.8 1.6 copy.44
  206.5 107.8 %shard_map.86 = bf16[2,2,512,128]{3,2,1,0:T(8,128)(2,1)} custom-call(f32[17,2,2,512,128]{4,3,2,1,0:T(8,128)} %bitcast.43), custom_call_target="tpu_custom_call" | custom-call | tf_op jit(solution)/shard_map/pallas_call | solution.py:181
  314.3 1.5 copy.50
  315.7 1.0 slice_bitcast_fusion
  (6 shorter events, 0.0 us)
Async XLA Ops:
  0.6 2.6 copy-start

commit v8 on v7

--- a/solution.py
+++ b/solution.py
@@ -195,7 +195,7 @@
     )(terms)
 
 
-def attention_kernel(skip_ref, q_ref, do_ref, win_ref, qdoc_ref, kdoc_ref,
+def attention_kernel(skip_ref, first_ref, q_ref, do_ref, win_ref, qstart_ref,
                      o_ref, dq_ref, terms_ref, cache):
     stream = pl.program_id(0)
     first = skip_ref[stream]
@@ -208,15 +208,15 @@
     q_t = q.astype(jnp.float32).T.astype(jnp.bfloat16)
     grad_t = grad_output.astype(jnp.float32).T
     grad_t_low = grad_t.astype(jnp.bfloat16)
-    query_doc = qdoc_ref[0]
-    later = lax.broadcasted_iota(jnp.int32, (span_len, span_len), 0) > lax.broadcasted_iota(
-        jnp.int32, (span_len, span_len), 1)
+    query_start = qstart_ref[0]
+    span = first_ref[stream]
+    query_pos = lax.broadcasted_iota(jnp.int32, (1, span_len), 1) + span * span_len
+    key_offset = lax.broadcasted_iota(jnp.int32, (span_len, span_len), 0)
 
     def scores(j, causal):
         sc = jnp.dot(win_ref[j, 0, 0, 0], q_t, preferred_element_type=jnp.float32) * scale
-        allowed = kdoc_ref[0, j] == query_doc
-        if causal:
-            allowed = jnp.logical_and(allowed, jnp.logical_not(later))
+        key_pos = key_offset + (span - last + j) * span_len
+        allowed = jnp.logical_and(key_pos >= query_start, key_pos <= query_pos)
         allowed = jnp.tile(allowed, (1, group))
         sc = jnp.where(allowed, sc, -jnp.inf)
         cache[j] = sc
@@ -269,11 +269,11 @@
     lax.fori_loop(0, first, clear, 0)
 
 
-def attention(skip, q, grad_out, window, query_doc, key_doc, group):
+def attention(skip, span_firsts, q, grad_out, window, query_start, group):
     streams, heads, span_len, head_dim = q.shape
     kv_heads = heads // group
     spans = window.shape[0]
-    head_block = pl.BlockSpec((1, group, span_len, head_dim), lambda s, h, sk: (s, h, 0, 0))
+    head_block = pl.BlockSpec((1, group, span_len, head_dim), lambda s, h, sk, sf: (s, h, 0, 0))
     return pl.pallas_call(
         attention_kernel,
         out_shape=(
@@ -282,34 +282,23 @@
             jax.ShapeDtypeStruct((spans, streams, 2, kv_heads, span_len, head_dim), jnp.float32),
         ),
         grid_spec=pltpu.PrefetchScalarGridSpec(
-            num_scalar_prefetch=1,
+            num_scalar_prefetch=2,
             grid=(streams, kv_heads),
             in_specs=[
                 head_block,
                 head_block,
-                pl.BlockSpec((spans, 1, 2, 1, span_len, head_dim), lambda s, h, sk: (0, s, 0, h, 0, 0)),
-                pl.BlockSpec((1, 1, span_len), lambda s, h, sk: (s, 0, 0)),
-                pl.BlockSpec((1, spans, span_len, 1), lambda s, h, sk: (s, 0, 0, 0)),
+                pl.BlockSpec((spans, 1, 2, 1, span_len, head_dim), lambda s, h, sk, sf: (0, s, 0, h, 0, 0)),
+                pl.BlockSpec((1, 1, span_len), lambda s, h, sk, sf: (s, 0, 0)),
             ],
             out_specs=[
                 head_block,
                 head_block,
-                pl.BlockSpec((spans, 1, 2, 1, span_len, head_dim), lambda s, h, sk: (0, s, 0, h, 0, 0)),
+                pl.BlockSpec((spans, 1, 2, 1, span_len, head_dim), lambda s, h, sk, sf: (0, s, 0, h, 0, 0)),
             ],
             scratch_shapes=[pltpu.VMEM((spans, span_len, group * span_len), jnp.float32)],
         ),
         compiler_params=pltpu.CompilerParams(vmem_limit_bytes=48 * 1024 * 1024),
-    )(skip, q, grad_out, window, query_doc, key_doc)
-
-
-def window_docs(doc_starts, key_pos):
-    width = key_pos.shape[1]
-    before = jnp.sum((doc_starts[None, :] < key_pos[:, :1]).astype(jnp.int32), axis=1)
-    padded = jnp.concatenate(
-        [doc_starts, jnp.full((width // 2,), jnp.iinfo(jnp.int32).max, doc_starts.dtype)])
-    local = jnp.stack([lax.dynamic_slice_in_dim(padded, before[i], width // 2) for i in range(2)])
-    inside = jnp.sum((local[:, None, :] <= key_pos[:, :, None]).astype(jnp.int32), axis=2)
-    return before[:, None] + inside - 1
+    )(skip, span_firsts, q, grad_out, window, query_start)
 
 
 def body(query, keys, values, grad_out, doc_starts):
@@ -326,15 +315,14 @@
                          jnp.transpose(values[:, 0], (0, 2, 1, 3))], axis=1)
     flat = current.reshape(2, 2, kv_heads * span_len, head_dim)
     spans = forward_chain(flat, shard_count).reshape((window + 1,) + current.shape)
-    span_firsts = jnp.stack([device_index, 2 * shard_count - 1 - device_index])
-    key_pos = (span_firsts[:, None] - window) * span_len + jnp.arange(
-        (window + 1) * span_len, dtype=jnp.int32)[None]
-    key_doc = window_docs(doc_starts, key_pos)
-    key_doc = key_doc.reshape(2, window + 1, span_len)
-    query_doc = key_doc[:, window]
-    skip = jnp.sum(key_doc[:, :window, span_len - 1] < query_doc[:, :1], axis=1).astype(jnp.int32)
+    span_firsts = jnp.stack([device_index, 2 * shard_count - 1 - device_index]).astype(jnp.int32)
+    query_pos = span_firsts[:, None] * span_len + jnp.arange(span_len, dtype=jnp.int32)[None]
+    query_start = jnp.max(
+        jnp.where(doc_starts[None, None, :] <= query_pos[:, :, None], doc_starts[None, None, :], -1), axis=2)
+    span_last = (span_firsts[:, None] - window + jnp.arange(window, dtype=jnp.int32)[None]) * span_len + span_len - 1
+    skip = jnp.sum(span_last < query_start[:, :1], axis=1).astype(jnp.int32)
     attended, grad_q, terms = attention(
-        skip, q, grad_o, spans, query_doc[:, None, :], key_doc[:, :, :, None], group)
+        skip, span_firsts, q, grad_o, spans, query_start[:, None, :], group)
     term_flat = terms.reshape(window + 1, 2, 2, kv_heads * span_len, head_dim)
     totals = backward_chain(term_flat, shard_count).reshape(current.shape)
     grad_kv = jnp.transpose(totals, (1, 0, 3, 2, 4))[:, :, None]

time: 317 us -> 332 us (1.047)
  Pallas kernels: 291 us -> 319 us
  other arithmetic: 6.8 us -> 1.8 us
  local copies, waits for them, and re-layouts: 14.7 us -> 9.9 us
  between operations: 4.61 us -> 0.68 us
    pallas_call x1, Pallas kernels: 77 us -> 111 us  [attention(): pl.pallas_call(attention_kernel, out_shape=(jax.ShapeDtypeStruct(q.shape,...]
    pallas_call x1, Pallas kernels: 108 us -> 101 us  [backward_chain(): pl.pallas_call(functools.partial(backward_chain_kernel, count), out_shape...]
    reduce_sum x2 -> x0, local copies, waits for them, and re-layouts: 3.53 us -> none  [window_docs(): jnp.sum((local[:, None, :] <= key_pos[:, :, None]).astype(jnp.int32), axi...]
    sub x2 -> x1, other arithmetic: 3.41 us -> 0.08 us  [body(): span_firsts[:, None] - window + jnp.arange(window, dtype=jnp.int32)[None]]
where the time goes in v8:
time: 332 us; the launch traced here: 331 us
  Pallas kernels  319 us (96%)
  local copies, waits for them, and re-layouts  9.9 us (3%)
    pallas_call x1, Pallas kernels, attention(): pl.pallas_call(attention_kernel, out_shape=(jax.ShapeDtypeStruct(q.shape,...  111 us
    pallas_call x1, Pallas kernels, forward_chain(): pl.pallas_call(functools.partial(forward_chain_kernel, count), out_shape=...  106 us
    pallas_call x1, Pallas kernels, backward_chain(): pl.pallas_call(functools.partial(backward_chain_kernel, count), out_shape...  101 us

profile of v8, /device:TPU:126, one launch (start us, length us, event | category | flops | bytes accessed | tf_op | source)
XLA Modules:
  0.0 331.3 jit_solution(14247753362756464438)
XLA Ops:
  0.6 0.1 broadcast_add_fusion
  0.7 0.1 iota_add_fusion
  0.8 1.4 select_reduce_fusion
  2.2 0.1 slice_reduce_fusion
  2.3 0.2 fusion.skip_ref
  2.5 1.0 copy.25
  3.5 1.0 copy.26
  4.5 0.1 pad_maximum_fusion.cur
  4.5 2.1 copy_bitcast_fusion
  6.6 106.0 %shard_map.84 = bf16[17,2,2,512,128]{4,3,2,1,0:T(8,128)(2,1)} custom-call(bf16[2,2,512,128]{3,2,1,0:T(8,128)(2,1)S(1)} %pad_maximum_fusion.cur), custom_call_target="tpu_custom_call" | custom-call | tf_op jit(solution)/shard_map/pallas_call | solution.py:164
  112.6 111.4 %shard_map.85 = (bf16[2,16,128,128]{3,2,1,0:T(8,128)(2,1)S(1)}, bf16[2,16,128,128]{3,2,1,0:T(8,128)(2,1)S(1)}, f32[17,2,2,4,128,128]{5,4,3,2,1,0:T(8,128)}) custom-call(s32[2]{0:T(128)S(1)} %fusion.skip_ref, s32[2]{0:T(128)S(1)} %get-tuple-element.23.first_ref, bf16[2,16,128,128]{3,2,1,0:T(8,128)(2,1)S(1)} %get-tuple-element.27.q_ref, ...), custom_call_target="tpu_custom_call" | custom-call | tf_op jit(solution)/shard_map/pallas_call | solution.py:277
  224.1 1.6 copy.28
  225.7 1.6 copy.29
  227.4 101.5 %shard_map.86 = bf16[2,2,512,128]{3,2,1,0:T(8,128)(2,1)} custom-call(f32[17,2,2,512,128]{4,3,2,1,0:T(8,128)} %bitcast.39), custom_call_target="tpu_custom_call" | custom-call | tf_op jit(solution)/shard_map/pallas_call | solution.py:181
  328.8 1.5 copy.33
  330.3 1.0 slice_bitcast_fusion
  (1 shorter events, 0.0 us)

commit v9 on v8

--- a/solution.py
+++ b/solution.py
@@ -196,7 +196,7 @@
 
 
 def attention_kernel(skip_ref, first_ref, q_ref, do_ref, win_ref, qstart_ref,
-                     o_ref, dq_ref, terms_ref, cache):
+                     o_ref, dq_ref, terms_ref, cache, tops):
     stream = pl.program_id(0)
     first = skip_ref[stream]
     group, span_len, head_dim = q_ref.shape[1:]
@@ -218,26 +218,30 @@
         key_pos = key_offset + (span - last + j) * span_len
         allowed = jnp.logical_and(key_pos >= query_start, key_pos <= query_pos)
         allowed = jnp.tile(allowed, (1, group))
-        sc = jnp.where(allowed, sc, -jnp.inf)
-        cache[j] = sc
-        return sc
+        return jnp.where(allowed, sc, -jnp.inf)
 
     sc = scores(last, True)
     top = jnp.max(sc, axis=0, keepdims=True)
-    total = jnp.sum(jnp.exp(sc - top), axis=0, keepdims=True)
+    expon = jnp.exp(sc - top)
+    cache[last] = expon
+    tops[last] = top
+    total = jnp.sum(expon, axis=0, keepdims=True)
 
     def stat_step(j, carry):
         top, total = carry
         sc = scores(j, False)
         new_top = jnp.maximum(top, jnp.max(sc, axis=0, keepdims=True))
-        total = total * jnp.exp(top - new_top) + jnp.sum(jnp.exp(sc - new_top), axis=0, keepdims=True)
+        expon = jnp.exp(sc - new_top)
+        cache[j] = expon
+        tops[j] = new_top
+        total = total * jnp.exp(top - new_top) + jnp.sum(expon, axis=0, keepdims=True)
         return new_top, total
 
     top, total = lax.fori_loop(first, last, stat_step, (top, total))
     inverse = 1.0 / total
 
     def out_step(j, acc):
-        prob = jnp.exp(cache[j] - top) * inverse
+        prob = cache[j] * (jnp.exp(tops[j] - top) * inverse)
         cache[j] = prob
         value_t = win_ref[j, 0, 1, 0].astype(jnp.float32).T.astype(jnp.bfloat16)
         return acc + jnp.dot(value_t, prob.astype(jnp.bfloat16), preferred_element_type=jnp.float32)
@@ -295,7 +299,8 @@
                 head_block,
                 pl.BlockSpec((spans, 1, 2, 1, span_len, head_dim), lambda s, h, sk, sf: (0, s, 0, h, 0, 0)),
             ],
-            scratch_shapes=[pltpu.VMEM((spans, span_len, group * span_len), jnp.float32)],
+            scratch_shapes=[pltpu.VMEM((spans, span_len, group * span_len), jnp.float32),
+                            pltpu.VMEM((spans, 1, group * span_len), jnp.float32)],
         ),
         compiler_params=pltpu.CompilerParams(vmem_limit_bytes=48 * 1024 * 1024),
     )(skip, span_firsts, q, grad_out, window, query_start)

time: 332 us -> 327 us (0.985)
  the two profiles are of different devices: /device:TPU:126 before, /device:TPU:129 now
where the time goes in v9:
time: 327 us
  Pallas kernels  314 us (96%)
  local copies, waits for them, and re-layouts  9.9 us (3%)
    pallas_call x1, Pallas kernels, attention(): pl.pallas_call(attention_kernel, out_shape=(jax.ShapeDtypeStruct(q.shape,...  120 us
    pallas_call x1, Pallas kernels, forward_chain(): pl.pallas_call(functools.partial(forward_chain_kernel, count), out_shape=...  105 us
    pallas_call x1, Pallas kernels, backward_chain(): pl.pallas_call(functools.partial(backward_chain_kernel, count), out_shape...  89.6 us

profile of v9, /device:TPU:129, one launch (start us, length us, event | category | flops | bytes accessed | tf_op | source)
XLA Modules:
  0.0 326.5 jit_solution(5687423834025102770)
XLA Ops:
  0.6 0.1 broadcast_add_fusion
  0.7 0.1 iota_add_fusion
  0.8 1.4 select_reduce_fusion
  2.2 0.1 slice_reduce_fusion
  2.3 0.2 fusion.skip_ref
  2.5 1.0 copy.25
  3.5 1.0 copy.26
  4.5 0.1 pad_maximum_fusion.cur
  4.5 2.1 copy_bitcast_fusion
  6.6 104.6 %shard_map.84 = bf16[17,2,2,512,128]{4,3,2,1,0:T(8,128)(2,1)} custom-call(bf16[2,2,512,128]{3,2,1,0:T(8,128)(2,1)S(1)} %pad_maximum_fusion.cur), custom_call_target="tpu_custom_call" | custom-call | tf_op jit(solution)/shard_map/pallas_call | solution.py:164
  111.3 119.9 %shard_map.85 = (bf16[2,16,128,128]{3,2,1,0:T(8,128)(2,1)S(1)}, bf16[2,16,128,128]{3,2,1,0:T(8,128)(2,1)S(1)}, f32[17,2,2,4,128,128]{5,4,3,2,1,0:T(8,128)}) custom-call(s32[2]{0:T(128)S(1)} %fusion.skip_ref, s32[2]{0:T(128)S(1)} %get-tuple-element.23.first_ref, bf16[2,16,128,128]{3,2,1,0:T(8,128)(2,1)S(1)} %get-tuple-element.27.q_ref, ...), custom_call_target="tpu_custom_call" | custom-call | tf_op jit(solution)/shard_map/pallas_call | solution.py:281
  231.2 1.6 copy.28
  232.8 1.6 copy.29
  234.5 89.6 %shard_map.86 = bf16[2,2,512,128]{3,2,1,0:T(8,128)(2,1)} custom-call(f32[17,2,2,512,128]{4,3,2,1,0:T(8,128)} %bitcast.39), custom_call_target="tpu_custom_call" | custom-call | tf_op jit(solution)/shard_map/pallas_call | solution.py:181
  324.1 1.5 copy.33
  325.6 1.0 slice_bitcast_fusion
  (1 shorter events, 0.0 us)

commit v10 on v8

--- a/solution.py
+++ b/solution.py
@@ -196,84 +196,120 @@
 
 
 def attention_kernel(skip_ref, first_ref, q_ref, do_ref, win_ref, qstart_ref,
-                     o_ref, dq_ref, terms_ref, cache):
+                     o_ref, dq_ref, terms_ref, cache, tops):
     stream = pl.program_id(0)
     first = skip_ref[stream]
-    group, span_len, head_dim = q_ref.shape[1:]
+    pair = win_ref.shape[3]
+    group = q_ref.shape[1] // pair
+    span_len, head_dim = q_ref.shape[2:]
     rows = group * span_len
     last = win_ref.shape[0] - 1
     scale = head_dim ** (-0.5)
-    q = q_ref[0].reshape(rows, head_dim)
-    grad_output = do_ref[0].reshape(rows, head_dim)
-    q_t = q.astype(jnp.float32).T.astype(jnp.bfloat16)
-    grad_t = grad_output.astype(jnp.float32).T
-    grad_t_low = grad_t.astype(jnp.bfloat16)
+    heads = range(pair)
+    qs = [q_ref[0, h * group:(h + 1) * group].reshape(rows, head_dim) for h in heads]
+    grads = [do_ref[0, h * group:(h + 1) * group].reshape(rows, head_dim) for h in heads]
+    q_ts = [q.astype(jnp.float32).T.astype(jnp.bfloat16) for q in qs]
+    grad_ts = [g.astype(jnp.float32).T for g in grads]
+    grad_t_lows = [g.astype(jnp.bfloat16) for g in grad_ts]
     query_start = qstart_ref[0]
     span = first_ref[stream]
     query_pos = lax.broadcasted_iota(jnp.int32, (1, span_len), 1) + span * span_len
     key_offset = lax.broadcasted_iota(jnp.int32, (span_len, span_len), 0)
 
-    def scores(j, causal):
-        sc = jnp.dot(win_ref[j, 0, 0, 0], q_t, preferred_element_type=jnp.float32) * scale
+    def mask(j):
         key_pos = key_offset + (span - last + j) * span_len
         allowed = jnp.logical_and(key_pos >= query_start, key_pos <= query_pos)
-        allowed = jnp.tile(allowed, (1, group))
-        sc = jnp.where(allowed, sc, -jnp.inf)
-        cache[j] = sc
-        return sc
-
-    sc = scores(last, True)
-    top = jnp.max(sc, axis=0, keepdims=True)
-    total = jnp.sum(jnp.exp(sc - top), axis=0, keepdims=True)
+        return jnp.tile(allowed, (1, group))
+
+    def scores(j, h, allowed):
+        sc = jnp.dot(win_ref[j, 0, 0, h], q_ts[h], preferred_element_type=jnp.float32) * scale
+        return jnp.where(allowed, sc, -jnp.inf)
+
+    allowed = mask(last)
+    top_list, total_list = [], []
+    for h in heads:
+        sc = scores(last, h, allowed)
+        top = jnp.max(sc, axis=0, keepdims=True)
+        expon = jnp.exp(sc - top)
+        cache[last, h] = expon
+        tops[last, h] = top
+        top_list.append(top)
+        total_list.append(jnp.sum(expon, axis=0, keepdims=True))
 
     def stat_step(j, carry):
-        top, total = carry
-        sc = scores(j, False)
-        new_top = jnp.maximum(top, jnp.max(sc, axis=0, keepdims=True))
-        total = total * jnp.exp(top - new_top) + jnp.sum(jnp.exp(sc - new_top), axis=0, keepdims=True)
-        return new_top, total
-
-    top, total = lax.fori_loop(first, last, stat_step, (top, total))
-    inverse = 1.0 / total
-
-    def out_step(j, acc):
-        prob = jnp.exp(cache[j] - top) * inverse
-        cache[j] = prob
-        value_t = win_ref[j, 0, 1, 0].astype(jnp.float32).T.astype(jnp.bfloat16)
-        return acc + jnp.dot(value_t, prob.astype(jnp.bfloat16), preferred_element_type=jnp.float32)
-
-    acc = out_step(last, jnp.zeros((head_dim, rows), jnp.float32))
-    acc = lax.fori_loop(first, last, out_step, acc)
-    attended_t = acc.astype(jnp.bfloat16)
-    o_ref[0] = attended_t.astype(jnp.float32).T.astype(jnp.bfloat16).reshape(group, span_len, head_dim)
-    delta = jnp.sum(grad_t * attended_t.astype(jnp.float32), axis=0, keepdims=True)
-
-    def grad_step(j, dq):
-        prob = cache[j]
-        low = prob.astype(jnp.bfloat16)
-        grad_w = jnp.dot(win_ref[j, 0, 1, 0], grad_t_low, preferred_element_type=jnp.float32)
-        grad_s = (prob * (grad_w - delta) * scale).astype(jnp.bfloat16)
-        terms_ref[j, 0, 0, 0] = jnp.dot(grad_s, q, preferred_element_type=jnp.float32)
-        terms_ref[j, 0, 1, 0] = jnp.dot(low, grad_output, preferred_element_type=jnp.float32)
-        key_t = win_ref[j, 0, 0, 0].astype(jnp.float32).T.astype(jnp.bfloat16)
-        return dq + jnp.dot(key_t, grad_s, preferred_element_type=jnp.float32)
-
-    dq = grad_step(last, jnp.zeros((head_dim, rows), jnp.float32))
-    dq = lax.fori_loop(first, last, grad_step, dq)
-    dq_ref[0] = dq.T.astype(jnp.bfloat16).reshape(group, span_len, head_dim)
+        top_c, total_c = carry
+        allowed = mask(j)
+        new_tops, new_totals = [], []
+        for h in heads:
+            sc = scores(j, h, allowed)
+            new_top = jnp.maximum(top_c[h], jnp.max(sc, axis=0, keepdims=True))
+            expon = jnp.exp(sc - new_top)
+            cache[j, h] = expon
+            tops[j, h] = new_top
+            new_tops.append(new_top)
+            new_totals.append(total_c[h] * jnp.exp(top_c[h] - new_top)
+                              + jnp.sum(expon, axis=0, keepdims=True))
+        return tuple(new_tops), tuple(new_totals)
+
+    top_list, total_list = lax.fori_loop(first, last, stat_step, (tuple(top_list), tuple(total_list)))
+    inverses = [1.0 / t for t in total_list]
+
+    def out_step(j, accs):
+        new = []
+        for h in heads:
+            prob = cache[j, h] * (jnp.exp(tops[j, h] - top_list[h]) * inverses[h])
+            cache[j, h] = prob
+            value_t = win_ref[j, 0, 1, h].astype(jnp.float32).T.astype(jnp.bfloat16)
+            new.append(accs[h] + jnp.dot(value_t, prob.astype(jnp.bfloat16),
+                                         preferred_element_type=jnp.float32))
+        return tuple(new)
+
+    zero = jnp.zeros((head_dim, rows), jnp.float32)
+    accs = out_step(last, tuple(zero for _ in heads))
+    accs = lax.fori_loop(first, last, out_step, accs)
+    deltas = []
+    for h in heads:
+        attended_t = accs[h].astype(jnp.bfloat16)
+        o_ref[0, h * group:(h + 1) * group] = attended_t.astype(jnp.float32).T.astype(
+            jnp.bfloat16).reshape(group, span_len, head_dim)
+        deltas.append(jnp.sum(grad_ts[h] * attended_t.astype(jnp.float32), axis=0, keepdims=True))
+
+    def grad_step(j, dqs):
+        new = []
+        for h in heads:
+            prob = cache[j, h]
+            low = prob.astype(jnp.bfloat16)
+            grad_w = jnp.dot(win_ref[j, 0, 1, h], grad_t_lows[h], preferred_element_type=jnp.float32)
+            grad_s = (prob * (grad_w - deltas[h]) * scale).astype(jnp.bfloat16)
+            terms_ref[j, 0, 0, h] = jnp.dot(grad_s, qs[h], preferred_element_type=jnp.float32)
+            terms_ref[j, 0, 1, h] = jnp.dot(low, grads[h], preferred_element_type=jnp.float32)
+            key_t = win_ref[j, 0, 0, h].astype(jnp.float32).T.astype(jnp.bfloat16)
+            new.append(dqs[h] + jnp.dot(key_t, grad_s, preferred_element_type=jnp.float32))
+        return tuple(new)
+
+    dqs = grad_step(last, tuple(zero for _ in heads))
+    dqs = lax.fori_loop(first, last, grad_step, dqs)
+    for h in heads:
+        dq_ref[0, h * group:(h + 1) * group] = dqs[h].T.astype(jnp.bfloat16).reshape(
+            group, span_len, head_dim)
 
     def clear(j, carry):
         terms_ref[j] = jnp.zeros(terms_ref.shape[1:], terms_ref.dtype)
         return carry
 
     lax.fori_loop(0, first, clear, 0)
+
+
+HEAD_PAIR = 2
 
 
 def attention(skip, span_firsts, q, grad_out, window, query_start, group):
     streams, heads, span_len, head_dim = q.shape
     kv_heads = heads // group
     spans = window.shape[0]
-    head_block = pl.BlockSpec((1, group, span_len, head_dim), lambda s, h, sk, sf: (s, h, 0, 0))
+    head_block = pl.BlockSpec((1, group * HEAD_PAIR, span_len, head_dim), lambda s, h, sk, sf: (s, h, 0, 0))
+    window_block = pl.BlockSpec((spans, 1, 2, HEAD_PAIR, span_len, head_dim),
+                                lambda s, h, sk, sf: (0, s, 0, h, 0, 0))
     return pl.pallas_call(
         attention_kernel,
         out_shape=(
@@ -283,21 +319,18 @@
         ),
         grid_spec=pltpu.PrefetchScalarGridSpec(
             num_scalar_prefetch=2,
-            grid=(streams, kv_heads),
+            grid=(streams, kv_heads // HEAD_PAIR),
             in_specs=[
                 head_block,
                 head_block,
-                pl.BlockSpec((spans, 1, 2, 1, span_len, head_dim), lambda s, h, sk, sf: (0, s, 0, h, 0, 0)),
+                window_block,
                 pl.BlockSpec((1, 1, span_len), lambda s, h, sk, sf: (s, 0, 0)),
             ],
-            out_specs=[
-                head_block,
-                head_block,
-                pl.BlockSpec((spans, 1, 2, 1, span_len, head_dim), lambda s, h, sk, sf: (0, s, 0, h, 0, 0)),
-            ],
-            scratch_shapes=[pltpu.VMEM((spans, span_len, group * span_len), jnp.float32)],
+            out_specs=[head_block, head_block, window_block],
+            scratch_shapes=[pltpu.VMEM((spans, HEAD_PAIR, span_len, group * span_len), jnp.float32),
+                            pltpu.VMEM((spans, HEAD_PAIR, 1, group * span_len), jnp.float32)],
         ),
-        compiler_params=pltpu.CompilerParams(vmem_limit_bytes=48 * 1024 * 1024),
+        compiler_params=pltpu.CompilerParams(vmem_limit_bytes=56 * 1024 * 1024),
     )(skip, span_firsts, q, grad_out, window, query_start)
 
 

time: 332 us -> 303 us (0.913)
  the two profiles are of different devices: /device:TPU:126 before, /device:TPU:118 now
where the time goes in v10:
time: 303 us
  Pallas kernels  286 us (94%)
  local copies, waits for them, and re-layouts  13.7 us (5%)
    pallas_call x1, Pallas kernels, backward_chain(): pl.pallas_call(functools.partial(backward_chain_kernel, count), out_shape...  107 us
    pallas_call x1, Pallas kernels, forward_chain(): pl.pallas_call(functools.partial(forward_chain_kernel, count), out_shape=...  106 us
    pallas_call x1, Pallas kernels, attention(): pl.pallas_call(attention_kernel, out_shape=(jax.ShapeDtypeStruct(q.shape,...  73 us

profile of v10, /device:TPU:118, one launch (start us, length us, event | category | flops | bytes accessed | tf_op | source)
XLA Modules:
  0.0 302.8 jit_solution(5055054785311057072)
XLA Ops:
  0.6 0.1 broadcast_add_fusion
  0.7 0.0 copy-start.1
  0.7 0.1 iota_add_fusion
  0.8 1.4 select_reduce_fusion
  2.2 0.0 copy-start
  2.2 0.1 slice_reduce_fusion
  2.3 0.7 fusion.skip_ref
  3.0 1.0 copy.25
  4.0 1.0 copy.26
  5.0 0.1 pad_maximum_fusion.cur
  5.1 3.4 %copy_bitcast_fusion = (bf16[2,16,128,128]{3,2,1,0:T(8,128)(2,1)}, bf16[2,16,128,128]{3,2,1,0:T(8,128)(2,1)}) fusion(bf16[2,1,128,16,128]{4,3,2,1,0:T(8,128)(2,1)} %param.8, bf16[2,1,128,16,128]{4,3,2,1,0:T(8,128)(2,1)} %param.5), kind=kLoop, calls=%fused_computation.1 | loop fusion | bytes 4194304 | tf_op jit(solution)/shard_map/transpose | solution.py:346
  8.5 105.8 %shard_map.84 = bf16[17,2,2,512,128]{4,3,2,1,0:T(8,128)(2,1)} custom-call(bf16[2,2,512,128]{3,2,1,0:T(8,128)(2,1)S(1)} %pad_maximum_fusion.cur), custom_call_target="tpu_custom_call" | custom-call | tf_op jit(solution)/shard_map/pallas_call | solution.py:164
  114.3 0.0 copy-done.1
  114.3 0.0 copy-done
  114.3 73.0 %shard_map.85 = (bf16[2,16,128,128]{3,2,1,0:T(8,128)(2,1)}, bf16[2,16,128,128]{3,2,1,0:T(8,128)(2,1)}, f32[17,2,2,4,128,128]{5,4,3,2,1,0:T(8,128)}) custom-call(s32[2]{0:T(128)} %fusion.skip_ref, s32[2]{0:T(128)} %copy-done.1, bf16[2,16,128,128]{3,2,1,0:T(8,128)(2,1)} %get-tuple-element.27.q_ref, bf16[2,16,128,128]{3,2,1,0:T(8,128)(2,1)} %get-tuple-element.26.do_ref, ...), custom_call_target="tpu_custom_call" | custom-call | tf_op jit(solution)/shard_map/pallas_call | solution.py:313
  187.3 2.9 copy.28
  190.2 2.9 copy.29
  193.1 107.3 %shard_map.86 = bf16[2,2,512,128]{3,2,1,0:T(8,128)(2,1)} custom-call(f32[17,2,2,512,128]{4,3,2,1,0:T(8,128)} %bitcast.36), custom_call_target="tpu_custom_call" | custom-call | tf_op jit(solution)/shard_map/pallas_call | solution.py:181
  300.4 1.5 copy.33
  301.8 1.0 slice_bitcast_fusion
  (1 shorter events, 0.0 us)
Async XLA Ops:
  0.7 113.6 %copy-start.1 = (s32[2]{0:T(128)}, s32[2]{0:T(128)S(1)}, u32[]{:S(2)}) copy-start(s32[2]{0:T(128)S(1)} %get-tuple-element.23.first_ref) | copy-start | bytes 28
  2.2 112.1 %copy-start = (s32[2,128]{1,0:T(2,128)}, s32[2,128]{1,0:T(2,128)S(1)}, u32[]{:S(2)}) copy-start(s32[2,128]{1,0:T(2,128)S(1)} %select_reduce_fusion) | copy-start | bytes 3076

commit v11 on v10

--- a/solution.py
+++ b/solution.py
@@ -300,7 +300,7 @@
     lax.fori_loop(0, first, clear, 0)
 
 
-HEAD_PAIR = 2
+HEAD_PAIR = 4
 
 
 def attention(skip, span_firsts, q, grad_out, window, query_start, group):
@@ -330,7 +330,7 @@
             scratch_shapes=[pltpu.VMEM((spans, HEAD_PAIR, span_len, group * span_len), jnp.float32),
                             pltpu.VMEM((spans, HEAD_PAIR, 1, group * span_len), jnp.float32)],
         ),
-        compiler_params=pltpu.CompilerParams(vmem_limit_bytes=56 * 1024 * 1024),
+        compiler_params=pltpu.CompilerParams(vmem_limit_bytes=63 * 1024 * 1024),
     )(skip, span_firsts, q, grad_out, window, query_start)
 
 

time: 303 us -> 309 us (1.020)
  the two profiles are of different devices: /device:TPU:118 before, /device:TPU:126 now
where the time goes in v11:
time: 309 us; the launch traced here: 307 us
  Pallas kernels  290 us (94%)
  local copies, waits for them, and re-layouts  13.7 us (4%)
    pallas_call x1, Pallas kernels, backward_chain(): pl.pallas_call(functools.partial(backward_chain_kernel, count), out_shape...  108 us
    pallas_call x1, Pallas kernels, forward_chain(): pl.pallas_call(functools.partial(forward_chain_kernel, count), out_shape=...  106 us
    pallas_call x1, Pallas kernels, attention(): pl.pallas_call(attention_kernel, out_shape=(jax.ShapeDtypeStruct(q.shape,...  75.9 us

profile of v11, /device:TPU:126, one launch (start us, length us, event | category | flops | bytes accessed | tf_op | source)
XLA Modules:
  0.0 306.6 jit_solution(5451210657013941059)
XLA Ops:
  0.6 0.1 broadcast_add_fusion
  0.7 0.0 copy-start.1
  0.7 0.1 iota_add_fusion
  0.8 1.4 select_reduce_fusion
  2.2 0.0 copy-start
  2.2 0.1 slice_reduce_fusion
  2.3 0.7 fusion.skip_ref
  3.0 1.0 copy.25
  4.0 1.0 copy.26
  5.0 0.1 pad_maximum_fusion.cur
  5.1 3.4 %copy_bitcast_fusion = (bf16[2,16,128,128]{3,2,1,0:T(8,128)(2,1)}, bf16[2,16,128,128]{3,2,1,0:T(8,128)(2,1)}) fusion(bf16[2,1,128,16,128]{4,3,2,1,0:T(8,128)(2,1)} %param.8, bf16[2,1,128,16,128]{4,3,2,1,0:T(8,128)(2,1)} %param.5), kind=kLoop, calls=%fused_computation.1 | loop fusion | bytes 4194304 | tf_op jit(solution)/shard_map/transpose | solution.py:346
  8.5 105.8 %shard_map.84 = bf16[17,2,2,512,128]{4,3,2,1,0:T(8,128)(2,1)} custom-call(bf16[2,2,512,128]{3,2,1,0:T(8,128)(2,1)S(1)} %pad_maximum_fusion.cur), custom_call_target="tpu_custom_call" | custom-call | tf_op jit(solution)/shard_map/pallas_call | solution.py:164
  114.3 0.0 copy-done.1
  114.3 0.0 copy-done
  114.3 75.9 %shard_map.85 = (bf16[2,16,128,128]{3,2,1,0:T(8,128)(2,1)}, bf16[2,16,128,128]{3,2,1,0:T(8,128)(2,1)}, f32[17,2,2,4,128,128]{5,4,3,2,1,0:T(8,128)}) custom-call(s32[2]{0:T(128)} %fusion.skip_ref, s32[2]{0:T(128)} %copy-done.1, bf16[2,16,128,128]{3,2,1,0:T(8,128)(2,1)} %get-tuple-element.27.q_ref, bf16[2,16,128,128]{3,2,1,0:T(8,128)(2,1)} %get-tuple-element.26.do_ref, ...), custom_call_target="tpu_custom_call" | custom-call | tf_op jit(solution)/shard_map/pallas_call | solution.py:313
  190.2 2.9 copy.28
  193.1 2.9 copy.29
  196.0 108.2 %shard_map.86 = bf16[2,2,512,128]{3,2,1,0:T(8,128)(2,1)} custom-call(f32[17,2,2,512,128]{4,3,2,1,0:T(8,128)} %bitcast.36), custom_call_target="tpu_custom_call" | custom-call | tf_op jit(solution)/shard_map/pallas_call | solution.py:181
  304.2 1.5 copy.33
  305.6 1.0 slice_bitcast_fusion
  (1 shorter events, 0.0 us)
Async XLA Ops:
  0.7 113.6 %copy-start.1 = (s32[2]{0:T(128)}, s32[2]{0:T(128)S(1)}, u32[]{:S(2)}) copy-start(s32[2]{0:T(128)S(1)} %get-tuple-element.23.first_ref) | copy-start | bytes 28
  2.2 112.1 %copy-start = (s32[2,128]{1,0:T(2,128)}, s32[2,128]{1,0:T(2,128)S(1)}, u32[]{:S(2)}) copy-start(s32[2,128]{1,0:T(2,128)S(1)} %select_reduce_fusion) | copy-start | bytes 3076

commit v12 on v11

--- a/solution.py
+++ b/solution.py
@@ -92,8 +92,14 @@
     own.wait()
 
 
-def backward_chain_kernel(count, terms, out, send_buf, recv_buf, send_sem, recv_sem, local_sem):
+def backward_chain_kernel(count, terms, out, send_buf, recv_buf, staged, send_sem, recv_sem, local_sem,
+                          fetch_sem):
     me = lax.axis_index("seq")
+
+    def fetch(t):
+        return pltpu.make_async_copy(terms.at[t], staged.at[t % 2], fetch_sem.at[t % 2])
+
+    fetch(0).start()
     greet_neighbours(me, count)
     total = terms.shape[3]
 
@@ -116,19 +122,24 @@
         pl.when(me < count - 1)(send_b.start)
         pl.when(me == count - 1)(local_b.start)
 
+    fetch(0).wait()
+    fetch(1).start()
     for i in range(PIECES):
         kv, rows = piece_rows(i, total)
-        send_buf[0, :, kv, rows] = terms[0, :, kv, rows].astype(send_buf.dtype)
+        send_buf[0, :, kv, rows] = staged[0, :, kv, rows].astype(send_buf.dtype)
         start(1, i)
     for t in range(1, ROUNDS + 1):
         slot = t - 1
+        fetch(t).wait()
+        if t < ROUNDS:
+            fetch(t + 1).start()
         for i in range(PIECES):
             kv, rows = piece_rows(i, total)
             send_a, send_b, local_b = copies(t, i)
             pl.when(me < count - 1)(send_a.wait_recv)
             pl.when(me == count - 1)(local_b.wait)
             pl.when(me > 0)(send_b.wait_recv)
-            total_a = recv_buf[slot, 0, kv, rows].astype(jnp.float32) + terms[t, 0, kv, rows]
+            total_a = recv_buf[slot, 0, kv, rows].astype(jnp.float32) + staged[t % 2, 0, kv, rows]
             if t < ROUNDS:
                 send_buf[t, 0, kv, rows] = total_a.astype(send_buf.dtype)
             else:
@@ -136,7 +147,7 @@
 
             @pl.when(me > 0)
             def _():
-                total_b = recv_buf[slot, 1, kv, rows].astype(jnp.float32) + terms[t, 1, kv, rows]
+                total_b = recv_buf[slot, 1, kv, rows].astype(jnp.float32) + staged[t % 2, 1, kv, rows]
                 if t < ROUNDS:
                     send_buf[t, 1, kv, rows] = total_b.astype(send_buf.dtype)
                 else:
@@ -144,7 +155,7 @@
 
             @pl.when(me == 0)
             def _():
-                total_b = terms[t, 1, kv, rows]
+                total_b = staged[t % 2, 1, kv, rows]
                 if t < ROUNDS:
                     send_buf[t, 1, kv, rows] = total_b.astype(send_buf.dtype)
                 else:
@@ -181,14 +192,16 @@
     return pl.pallas_call(
         functools.partial(backward_chain_kernel, count),
         out_shape=jax.ShapeDtypeStruct(shape, jnp.bfloat16),
-        in_specs=[pl.BlockSpec(memory_space=pltpu.VMEM)],
+        in_specs=[pl.BlockSpec(memory_space=pl.ANY)],
         out_specs=pl.BlockSpec(memory_space=pltpu.VMEM),
         scratch_shapes=[
             pltpu.VMEM((ROUNDS,) + shape, jnp.bfloat16),
             pltpu.VMEM((ROUNDS,) + shape, jnp.bfloat16),
+            pltpu.VMEM((2,) + shape, jnp.float32),
             pltpu.SemaphoreType.DMA((ROUNDS, 2, PIECES)),
             pltpu.SemaphoreType.DMA((ROUNDS, 2, PIECES)),
             pltpu.SemaphoreType.DMA((ROUNDS, PIECES)),
+            pltpu.SemaphoreType.DMA((2,)),
         ],
         compiler_params=pltpu.CompilerParams(
             collective_id=1, has_side_effects=True, vmem_limit_bytes=60 * 1024 * 1024),

time: 309 us -> 283 us (0.916)
  Pallas kernels: 290 us -> 262 us
    pallas_call x1, Pallas kernels: 75.9 us -> 56 us  [attention(): pl.pallas_call(attention_kernel, out_shape=(jax.ShapeDtypeStruct(q.shape,...]
    pallas_call x1, Pallas kernels: 108 us -> 100 us  [backward_chain(): pl.pallas_call(functools.partial(backward_chain_kernel, count), out_shape...]
where the time goes in v12:
time: 283 us; the launch traced here: 279 us
  Pallas kernels  262 us (93%)
  local copies, waits for them, and re-layouts  13.7 us (5%)
    pallas_call x1, Pallas kernels, forward_chain(): pl.pallas_call(functools.partial(forward_chain_kernel, count), out_shape=...  106 us
    pallas_call x1, Pallas kernels, backward_chain(): pl.pallas_call(functools.partial(backward_chain_kernel, count), out_shape...  100 us
    pallas_call x1, Pallas kernels, attention(): pl.pallas_call(attention_kernel, out_shape=(jax.ShapeDtypeStruct(q.shape,...  56 us
    unnamed x6, local copies, waits for them, and re-layouts  5.76 us

profile of v12, /device:TPU:126, one launch (start us, length us, event | category | flops | bytes accessed | tf_op | source)
XLA Modules:
  0.0 278.6 jit_solution(6134864102780133628)
XLA Ops:
  0.6 0.1 broadcast_add_fusion
  0.7 0.0 copy-start.1
  0.7 0.1 iota_add_fusion
  0.8 1.4 select_reduce_fusion
  2.2 0.0 copy-start
  2.2 0.1 slice_reduce_fusion
  2.3 0.7 fusion.skip_ref
  3.0 1.0 copy.25
  4.0 1.0 copy.26
  5.0 0.1 pad_maximum_fusion.cur
  5.1 3.4 %copy_bitcast_fusion = (bf16[2,16,128,128]{3,2,1,0:T(8,128)(2,1)}, bf16[2,16,128,128]{3,2,1,0:T(8,128)(2,1)}) fusion(bf16[2,1,128,16,128]{4,3,2,1,0:T(8,128)(2,1)} %param.8, bf16[2,1,128,16,128]{4,3,2,1,0:T(8,128)(2,1)} %param.5), kind=kLoop, calls=%fused_computation.1 | loop fusion | bytes 4194304 | tf_op jit(solution)/shard_map/transpose | solution.py:359
  8.5 105.8 %shard_map.84 = bf16[17,2,2,512,128]{4,3,2,1,0:T(8,128)(2,1)} custom-call(bf16[2,2,512,128]{3,2,1,0:T(8,128)(2,1)S(1)} %pad_maximum_fusion.cur), custom_call_target="tpu_custom_call" | custom-call | tf_op jit(solution)/shard_map/pallas_call | solution.py:175
  114.3 0.0 copy-done.1
  114.3 0.0 copy-done
  114.3 56.0 %shard_map.85 = (bf16[2,16,128,128]{3,2,1,0:T(8,128)(2,1)}, bf16[2,16,128,128]{3,2,1,0:T(8,128)(2,1)}, f32[17,2,2,4,128,128]{5,4,3,2,1,0:T(8,128)}) custom-call(s32[2]{0:T(128)} %fusion.skip_ref, s32[2]{0:T(128)} %copy-done.1, bf16[2,16,128,128]{3,2,1,0:T(8,128)(2,1)} %get-tuple-element.27.q_ref, bf16[2,16,128,128]{3,2,1,0:T(8,128)(2,1)} %get-tuple-element.26.do_ref, ...), custom_call_target="tpu_custom_call" | custom-call | tf_op jit(solution)/shard_map/pallas_call | solution.py:326
  170.3 2.9 %copy.28 = bf16[2,1,128,16,128]{4,3,2,1,0:T(8,128)(2,1)} copy(bf16[2,1,128,16,128]{4,2,3,0,1:T(8,128)(2,1)} %bitcast.40) | data formatting | bytes 2097152
  173.2 2.9 %copy.29 = bf16[2,1,128,16,128]{4,3,2,1,0:T(8,128)(2,1)} copy(bf16[2,1,128,16,128]{4,2,3,0,1:T(8,128)(2,1)} %bitcast.39) | data formatting | bytes 2097152
  176.0 100.1 %shard_map.86 = bf16[2,2,512,128]{3,2,1,0:T(8,128)(2,1)} custom-call(f32[17,2,2,512,128]{4,3,2,1,0:T(8,128)} %bitcast.36), custom_call_target="tpu_custom_call" | custom-call | tf_op jit(solution)/shard_map/pallas_call | solution.py:192
  276.2 1.5 copy.33
  277.6 1.0 slice_bitcast_fusion
  (1 shorter events, 0.0 us)
Async XLA Ops:
  0.7 113.6 %copy-start.1 = (s32[2]{0:T(128)}, s32[2]{0:T(128)S(1)}, u32[]{:S(2)}) copy-start(s32[2]{0:T(128)S(1)} %get-tuple-element.23.first_ref) | copy-start | bytes 28
  2.2 112.1 %copy-start = (s32[2,128]{1,0:T(2,128)}, s32[2,128]{1,0:T(2,128)S(1)}, u32[]{:S(2)}) copy-start(s32[2,128]{1,0:T(2,128)S(1)} %select_reduce_fusion) | copy-start | bytes 3076

commit v13 on v12

--- a/solution.py
+++ b/solution.py
@@ -219,11 +219,14 @@
     last = win_ref.shape[0] - 1
     scale = head_dim ** (-0.5)
     heads = range(pair)
-    qs = [q_ref[0, h * group:(h + 1) * group].reshape(rows, head_dim) for h in heads]
-    grads = [do_ref[0, h * group:(h + 1) * group].reshape(rows, head_dim) for h in heads]
-    q_ts = [q.astype(jnp.float32).T.astype(jnp.bfloat16) for q in qs]
-    grad_ts = [g.astype(jnp.float32).T for g in grads]
-    grad_t_lows = [g.astype(jnp.bfloat16) for g in grad_ts]
+    def lanes(ref, h):
+        block = ref[0, h * group:(h + 1) * group]
+        return jnp.concatenate([block[g] for g in range(group)], axis=1)
+
+    q_ts = [lanes(q_ref, h) for h in heads]
+    grad_t_lows = [lanes(do_ref, h) for h in heads]
+    grad_ts = [g.astype(jnp.float32) for g in grad_t_lows]
+    contract_last = (((1,), (1,)), ((), ()))
     query_start = qstart_ref[0]
     span = first_ref[stream]
     query_pos = lax.broadcasted_iota(jnp.int32, (1, span_len), 1) + span * span_len
@@ -283,8 +286,8 @@
     deltas = []
     for h in heads:
         attended_t = accs[h].astype(jnp.bfloat16)
-        o_ref[0, h * group:(h + 1) * group] = attended_t.astype(jnp.float32).T.astype(
-            jnp.bfloat16).reshape(group, span_len, head_dim)
+        for g in range(group):
+            o_ref[0, h * group + g] = attended_t[:, g * span_len:(g + 1) * span_len]
         deltas.append(jnp.sum(grad_ts[h] * attended_t.astype(jnp.float32), axis=0, keepdims=True))
 
     def grad_step(j, dqs):
@@ -294,8 +297,10 @@
             low = prob.astype(jnp.bfloat16)
             grad_w = jnp.dot(win_ref[j, 0, 1, h], grad_t_lows[h], preferred_element_type=jnp.float32)
             grad_s = (prob * (grad_w - deltas[h]) * scale).astype(jnp.bfloat16)
-            terms_ref[j, 0, 0, h] = jnp.dot(grad_s, qs[h], preferred_element_type=jnp.float32)
-            terms_ref[j, 0, 1, h] = jnp.dot(low, grads[h], preferred_element_type=jnp.float32)
+            terms_ref[j, 0, 0, h] = lax.dot_general(q_ts[h], grad_s, contract_last,
+                                                    preferred_element_type=jnp.float32)
+            terms_ref[j, 0, 1, h] = lax.dot_general(grad_t_lows[h], low, contract_last,
+                                                    preferred_element_type=jnp.float32)
             key_t = win_ref[j, 0, 0, h].astype(jnp.float32).T.astype(jnp.bfloat16)
             new.append(dqs[h] + jnp.dot(key_t, grad_s, preferred_element_type=jnp.float32))
         return tuple(new)
@@ -303,8 +308,9 @@
     dqs = grad_step(last, tuple(zero for _ in heads))
     dqs = lax.fori_loop(first, last, grad_step, dqs)
     for h in heads:
-        dq_ref[0, h * group:(h + 1) * group] = dqs[h].T.astype(jnp.bfloat16).reshape(
-            group, span_len, head_dim)
+        dq_low = dqs[h].astype(jnp.bfloat16)
+        for g in range(group):
+            dq_ref[0, h * group + g] = dq_low[:, g * span_len:(g + 1) * span_len]
 
     def clear(j, carry):
         terms_ref[j] = jnp.zeros(terms_ref.shape[1:], terms_ref.dtype)
@@ -355,8 +361,8 @@
     kv_heads = keys.shape[3]
     head_dim = query.shape[4]
     group = query.shape[3] // kv_heads
-    q = jnp.transpose(query[:, 0], (0, 2, 1, 3))
-    grad_o = jnp.transpose(grad_out[:, 0], (0, 2, 1, 3))
+    q = jnp.transpose(query[:, 0], (0, 2, 3, 1))
+    grad_o = jnp.transpose(grad_out[:, 0], (0, 2, 3, 1))
     current = jnp.stack([jnp.transpose(keys[:, 0], (0, 2, 1, 3)),
                          jnp.transpose(values[:, 0], (0, 2, 1, 3))], axis=1)
     flat = current.reshape(2, 2, kv_heads * span_len, head_dim)
@@ -371,10 +377,10 @@
         skip, span_firsts, q, grad_o, spans, query_start[:, None, :], group)
     term_flat = terms.reshape(window + 1, 2, 2, kv_heads * span_len, head_dim)
     totals = backward_chain(term_flat, shard_count).reshape(current.shape)
-    grad_kv = jnp.transpose(totals, (1, 0, 3, 2, 4))[:, :, None]
+    grad_kv = jnp.transpose(totals, (1, 0, 4, 2, 3))[:, :, None]
     return (
-        jnp.transpose(attended, (0, 2, 1, 3))[:, None],
-        jnp.transpose(grad_q, (0, 2, 1, 3))[:, None],
+        jnp.transpose(attended, (0, 3, 1, 2))[:, None],
+        jnp.transpose(grad_q, (0, 3, 1, 2))[:, None],
         grad_kv[0],
         grad_kv[1],
     )

time: 283 us -> 283 us (level)
    unnamed x6 -> x10, local copies, waits for them, and re-layouts: 5.76 us -> 9.62 us
    transpose x1 -> x0, local copies, waits for them, and re-layouts: 3.4 us -> none  [body(): grad_o = jnp.transpose(grad_out[:, 0], (0, 2, 1, 3))]
where the time goes in v13:
time: 283 us; the launch traced here: 280 us
  Pallas kernels  262 us (93%)
  local copies, waits for them, and re-layouts  14 us (5%)
    pallas_call x1, Pallas kernels, forward_chain(): pl.pallas_call(functools.partial(forward_chain_kernel, count), out_shape=...  106 us
    pallas_call x1, Pallas kernels, backward_chain(): pl.pallas_call(functools.partial(backward_chain_kernel, count), out_shape...  102 us
    pallas_call x1, Pallas kernels, attention(): pl.pallas_call(attention_kernel, out_shape=(jax.ShapeDtypeStruct(q.shape,...  54.9 us
    unnamed x10, local copies, waits for them, and re-layouts  9.62 us

profile of v13, /device:TPU:126, one launch (start us, length us, event | category | flops | bytes accessed | tf_op | source)
XLA Modules:
  0.0 279.6 jit_solution(13587105004257477324)
XLA Ops:
  0.6 0.0 copy-start
  0.6 0.1 broadcast_add_fusion
  0.7 0.0 copy-start.2
  0.7 0.1 iota_add_fusion
  0.8 1.5 select_reduce_fusion
  2.3 0.0 copy-start.1
  2.3 0.1 slice_reduce_fusion
  2.4 0.7 fusion.skip_ref
  3.1 1.0 copy.25
  4.1 1.0 copy.26
  5.1 0.1 pad_maximum_fusion.cur
  5.2 2.7 copy.23
  7.8 0.0 copy-done
  7.8 1.7 copy.24
  9.5 105.8 %shard_map.84 = bf16[17,2,2,512,128]{4,3,2,1,0:T(8,128)(2,1)} custom-call(bf16[2,2,512,128]{3,2,1,0:T(8,128)(2,1)S(1)} %pad_maximum_fusion.cur), custom_call_target="tpu_custom_call" | custom-call | tf_op jit(solution)/shard_map/pallas_call | solution.py:175
  115.3 0.0 copy-done.2
  115.4 0.0 copy-done.1
  115.4 54.9 %shard_map.85 = (bf16[2,16,128,128]{3,2,1,0:T(8,128)(2,1)}, bf16[2,16,128,128]{3,2,1,0:T(8,128)(2,1)}, f32[17,2,2,4,128,128]{5,4,3,2,1,0:T(8,128)}) custom-call(s32[2]{0:T(128)} %fusion.skip_ref, s32[2]{0:T(128)} %copy-done.2, bf16[2,16,128,128]{3,2,1,0:T(8,128)(2,1)} %bitcast.33, bf16[2,16,128,128]{3,2,1,0:T(8,128)(2,1)} %bitcast.34, ...), custom_call_target="tpu_custom_call" | custom-call | tf_op jit(solution)/shard_map/pallas_call | solution.py:332
  170.3 2.6 copy.28
  172.9 2.6 copy.29
  175.6 101.7 %shard_map.86 = bf16[2,2,512,128]{3,2,1,0:T(8,128)(2,1)} custom-call(f32[17,2,2,512,128]{4,3,2,1,0:T(8,128)} %bitcast.32), custom_call_target="tpu_custom_call" | custom-call | tf_op jit(solution)/shard_map/pallas_call | solution.py:192
  277.2 1.3 copy.27
  278.6 1.0 slice_bitcast_fusion
  (1 shorter events, 0.0 us)
Async XLA Ops:
  0.6 7.2 %copy-start = (bf16[2,1,128,16,128]{4,3,2,1,0:T(8,128)(2,1)S(1)}, bf16[2,1,128,16,128]{4,3,2,1,0:T(8,128)(2,1)}, u32[]{:S(2)}) copy-start(bf16[2,1,128,16,128]{4,3,2,1,0:T(8,128)(2,1)} %param.8) | copy-start | bytes 3145732
  0.7 114.6 %copy-start.2 = (s32[2]{0:T(128)}, s32[2]{0:T(128)S(1)}, u32[]{:S(2)}) copy-start(s32[2]{0:T(128)S(1)} %get-tuple-element.23.first_ref) | copy-start | bytes 28
  2.3 113.1 %copy-start.1 = (s32[2,128]{1,0:T(2,128)}, s32[2,128]{1,0:T(2,128)S(1)}, u32[]{:S(2)}) copy-start(s32[2,128]{1,0:T(2,128)S(1)} %select_reduce_fusion) | copy-start | bytes 3076

commit v14 on v12

--- a/solution.py
+++ b/solution.py
@@ -219,11 +219,15 @@
     last = win_ref.shape[0] - 1
     scale = head_dim ** (-0.5)
     heads = range(pair)
-    qs = [q_ref[0, h * group:(h + 1) * group].reshape(rows, head_dim) for h in heads]
-    grads = [do_ref[0, h * group:(h + 1) * group].reshape(rows, head_dim) for h in heads]
-    q_ts = [q.astype(jnp.float32).T.astype(jnp.bfloat16) for q in qs]
-    grad_ts = [g.astype(jnp.float32).T for g in grads]
-    grad_t_lows = [g.astype(jnp.bfloat16) for g in grad_ts]
+    def lanes(ref, h):
+        block = ref[0, h * group:(h + 1) * group]
+        return jnp.concatenate([block[g] for g in range(group)], axis=1)
+
+    q_ts = [lanes(q_ref, h) for h in heads]
+    grad_t_lows = [lanes(do_ref, h) for h in heads]
+    grad_ts = [g.astype(jnp.float32) for g in grad_t_lows]
+    qs = [q.astype(jnp.float32).T.astype(jnp.bfloat16) for q in q_ts]
+    grads = [g.T.astype(jnp.bfloat16) for g in grad_ts]
     query_start = qstart_ref[0]
     span = first_ref[stream]
     query_pos = lax.broadcasted_iota(jnp.int32, (1, span_len), 1) + span * span_len
@@ -355,8 +359,8 @@
     kv_heads = keys.shape[3]
     head_dim = query.shape[4]
     group = query.shape[3] // kv_heads
-    q = jnp.transpose(query[:, 0], (0, 2, 1, 3))
-    grad_o = jnp.transpose(grad_out[:, 0], (0, 2, 1, 3))
+    q = jnp.transpose(query[:, 0], (0, 2, 3, 1))
+    grad_o = jnp.transpose(grad_out[:, 0], (0, 2, 3, 1))
     current = jnp.stack([jnp.transpose(keys[:, 0], (0, 2, 1, 3)),
                          jnp.transpose(values[:, 0], (0, 2, 1, 3))], axis=1)
     flat = current.reshape(2, 2, kv_heads * span_len, head_dim)

time: 283 us -> 282 us (level)
  the two profiles are of different devices: /device:TPU:126 before, /device:TPU:119 now
where the time goes in v14:
time: 282 us
  Pallas kernels  264 us (94%)
  local copies, waits for them, and re-layouts  14.6 us (5%)
    pallas_call x1, Pallas kernels, backward_chain(): pl.pallas_call(functools.partial(backward_chain_kernel, count), out_shape...  120 us
    pallas_call x1, Pallas kernels, forward_chain(): pl.pallas_call(functools.partial(forward_chain_kernel, count), out_shape=...  105 us
    pallas_call x1, Pallas kernels, attention(): pl.pallas_call(attention_kernel, out_shape=(jax.ShapeDtypeStruct(q.shape,...  40.3 us
    unnamed x10, local copies, waits for them, and re-layouts  10.1 us

profile of v14, /device:TPU:119, one launch (start us, length us, event | category | flops | bytes accessed | tf_op | source)
XLA Modules:
  0.0 282.1 jit_solution(7082423094398295029)
XLA Ops:
  0.6 0.0 copy-start
  0.6 0.1 broadcast_add_fusion
  0.7 0.0 copy-start.2
  0.7 0.1 iota_add_fusion
  0.8 1.5 select_reduce_fusion
  2.3 0.0 copy-start.1
  2.3 0.1 slice_reduce_fusion
  2.4 0.7 fusion.skip_ref
  3.1 1.0 copy.25
  4.1 1.0 copy.26
  5.1 0.1 pad_maximum_fusion.cur
  5.2 2.7 copy.23
  7.8 0.0 copy-done
  7.8 1.7 copy.24
  9.5 104.5 %shard_map.84 = bf16[17,2,2,512,128]{4,3,2,1,0:T(8,128)(2,1)} custom-call(bf16[2,2,512,128]{3,2,1,0:T(8,128)(2,1)S(1)} %pad_maximum_fusion.cur), custom_call_target="tpu_custom_call" | custom-call | tf_op jit(solution)/shard_map/pallas_call | solution.py:175
  114.0 0.0 copy-done.2
  114.0 0.0 copy-done.1
  114.0 40.3 %shard_map.85 = (bf16[2,16,128,128]{3,2,1,0:T(8,128)(2,1)}, bf16[2,16,128,128]{3,2,1,0:T(8,128)(2,1)}, f32[17,2,2,4,128,128]{5,4,3,2,1,0:T(8,128)}) custom-call(s32[2]{0:T(128)} %fusion.skip_ref, s32[2]{0:T(128)} %copy-done.2, bf16[2,16,128,128]{3,2,1,0:T(8,128)(2,1)} %bitcast.35, bf16[2,16,128,128]{3,2,1,0:T(8,128)(2,1)} %bitcast.36, ...), custom_call_target="tpu_custom_call" | custom-call | tf_op jit(solution)/shard_map/pallas_call | solution.py:330
  154.4 2.9 %copy.28 = bf16[2,1,128,16,128]{4,3,2,1,0:T(8,128)(2,1)} copy(bf16[2,1,128,16,128]{4,2,3,0,1:T(8,128)(2,1)} %bitcast.40) | data formatting | bytes 2097152
  157.3 2.9 %copy.29 = bf16[2,1,128,16,128]{4,3,2,1,0:T(8,128)(2,1)} copy(bf16[2,1,128,16,128]{4,2,3,0,1:T(8,128)(2,1)} %bitcast.39) | data formatting | bytes 2097152
  160.1 119.5 %shard_map.86 = bf16[2,2,512,128]{3,2,1,0:T(8,128)(2,1)} custom-call(f32[17,2,2,512,128]{4,3,2,1,0:T(8,128)} %bitcast.34), custom_call_target="tpu_custom_call" | custom-call | tf_op jit(solution)/shard_map/pallas_call | solution.py:192
  279.7 1.5 copy.31
  281.1 1.0 slice_bitcast_fusion
  (1 shorter events, 0.0 us)
Async XLA Ops:
  0.6 7.2 %copy-start = (bf16[2,1,128,16,128]{4,3,2,1,0:T(8,128)(2,1)S(1)}, bf16[2,1,128,16,128]{4,3,2,1,0:T(8,128)(2,1)}, u32[]{:S(2)}) copy-start(bf16[2,1,128,16,128]{4,3,2,1,0:T(8,128)(2,1)} %param.8) | copy-start | bytes 3145732
  0.7 113.3 %copy-start.2 = (s32[2]{0:T(128)}, s32[2]{0:T(128)S(1)}, u32[]{:S(2)}) copy-start(s32[2]{0:T(128)S(1)} %get-tuple-element.23.first_ref) | copy-start | bytes 28
  2.3 111.7 %copy-start.1 = (s32[2,128]{1,0:T(2,128)}, s32[2,128]{1,0:T(2,128)S(1)}, u32[]{:S(2)}) copy-start(s32[2,128]{1,0:T(2,128)S(1)} %select_reduce_fusion) | copy-start | bytes 3076

commit v15 on v13

--- a/solution.py
+++ b/solution.py
@@ -139,7 +139,7 @@
             pl.when(me < count - 1)(send_a.wait_recv)
             pl.when(me == count - 1)(local_b.wait)
             pl.when(me > 0)(send_b.wait_recv)
-            total_a = recv_buf[slot, 0, kv, rows].astype(jnp.float32) + staged[t % 2, 0, kv, rows]
+            total_a = recv_buf[slot, 0, kv, rows].astype(jnp.float32) + staged[t % 2, 0, kv, rows].astype(jnp.float32)
             if t < ROUNDS:
                 send_buf[t, 0, kv, rows] = total_a.astype(send_buf.dtype)
             else:
@@ -147,7 +147,7 @@
 
             @pl.when(me > 0)
             def _():
-                total_b = recv_buf[slot, 1, kv, rows].astype(jnp.float32) + staged[t % 2, 1, kv, rows]
+                total_b = recv_buf[slot, 1, kv, rows].astype(jnp.float32) + staged[t % 2, 1, kv, rows].astype(jnp.float32)
                 if t < ROUNDS:
                     send_buf[t, 1, kv, rows] = total_b.astype(send_buf.dtype)
                 else:
@@ -155,7 +155,7 @@
 
             @pl.when(me == 0)
             def _():
-                total_b = staged[t % 2, 1, kv, rows]
+                total_b = staged[t % 2, 1, kv, rows].astype(jnp.float32)
                 if t < ROUNDS:
                     send_buf[t, 1, kv, rows] = total_b.astype(send_buf.dtype)
                 else:
@@ -197,7 +197,7 @@
         scratch_shapes=[
             pltpu.VMEM((ROUNDS,) + shape, jnp.bfloat16),
             pltpu.VMEM((ROUNDS,) + shape, jnp.bfloat16),
-            pltpu.VMEM((2,) + shape, jnp.float32),
+            pltpu.VMEM((2,) + shape, terms.dtype),
             pltpu.SemaphoreType.DMA((ROUNDS, 2, PIECES)),
             pltpu.SemaphoreType.DMA((ROUNDS, 2, PIECES)),
             pltpu.SemaphoreType.DMA((ROUNDS, PIECES)),
@@ -298,9 +298,9 @@
             grad_w = jnp.dot(win_ref[j, 0, 1, h], grad_t_lows[h], preferred_element_type=jnp.float32)
             grad_s = (prob * (grad_w - deltas[h]) * scale).astype(jnp.bfloat16)
             terms_ref[j, 0, 0, h] = lax.dot_general(q_ts[h], grad_s, contract_last,
-                                                    preferred_element_type=jnp.float32)
+                                                    preferred_element_type=jnp.float32).astype(terms_ref.dtype)
             terms_ref[j, 0, 1, h] = lax.dot_general(grad_t_lows[h], low, contract_last,
-                                                    preferred_element_type=jnp.float32)
+                                                    preferred_element_type=jnp.float32).astype(terms_ref.dtype)
             key_t = win_ref[j, 0, 0, h].astype(jnp.float32).T.astype(jnp.bfloat16)
             new.append(dqs[h] + jnp.dot(key_t, grad_s, preferred_element_type=jnp.float32))
         return tuple(new)
@@ -334,7 +334,7 @@
         out_shape=(
             jax.ShapeDtypeStruct(q.shape, jnp.bfloat16),
             jax.ShapeDtypeStruct(q.shape, jnp.bfloat16),
-            jax.ShapeDtypeStruct((spans, streams, 2, kv_heads, span_len, head_dim), jnp.float32),
+            jax.ShapeDtypeStruct((spans, streams, 2, kv_heads, span_len, head_dim), jnp.bfloat16),
         ),
         grid_spec=pltpu.PrefetchScalarGridSpec(
             num_scalar_prefetch=2,

time: 283 us -> 283 us (level); the launches traced: 280 us -> 283 us
  Pallas kernels: 262 us -> 266 us
    pallas_call x1, Pallas kernels: 54.9 us -> 60.7 us  [attention(): pl.pallas_call(attention_kernel, out_shape=(jax.ShapeDtypeStruct(q.shape,...]
where the time goes in v15:
time: 283 us
  Pallas kernels  266 us (94%)
  local copies, waits for them, and re-layouts  14 us (5%)
    pallas_call x1, Pallas kernels, forward_chain(): pl.pallas_call(functools.partial(forward_chain_kernel, count), out_shape=...  106 us
    pallas_call x1, Pallas kernels, backward_chain(): pl.pallas_call(functools.partial(backward_chain_kernel, count), out_shape...  99.1 us
    pallas_call x1, Pallas kernels, attention(): pl.pallas_call(attention_kernel, out_shape=(jax.ShapeDtypeStruct(q.shape,...  60.7 us
    unnamed x10, local copies, waits for them, and re-layouts  9.62 us

profile of v15, /device:TPU:126, one launch (start us, length us, event | category | flops | bytes accessed | tf_op | source)
XLA Modules:
  0.0 282.7 jit_solution(5744362485017847399)
XLA Ops:
  0.6 0.0 copy-start
  0.6 0.1 broadcast_add_fusion
  0.7 0.0 copy-start.2
  0.7 0.1 iota_add_fusion
  0.8 1.5 select_reduce_fusion
  2.3 0.0 copy-start.1
  2.3 0.1 slice_reduce_fusion
  2.4 0.7 fusion.skip_ref
  3.1 1.0 copy.25
  4.1 1.0 copy.26
  5.1 0.1 pad_maximum_fusion.cur
  5.2 2.7 copy.23
  7.8 0.0 copy-done
  7.8 1.7 copy.24
  9.5 105.8 %shard_map.84 = bf16[17,2,2,512,128]{4,3,2,1,0:T(8,128)(2,1)} custom-call(bf16[2,2,512,128]{3,2,1,0:T(8,128)(2,1)S(1)} %pad_maximum_fusion.cur), custom_call_target="tpu_custom_call" | custom-call | tf_op jit(solution)/shard_map/pallas_call | solution.py:175
  115.3 0.0 copy-done.2
  115.3 0.0 copy-done.1
  115.3 60.7 %shard_map.85 = (bf16[2,16,128,128]{3,2,1,0:T(8,128)(2,1)}, bf16[2,16,128,128]{3,2,1,0:T(8,128)(2,1)}, bf16[17,2,2,4,128,128]{5,4,3,2,1,0:T(8,128)(2,1)}) custom-call(s32[2]{0:T(128)} %fusion.skip_ref, s32[2]{0:T(128)} %copy-done.2, bf16[2,16,128,128]{3,2,1,0:T(8,128)(2,1)} %bitcast.33, bf16[2,16,128,128]{3,2,1,0:T(8,128)(2,1)} %bitcast.34, ...), custom_call_target="tpu_custom_call" | custom-call | tf_op jit(solution)/shard_map/pallas_call | solution.py:332
  176.0 2.6 copy.28
  178.6 2.6 copy.29
  181.3 99.1 %shard_map.86 = bf16[2,2,512,128]{3,2,1,0:T(8,128)(2,1)} custom-call(bf16[17,2,2,512,128]{4,3,2,1,0:T(8,128)(2,1)} %bitcast.32), custom_call_target="tpu_custom_call" | custom-call | tf_op jit(solution)/shard_map/pallas_call | solution.py:192
  280.3 1.3 copy.27
  281.7 1.0 slice_bitcast_fusion
  (1 shorter events, 0.0 us)
Async XLA Ops:
  0.6 7.2 %copy-start = (bf16[2,1,128,16,128]{4,3,2,1,0:T(8,128)(2,1)S(1)}, bf16[2,1,128,16,128]{4,3,2,1,0:T(8,128)(2,1)}, u32[]{:S(2)}) copy-start(bf16[2,1,128,16,128]{4,3,2,1,0:T(8,128)(2,1)} %param.8) | copy-start | bytes 3145732
  0.7 114.6 %copy-start.2 = (s32[2]{0:T(128)}, s32[2]{0:T(128)S(1)}, u32[]{:S(2)}) copy-start(s32[2]{0:T(128)S(1)} %get-tuple-element.23.first_ref) | copy-start | bytes 28
  2.3 113.0 %copy-start.1 = (s32[2,128]{1,0:T(2,128)}, s32[2,128]{1,0:T(2,128)S(1)}, u32[]{:S(2)}) copy-start(s32[2,128]{1,0:T(2,128)S(1)} %select_reduce_fusion) | copy-start | bytes 3076

commit v16 on v14

--- a/solution.py
+++ b/solution.py
@@ -139,7 +139,7 @@
             pl.when(me < count - 1)(send_a.wait_recv)
             pl.when(me == count - 1)(local_b.wait)
             pl.when(me > 0)(send_b.wait_recv)
-            total_a = recv_buf[slot, 0, kv, rows].astype(jnp.float32) + staged[t % 2, 0, kv, rows]
+            total_a = recv_buf[slot, 0, kv, rows].astype(jnp.float32) + staged[t % 2, 0, kv, rows].astype(jnp.float32)
             if t < ROUNDS:
                 send_buf[t, 0, kv, rows] = total_a.astype(send_buf.dtype)
             else:
@@ -147,7 +147,7 @@
 
             @pl.when(me > 0)
             def _():
-                total_b = recv_buf[slot, 1, kv, rows].astype(jnp.float32) + staged[t % 2, 1, kv, rows]
+                total_b = recv_buf[slot, 1, kv, rows].astype(jnp.float32) + staged[t % 2, 1, kv, rows].astype(jnp.float32)
                 if t < ROUNDS:
                     send_buf[t, 1, kv, rows] = total_b.astype(send_buf.dtype)
                 else:
@@ -155,7 +155,7 @@
 
             @pl.when(me == 0)
             def _():
-                total_b = staged[t % 2, 1, kv, rows]
+                total_b = staged[t % 2, 1, kv, rows].astype(jnp.float32)
                 if t < ROUNDS:
                     send_buf[t, 1, kv, rows] = total_b.astype(send_buf.dtype)
                 else:
@@ -197,7 +197,7 @@
         scratch_shapes=[
             pltpu.VMEM((ROUNDS,) + shape, jnp.bfloat16),
             pltpu.VMEM((ROUNDS,) + shape, jnp.bfloat16),
-            pltpu.VMEM((2,) + shape, jnp.float32),
+            pltpu.VMEM((2,) + shape, terms.dtype),
             pltpu.SemaphoreType.DMA((ROUNDS, 2, PIECES)),
             pltpu.SemaphoreType.DMA((ROUNDS, 2, PIECES)),
             pltpu.SemaphoreType.DMA((ROUNDS, PIECES)),
@@ -298,8 +298,10 @@
             low = prob.astype(jnp.bfloat16)
             grad_w = jnp.dot(win_ref[j, 0, 1, h], grad_t_lows[h], preferred_element_type=jnp.float32)
             grad_s = (prob * (grad_w - deltas[h]) * scale).astype(jnp.bfloat16)
-            terms_ref[j, 0, 0, h] = jnp.dot(grad_s, qs[h], preferred_element_type=jnp.float32)
-            terms_ref[j, 0, 1, h] = jnp.dot(low, grads[h], preferred_element_type=jnp.float32)
+            terms_ref[j, 0, 0, h] = jnp.dot(grad_s, qs[h], preferred_element_type=jnp.float32).astype(
+                terms_ref.dtype)
+            terms_ref[j, 0, 1, h] = jnp.dot(low, grads[h], preferred_element_type=jnp.float32).astype(
+                terms_ref.dtype)
             key_t = win_ref[j, 0, 0, h].astype(jnp.float32).T.astype(jnp.bfloat16)
             new.append(dqs[h] + jnp.dot(key_t, grad_s, preferred_element_type=jnp.float32))
         return tuple(new)
@@ -332,7 +334,7 @@
         out_shape=(
             jax.ShapeDtypeStruct(q.shape, jnp.bfloat16),
             jax.ShapeDtypeStruct(q.shape, jnp.bfloat16),
-            jax.ShapeDtypeStruct((spans, streams, 2, kv_heads, span_len, head_dim), jnp.float32),
+            jax.ShapeDtypeStruct((spans, streams, 2, kv_heads, span_len, head_dim), jnp.bfloat16),
         ),
         grid_spec=pltpu.PrefetchScalarGridSpec(
             num_scalar_prefetch=2,

time: 282 us -> 288 us (1.021)
  the two profiles are of different devices: /device:TPU:119 before, /device:TPU:126 now
where the time goes in v16:
time: 288 us; the launch traced here: 293 us
  Pallas kernels  276 us (96%)
  local copies, waits for them, and re-layouts  14.6 us (5%)
    pallas_call x1, Pallas kernels, forward_chain(): pl.pallas_call(functools.partial(forward_chain_kernel, count), out_shape=...  106 us
    pallas_call x1, Pallas kernels, backward_chain(): pl.pallas_call(functools.partial(backward_chain_kernel, count), out_shape...  97.3 us
    pallas_call x1, Pallas kernels, attention(): pl.pallas_call(attention_kernel, out_shape=(jax.ShapeDtypeStruct(q.shape,...  72.4 us
    unnamed x10, local copies, waits for them, and re-layouts  10.1 us

profile of v16, /device:TPU:126, one launch (start us, length us, event | category | flops | bytes accessed | tf_op | source)
XLA Modules:
  0.0 293.2 jit_solution(5603079072057455231)
XLA Ops:
  0.6 0.0 copy-start
  0.6 0.1 broadcast_add_fusion
  0.7 0.0 copy-start.2
  0.7 0.1 iota_add_fusion
  0.8 1.5 select_reduce_fusion
  2.3 0.0 copy-start.1
  2.3 0.1 slice_reduce_fusion
  2.4 0.7 fusion.skip_ref
  3.1 1.0 copy.25
  4.1 1.0 copy.26
  5.1 0.1 pad_maximum_fusion.cur
  5.2 2.7 copy.23
  7.8 0.0 copy-done
  7.8 1.7 copy.24
  9.5 105.8 %shard_map.84 = bf16[17,2,2,512,128]{4,3,2,1,0:T(8,128)(2,1)} custom-call(bf16[2,2,512,128]{3,2,1,0:T(8,128)(2,1)S(1)} %pad_maximum_fusion.cur), custom_call_target="tpu_custom_call" | custom-call | tf_op jit(solution)/shard_map/pallas_call | solution.py:175
  115.3 0.0 copy-done.2
  115.3 0.0 copy-done.1
  115.3 72.4 %shard_map.85 = (bf16[2,16,128,128]{3,2,1,0:T(8,128)(2,1)}, bf16[2,16,128,128]{3,2,1,0:T(8,128)(2,1)}, bf16[17,2,2,4,128,128]{5,4,3,2,1,0:T(8,128)(2,1)}) custom-call(s32[2]{0:T(128)} %fusion.skip_ref, s32[2]{0:T(128)} %copy-done.2, bf16[2,16,128,128]{3,2,1,0:T(8,128)(2,1)} %bitcast.35, bf16[2,16,128,128]{3,2,1,0:T(8,128)(2,1)} %bitcast.36, ...), custom_call_target="tpu_custom_call" | custom-call | tf_op jit(solution)/shard_map/pallas_call | solution.py:332
  187.7 2.9 copy.28
  190.6 2.9 copy.29
  193.5 97.3 %shard_map.86 = bf16[2,2,512,128]{3,2,1,0:T(8,128)(2,1)} custom-call(bf16[17,2,2,512,128]{4,3,2,1,0:T(8,128)(2,1)} %bitcast.34), custom_call_target="tpu_custom_call" | custom-call | tf_op jit(solution)/shard_map/pallas_call | solution.py:192
  290.8 1.5 copy.31
  292.3 1.0 slice_bitcast_fusion
  (1 shorter events, 0.0 us)
Async XLA Ops:
  0.6 7.2 %copy-start = (bf16[2,1,128,16,128]{4,3,2,1,0:T(8,128)(2,1)S(1)}, bf16[2,1,128,16,128]{4,3,2,1,0:T(8,128)(2,1)}, u32[]{:S(2)}) copy-start(bf16[2,1,128,16,128]{4,3,2,1,0:T(8,128)(2,1)} %param.8) | copy-start | bytes 3145732
  0.7 114.6 %copy-start.2 = (s32[2]{0:T(128)}, s32[2]{0:T(128)S(1)}, u32[]{:S(2)}) copy-start(s32[2]{0:T(128)S(1)} %get-tuple-element.23.first_ref) | copy-start | bytes 28
  2.3 113.0 %copy-start.1 = (s32[2,128]{1,0:T(2,128)}, s32[2,128]{1,0:T(2,128)S(1)}, u32[]{:S(2)}) copy-start(s32[2,128]{1,0:T(2,128)S(1)} %select_reduce_fusion) | copy-start | bytes 3076
